TPU v7x, 32 devices: a whole 2x2x4 slice. The times are simulated.
32 devices in a mesh: pairs: 4 (over y, core), stripe: 8 (over z, x).
Axes of the slice: x: 2, y: 2, z: 4, core: 2. Of those that a mesh axis runs over, the one named last changes fastest.
Arguments:
- slc_stack: bfloat16 [256, 2, 128, 1024], P(('pairs', 'stripe')), may hold values from -16 to 16
- az_offset: int32 [256], replicated, may hold values from -8 to 8
- rg_offset: int32 [256], replicated, may hold values from -16 to 16
- pair_list: int32 [1000, 2], replicated, may hold values from 0 to 255, as said below
Outputs:
- screen: float32 [256, 2, 32, 64], P(None, None, 'pairs', 'stripe')
- motion: float32 [256, 2, 32, 64], P(None, None, 'pairs', 'stripe')
Inputs may be any that keep to these rules, and one draw needn't show every extreme that they name: `pair_list`: rows g * 250 to (g + 1) * 250 - 1 form pair group g: their reference dates lie in g * 64 to (g + 1) * 64 - 1, each secondary date is 1 to 5 dates after its reference, and no pair repeats.
All inputs are finite; a program needn't handle non-finite values.
Results may differ from a plain program's by a relative error of at most 0.0029.
Values may be sent and summed in bfloat16 or wider, within the bound.
No kernel may reach another device: no remote copies, remote signals or barrier semaphores. Data moves between devices by JAX's collectives and lax.ppermute only.
A program may use at most 64 MiB of HBM per device.

v0:
```python
from functools import partial

import jax
import jax.numpy as jnp
from jax import lax
from jax.experimental import pallas as pl
from jax.experimental.pallas import tpu as pltpu
from jax.sharding import Mesh, PartitionSpec as P


MAXB = 5
LA = 4
LR = 16
MAXA = 8
FILTER_R = 3
LANES = 128
GRANT = 16 << 20
damping = 0.5


def vmem():
    return pl.BlockSpec(memory_space=pltpu.VMEM)


def tap(k):
    sigma = FILTER_R / 2.0
    return jnp.exp(-jnp.float32(k * k) / jnp.float32(2.0 * sigma * sigma))


def resample_kernel(first, per_stripe, chunks, info, az, rg, img, *rest):
    rest = rest[-2 - chunks :]
    keep, sends, shifted = rest[0], rest[1 : 1 + chunks], rest[1 + chunks]
    lines, full = img.shape[2], img.shape[3]
    tiles = full // LANES
    half = tiles // 2
    high = lines + 2 * MAXA
    groups = lines // 8
    date = info[1] + first + pl.program_id(0)
    x = info[0]
    shift = rg[date]
    step = az[date]
    behind = shift < 0
    origin = jnp.where(behind, -1, 0)
    amount = shift - origin * LANES
    turn = lax.rem(LANES - amount, LANES)
    lane = lax.broadcasted_iota(jnp.int32, (lines, LANES), 1)
    own = lane + amount < LANES

    @pl.when((pl.program_id(0) == 0) & (pl.program_id(1) == 0))
    def _():
        blank = jnp.zeros((MAXA, LANES), jnp.float32)
        for t in range(tiles):
            shifted[pl.ds(t * high, MAXA), :] = blank
            shifted[pl.ds(t * high + MAXA + lines, MAXA), :] = blank

    def turned(t):
        place = jnp.clip(t + origin, 0, tiles - 1)
        tile = img[0, 0, :, pl.ds(pl.multiple_of(place * LANES, LANES), LANES)]
        out = pltpu.roll(tile.astype(jnp.float32), turn, 1)
        if t == 0:
            out = jnp.where(behind, 0.0, out)
        if t == tiles:
            out = jnp.where(behind, out, 0.0)
        return out

    here = turned(0)
    for t in range(tiles):
        after = turned(t + 1)
        shifted[pl.ds(t * high + MAXA, lines), :] = jnp.where(own, here, after)
        here = after

    def put(out, place, source):
        base = source * high + MAXA + step
        for pair in range(groups // 2):
            both = [shifted[pl.ds(base + 2 * pair + k, 8, stride=groups), :] for k in range(2)]
            out[0, 0, place, pl.ds(16 * pair, 16), :] = jnp.concatenate(both, 0).astype(
                jnp.bfloat16
            )

    per_chunk = half // chunks
    for h in range(half):
        stripe, inner = h // per_stripe, h % per_stripe
        put(sends[h // per_chunk], h % per_chunk, (2 * stripe + 1 - x) * per_stripe + inner)
        put(keep, h, (2 * stripe + x) * per_stripe + inner)


def resample(images, az, rg, info, first, count, per_stripe, chunks, earlier):
    lines, full = images.shape[2], images.shape[3]
    tiles = full // LANES
    half = tiles // 2

    def block(width):
        return pl.BlockSpec((1, 1, width, lines, LANES), lambda i, c, *_: (i, c, 0, 0, 0))

    def shape(width):
        return jax.ShapeDtypeStruct((count, 2, width, lines, LANES), jnp.bfloat16)

    return pl.pallas_call(
        partial(resample_kernel, first, per_stripe, chunks),
        grid_spec=pltpu.PrefetchScalarGridSpec(
            num_scalar_prefetch=3,
            grid=(count, 2),
            in_specs=[pl.BlockSpec((1, 1, lines, full), lambda i, c, *_: (i + first, c, 0, 0))]
            + [pl.BlockSpec(memory_space=pl.ANY)] * len(earlier),
            out_specs=[block(half)] + [block(half // chunks)] * chunks,
            scratch_shapes=[pltpu.VMEM((tiles * (lines + 2 * MAXA), LANES), jnp.float32)],
        ),
        out_shape=[shape(half)] + [shape(half // chunks)] * chunks,
        compiler_params=pltpu.CompilerParams(vmem_limit_bytes=GRANT),
        cost_estimate=pl.CostEstimate(
            flops=count * lines * full * 4,
            transcendentals=0,
            bytes_accessed=count * lines * full * 8,
        ),
    )(info, az, rg, images, *earlier)


def merge(x, y, bit, distance):
    return jnp.where(
        bit, x + pltpu.roll(x, LANES - distance, 1), y + pltpu.roll(y, distance, 1)
    )


def pair_kernel(own, starts, reached, info, mask, *refs):
    count = len(starts)
    parts, following = refs[: 2 * count], refs[2 * count : 2 * count + len(reached)]
    right, images, products, sums = refs[-4:]
    block = 2 * own
    x = info[0]
    mine, other = x * own, (1 - x) * own
    for s, start in enumerate(starts):
        for where, ref in ((mine, parts[2 * s]), (other, parts[2 * s + 1])):
            for i in range(ref.shape[0]):
                images[where + start + i] = ref[i, :, 0].astype(jnp.float32)
    for start, ref in zip(reached, following):
        for i in range(ref.shape[0]):
            images[block + start + i] = ref[i, :, 0].astype(jnp.float32)
    sums[...] = jnp.zeros_like(sums)

    def multiply(d, carry):
        for low in range(4):
            totals = [[None] * 2 for _ in range(MAXB)]
            for k in range(LA):
                at = pl.ds(8 * (LA * low + k), 8)
                a, b = images[d, 0, at, :], images[d, 1, at, :]
                for g in range(MAXB):
                    c, e = images[d + g + 1, 0, at, :], images[d + g + 1, 1, at, :]
                    terms = (a * c + b * e, b * c - a * e)
                    for comp, term in enumerate(terms):
                        old = totals[g][comp]
                        totals[g][comp] = term if old is None else old + term
            for g in range(MAXB):
                for comp in range(2):
                    at = (d * MAXB + g) * 64 + comp * 32 + low * 8
                    products[pl.ds(pl.multiple_of(at, 8), 8), :] = totals[g][comp]
        return carry

    lax.fori_loop(0, block, multiply, 0)
    lane = lax.broadcasted_iota(jnp.int32, (8, LANES), 1)
    bits = [lane & (1 << k) == 0 for k in range(4)]

    def slot(d, g):
        def load(comp, low):
            at = (d * MAXB + g) * 64 + comp * 32 + low * 8
            return products[pl.ds(pl.multiple_of(at, 8), 8), :]

        joined = []
        for comp in range(2):
            first = merge(load(comp, 0), load(comp, 1), bits[0], 1)
            second = merge(load(comp, 2), load(comp, 3), bits[0], 1)
            joined.append(merge(first, second, bits[1], 2))
        both = merge(joined[0], joined[1], bits[3], 8)
        result = merge(both, pltpu.roll(both, 7, 0), bits[2], 4)
        result = (result * (1.0 / (LA * LR))).astype(jnp.bfloat16).astype(jnp.float32)
        return result * mask[(info[2] + d) * MAXB + g].astype(jnp.float32)

    step = 4 if block % 4 == 0 else 1

    def gather(i, carry):
        totals = [None] * (step + MAXB)

        def add(at, value):
            totals[at] = value if totals[at] is None else totals[at] + value

        for j in range(step):
            for g in range(MAXB):
                value = slot(i * step + j, g)
                add(j, value)
                add(j + g + 1, -value)
        for j, value in enumerate(totals):
            at = pl.ds(pl.multiple_of(8 * (i * step + j), 8), 8)
            sums[at, :] = sums[at, :] + value
        return carry

    lax.fori_loop(0, block // step, gather, 0)
    for row in range(right.shape[1]):
        for group in range(right.shape[2] // 8):
            right[0, row, pl.ds(8 * group, 8), :] = sums[
                pl.ds(64 * group + 2 * row, 8, stride=8), :
            ]


def pair_sums(info, mask, pieces, following, earlier, chunk, chunks, width, own, rows, deep):
    lines = pieces[0][1].shape[3]

    def window(array, tiles):
        offset = chunk * width % tiles
        return pl.BlockSpec(
            (array.shape[0], 2, 1, lines, LANES), lambda i, *_: (0, 0, offset + i, 0, 0)
        )

    operands, specs = [], []
    for _, keep, received in pieces:
        got = received[chunk * len(received) // chunks]
        operands += [keep, got]
        specs += [window(keep, keep.shape[2]), window(got, got.shape[2])]
    for _, received in following:
        got = received[chunk * len(received) // chunks]
        operands.append(got)
        specs.append(window(got, got.shape[2]))
    if earlier is not None:
        operands.append(earlier)
        specs.append(pl.BlockSpec(memory_space=pl.ANY))
    work = 2 * own * MAXB * lines * LANES * width
    return pl.pallas_call(
        partial(pair_kernel, own, [p[0] for p in pieces], [f[0] for f in following]),
        grid_spec=pltpu.PrefetchScalarGridSpec(
            num_scalar_prefetch=2,
            grid=(width,),
            in_specs=specs,
            out_specs=pl.BlockSpec((1, rows, deep, LANES), lambda i, *_: (i, 0, 0, 0)),
            scratch_shapes=[
                pltpu.VMEM((2 * own + MAXB, 2, lines, LANES), jnp.float32),
                pltpu.VMEM((2 * own * MAXB * 64, LANES), jnp.float32),
                pltpu.VMEM((8 * deep, LANES), jnp.float32),
            ],
        ),
        out_shape=jax.ShapeDtypeStruct((width, rows, deep, LANES), jnp.float32),
        compiler_params=pltpu.CompilerParams(vmem_limit_bytes=GRANT),
        cost_estimate=pl.CostEstimate(flops=work * 8, transcendentals=0, bytes_accessed=work),
    )(info, mask, *operands)


def filter_kernel(per_stripe, chunks, info, *rest):
    own, partner = rest[:chunks], rest[chunks : 2 * chunks]
    weight, out, whole, along = rest[2 * chunks :]
    width, rows, deep = own[0].shape[:3]
    total = 2 * width * chunks
    x = info[0]
    blank = jnp.zeros((rows, deep, LANES), jnp.float32)
    along[0] = blank
    along[total + 1] = blank
    for c in range(chunks):
        for i in range(width):
            stripe, inner = divmod(c * width + i, per_stripe)
            whole[(2 * stripe + x) * per_stripe + inner] = own[c][i]
            whole[(2 * stripe + 1 - x) * per_stripe + inner] = partner[c][i]
    lane = lax.broadcasted_iota(jnp.int32, (deep, LANES), 1)
    place = lane & 7
    taps = [tap(k) for k in range(FILTER_R + 1)]

    def turn(v, k):
        return pltpu.roll(v, k % LANES, 1)

    def filter_rows(i, carry):
        for r in range(rows):
            v = whole[i, r]
            acc = v
            for k in range(1, FILTER_R + 1):
                up = turn(whole[i, r + 1], 8 - k) if r + 1 < rows else jnp.zeros_like(v)
                down = turn(whole[i, r - 1], k - 8) if r > 0 else jnp.zeros_like(v)
                near = jnp.where(place < 8 - k, turn(v, -k), up) + jnp.where(
                    place >= k, turn(v, k), down
                )
                acc = acc + taps[k] * near
            along[i + 1, r] = acc
        return carry

    lax.fori_loop(0, total, filter_rows, 0)

    for c in range(chunks):
        for i in range(width):
            h = c * width + i
            stripe, inner = divmod(h, per_stripe)
            at = (2 * stripe + x) * per_stripe + inner + 1
            for r in range(rows):
                v, left, right = along[at, r], along[at - 1, r], along[at + 1, r]
                acc = v
                for k in range(1, FILTER_R + 1):
                    reach = 16 * k
                    near = jnp.where(
                        lane < LANES - reach, turn(v, -reach), turn(right, -reach)
                    ) + jnp.where(lane >= reach, turn(v, reach), turn(left, reach))
                    acc = acc + taps[k] * near
                out[r, stripe, inner, 0] = own[c][i, r]
                out[r, stripe, inner, 1] = acc * weight[h, r : r + 1, :]


def filtered(info, own, partner, weight, per_stripe):
    chunks = len(own)
    width, rows, deep = own[0].shape[:3]
    tiles = width * chunks
    stripes = tiles // per_stripe
    smem = pl.BlockSpec(memory_space=pltpu.SMEM)
    return pl.pallas_call(
        partial(filter_kernel, per_stripe, chunks),
        in_specs=[smem] + [vmem()] * (2 * chunks + 1),
        out_specs=vmem(),
        out_shape=jax.ShapeDtypeStruct((rows, stripes, per_stripe, 2, deep, LANES), jnp.float32),
        scratch_shapes=[
            pltpu.VMEM((2 * tiles, rows, deep, LANES), jnp.float32),
            pltpu.VMEM((2 * tiles + 2, rows, deep, LANES), jnp.float32),
        ],
        name="smooth",
        compiler_params=pltpu.CompilerParams(vmem_limit_bytes=GRANT),
    )(info, *own, *partner, weight)


def edge_weights(positions, whole):
    total = jnp.zeros(positions.shape, jnp.float32)
    for k in range(-FILTER_R, FILTER_R + 1):
        at = positions + k
        total = total + jnp.where((at >= 0) & (at < whole), tap(k), 0.0)
    return total


def invert_kernel(normal, out):
    size = normal.shape[0]
    low, high = damping, damping + 4.0 * MAXB
    middle, spread = high + low, high - low
    peak = 2.0 * (middle / spread) ** 2 - 1.0
    row = lax.broadcasted_iota(jnp.int32, (size, size), 0)
    col = lax.broadcasted_iota(jnp.int32, (size, size), 1)
    unit = jnp.where(row == col, 1.0, 0.0).astype(jnp.float32)
    n = normal[...]
    guess = (8.0 * middle / spread**2 / peak) * unit - (8.0 / spread**2 / peak) * n
    whole = n.astype(jnp.bfloat16)

    def times_normal(value):
        total = None
        for _ in range(3):
            part = value.astype(jnp.bfloat16)
            value = value - part.astype(jnp.float32)
            term = jnp.dot(whole, part, preferred_element_type=jnp.float32)
            total = term if total is None else total + term
        return total

    error = 1.0 / peak
    while error > 1e-8:
        scale = 2.0 / (2.0 - error * error)
        residual = unit - times_normal(guess)
        precision = lax.Precision.HIGHEST if error < 0.1 else lax.Precision.DEFAULT
        change = jnp.dot(guess, residual, precision=precision, preferred_element_type=jnp.float32)
        guess = scale * (guess + change)
        error = error * error / (2.0 - error * error)
    out[...] = guess


def invert(normal):
    size = normal.shape[0]
    return pl.pallas_call(
        invert_kernel,
        in_specs=[vmem()],
        out_specs=vmem(),
        out_shape=jax.ShapeDtypeStruct((size, size), jnp.float32),
        name="invert",
        compiler_params=pltpu.CompilerParams(vmem_limit_bytes=GRANT),
        cost_estimate=pl.CostEstimate(
            flops=120 * size**3, transcendentals=0, bytes_accessed=8 * size * size
        ),
    )(normal)


def series_kernel(block, got, inverse, screen, motion, right, solved):
    sources, per_stripe, _, deep = got.shape[:4]
    for q in range(per_stripe):
        for part in range(2):
            lanes = pl.ds(part * LANES, LANES)
            right[:, lanes] = jnp.zeros((right.shape[0], LANES), jnp.float32)
            for s in range(sources):
                at = pl.ds(s * block, deep)
                right[at, lanes] = right[at, lanes] + got[s, q, part]
        result = jnp.dot(
            right[: inverse.shape[0], :].T,
            inverse[...],
            precision=lax.Precision.HIGHEST,
            preferred_element_type=jnp.float32,
        )
        for part in range(inverse.shape[1] // LANES):
            lanes = pl.ds(part * LANES, LANES)
            solved[...] = result[:, part * LANES : (part + 1) * LANES]
            for comp in range(2):
                for u in range(8):
                    first = solved[pl.ds(comp * 8 + u, 8, stride=16), :]
                    second = solved[pl.ds(LANES + comp * 8 + u, 8, stride=16), :]
                    screen[comp, u, pl.ds(8 * q, 8), lanes] = second
                    motion[comp, u, pl.ds(8 * q, 8), lanes] = first - second


def invert_pixels(got, inverse, block):
    per_stripe = got.shape[1]
    dates = inverse.shape[0]
    shape = jax.ShapeDtypeStruct((2, 8, 8 * per_stripe, dates), jnp.float32)
    return pl.pallas_call(
        partial(series_kernel, block),
        in_specs=[vmem(), vmem()],
        out_specs=[vmem(), vmem()],
        out_shape=[shape, shape],
        scratch_shapes=[
            pltpu.VMEM((dates + got.shape[3] - block, 2 * LANES), jnp.float32),
            pltpu.VMEM((2 * LANES, LANES), jnp.float32),
        ],
        name="series",
        compiler_params=pltpu.CompilerParams(vmem_limit_bytes=GRANT),
    )(got, inverse)


def local(images, az, rg, pair_list):
    own, _, lines, full = images.shape
    dates = az.shape[0]
    groups, along, _ = (lax.axis_size(name) for name in ("pairs", "z", "x"))
    blocks = groups * along
    block = 2 * own
    deep = -(-(block + MAXB) // 8) * 8
    rows = groups
    tiles = full // LANES
    half = tiles // 2
    per_stripe = tiles // (2 * along)
    chunks = 4 if half % 4 == 0 else 1
    width = half // chunks
    x = lax.axis_index("x")
    place = lax.axis_index(("pairs", "z"))
    info = jnp.stack([x, (2 * place + x) * own, place * block]).astype(jnp.int32)

    date_ids = jnp.arange(dates, dtype=jnp.int32)
    is_reference = date_ids[:, None] == pair_list[None, :, 0]
    is_secondary = date_ids[:, None] == pair_list[None, :, 1]
    design = (is_reference.astype(jnp.float32) - is_secondary.astype(jnp.float32)).astype(
        jnp.bfloat16
    )
    normal = jnp.dot(design, design.T, preferred_element_type=jnp.float32)
    normal = normal + damping * jnp.eye(dates, dtype=jnp.float32)
    gaps = pair_list[:, 1] - pair_list[:, 0]
    is_gap = gaps[:, None] == jnp.arange(1, MAXB + 1, dtype=jnp.int32)[None, :]
    mask = jnp.dot(
        is_reference.astype(jnp.bfloat16),
        is_gap.astype(jnp.bfloat16),
        preferred_element_type=jnp.float32,
    )
    mask = mask.astype(jnp.int32).reshape(-1)
    inverse = invert(normal)

    swap = [(0, 1), (1, 0)]
    cuts = [0, own] if own <= MAXB else [0, 2, MAXB, own]
    pieces, following = [], []
    left, turn = x == 0, 0
    for k, (start, end) in enumerate(zip(cuts, cuts[1:])):
        keep, *sends = resample(
            images,
            az,
            rg,
            info,
            start,
            end - start,
            per_stripe,
            min(chunks, 2**k),
            [p[1] for p in pieces[-1:]],
        )
        received = []
        for v in sends:
            received.append(lax.ppermute(v, "x", swap))
            turn += 1
        pieces.append((start, keep, received))
        if start >= MAXB:
            continue
        hops = []
        for c, other in enumerate(pieces[-1][2]):
            tiles = other.shape[2]
            mine = lax.slice_in_dim(keep, c * tiles, (c + 1) * tiles, axis=2)
            lower, upper = mine, other
            if own < MAXB:
                lower = jnp.concatenate([mine, other], 0)[:MAXB]
                upper = jnp.concatenate([other, mine], 0)[:MAXB]
            hops.append(jnp.where(left, lower, upper))
            if end == own:
                continue
            waited = (left, hops[-1]) if following else (left, hops[-1], inverse)
            left, hops[-1], *waited = lax.optimization_barrier(waited)
            inverse = waited[0] if waited else inverse
        if own < MAXB:
            for hop in range(1, -(-MAXB // block) + 1):
                route = [(i + hop, i) for i in range(blocks - hop)]
                count = min(block, MAXB - (hop - 1) * block)
                going = [lax.ppermute(v[:count], ("pairs", "z"), route) for v in hops]
                following.append(((hop - 1) * block, going))
        else:
            route = [(i + 1, i) for i in range(blocks - 1)]
            following.append((start, [lax.ppermute(v, ("pairs", "z"), route) for v in hops]))

    sums = []
    for c in range(chunks):
        earlier = sums[-1] if sums else None
        sums.append(
            pair_sums(
                info, mask, pieces, following, earlier, c, chunks, width, own, rows, deep
            )
        )
    partner = [lax.ppermute(s, "x", swap) for s in sums]

    lane = jnp.arange(LANES, dtype=jnp.int32)
    row_at = jnp.arange(rows, dtype=jnp.int32)[:, None] * 8 + (lane & 7)[None, :]
    tile = jnp.arange(half, dtype=jnp.int32)
    tile = (2 * (tile // per_stripe) + x) * per_stripe + tile % per_stripe
    col_at = tile[:, None] * 8 + (lane // 16)[None, :]
    row_weight = edge_weights(row_at, lines // LA)
    col_weight = edge_weights(col_at, full // LR)
    weight = 1.0 / (row_weight[None, :, :] * col_weight[:, None, :])

    outgoing = filtered(info, sums, partner, weight, per_stripe)
    outgoing = outgoing.reshape((rows * along,) + outgoing.shape[2:])
    got = lax.all_to_all(outgoing, ("pairs", "z"), split_axis=0, concat_axis=0, tiled=True)
    screen, motion = invert_pixels(got, inverse, block)
    return tuple(jnp.transpose(v, (3, 0, 1, 2)) for v in (screen, motion))


def solution(mesh):
    shape = (mesh.shape["pairs"], mesh.shape["stripe"] // 2, 2)
    if isinstance(mesh, Mesh):
        finer = Mesh(mesh.devices.reshape(shape), ("pairs", "z", "x"))
    else:
        finer = jax.sharding.AbstractMesh(shape, ("pairs", "z", "x"))
    placed = P(None, None, "pairs", ("z", "x"))

    return jax.shard_map(
        local,
        mesh=finer,
        in_specs=(P(("pairs", "z", "x"), None, None, None), P(), P(), P()),
        out_specs=(placed, placed),
        check_vma=False,
    )
```

profile of v0, /device:TPU:1, one launch (start us, length us, event | category | flops | bytes accessed | tf_op | source)
XLA Modules:
  0.0 119.7 jit_solution(9562264700424367815)
XLA Ops:
  0.6 0.1 pad_add_fusion.info
  0.7 0.0 copy-start
  0.7 2.2 %copy-done = bf16[8,2,128,1024]{3,2,1,0:T(8,128)(2,1)S(1)} copy-done((bf16[8,2,128,1024]{3,2,1,0:T(8,128)(2,1)S(1)}, bf16[8,2,128,1024]{3,2,1,0:T(8,128)(2,1)}, u32[]{:S(2)}) %copy-start) | copy-done | bytes 4194328
  2.9 0.0 copy-start.3
  2.9 0.7 copy-done.3
  3.6 0.0 copy-start.4
  3.6 0.7 copy-done.4
  4.3 2.8 %shard_map.59 = (bf16[2,2,4,128,128]{4,3,2,1,0:T(8,128)(2,1)S(1)}, bf16[2,2,4,128,128]{4,3,2,1,0:T(8,128)(2,1)}) custom-call(s32[3]{0:T(128)S(1)} %pad_add_fusion.info, s32[256]{0:T(256)S(1)} %copy-done.3, s32[256]{0:T(256)S(1)} %copy-done.4, bf16[8,2,128,1024]{3,2,1,0:T(8,128)(2,1)S(1)} %copy-done), custom_call_target="tpu_custom_call" | custom-call | flops 1048576 | bytes 2097152 | tf_op jit(solution)/shard_map/pallas_call | solution.py:98
  7.1 2.0 %collective-permute-start = (bf16[2,2,4,128,128]{4,3,2,1,0:T(8,128)(2,1)}, bf16[2,2,4,128,128]{4,3,2,1,0:T(8,128)(2,1)S(1)}, u32[]{:S(2)}, u32[]{:S(2)}) collective-permute-start(bf16[2,2,4,128,128]{4,3,2,1,0:T(8,128)(2,1)} %get-tuple-element.21), channel_id=1, source_target_pairs={{0,1},{1,0},{2,3},{3,2},{4,5},{5,4},{6,7},{7,6},{8,9},{9,8},{10,11... | collective-permute-start | bytes 1572872 | tf_op jit(solution)/shard_map/ppermute | solution.py:471
  9.1 0.0 copy-start.7
  9.1 3.7 %shard_map.60 = (bf16[3,2,4,128,128]{4,3,2,1,0:T(8,128)(2,1)S(1)}, bf16[3,2,2,128,128]{4,3,2,1,0:T(8,128)(2,1)}, bf16[3,2,2,128,128]{4,3,2,1,0:T(8,128)(2,1)}) custom-call(s32[3]{0:T(128)S(1)} %pad_add_fusion.info, s32[256]{0:T(256)S(1)} %copy-done.3, s32[256]{0:T(256)S(1)} %copy-done.4, bf16[8,2,128,1024]{3,2,1,0:T(8,128)(2,1)S(1)} %copy-done, ...), custom_call_target="tpu_custom_call" | custom-call | flops 1572864 | bytes 3145728 | tf_op jit(solution)/shard_map/pallas_call | solution.py:98
  12.8 0.0 collective-permute-start.1
  12.8 3.7 %shard_map.61 = (bf16[3,2,4,128,128]{4,3,2,1,0:T(8,128)(2,1)S(1)}, bf16[3,2,1,128,128]{4,3,2,1,0:T(8,128)(2,1)}, bf16[3,2,1,128,128]{4,3,2,1,0:T(8,128)(2,1)}, b...) custom-call(s32[3]{0:T(128)S(1)} %pad_add_fusion.info, s32[256]{0:T(256)S(1)} %copy-done.3, ...), custom_call_target="tpu_custom_call" | custom-call | flops 1572864 | bytes 3145728 | tf_op jit(solution)/shard_map/pallas_call | solution.py:98
  16.5 0.7 copy-done.5
  17.2 0.7 copy-done.6
  17.9 1.5 %collective-permute-start.2 = (bf16[3,2,1,128,128]{4,3,2,1,0:T(8,128)(2,1)}, bf16[3,2,1,128,128]{4,3,2,1,0:T(8,128)(2,1)}, u32[]{:S(2)}, u32[]{:S(2)}) collective-permute-start(bf16[3,2,1,128,128]{4,3,2,1,0:T(8,128)(2,1)} %get-tuple-element.25), channel_id=1, source_target_pairs={{0,1},{1,0},{2,3},{3,2},{4,5},{5,4},{6,7},{7,6},{8,9},{9,8},{10,11... | collective-permute-start | bytes 589832 | tf_op jit(solution)/shard_map/ppermute | solution.py:471
  19.4 0.0 collective-permute-start.5
  19.4 1.4 %collective-permute-start.6 = (bf16[3,2,2,128,128]{4,3,2,1,0:T(8,128)(2,1)}, bf16[3,2,2,128,128]{4,3,2,1,0:T(8,128)(2,1)S(1)}, u32[]{:S(2)}, u32[]{:S(2)}) collective-permute-start(bf16[3,2,2,128,128]{4,3,2,1,0:T(8,128)(2,1)} %get-tuple-element.30), channel_id=1, source_target_pairs={{0,1},{1,0},{2,3},{3,2},{4,5},{5,4},{6,7},{7,6},{8,9},{9,8},{10,11... | collective-permute-start | bytes 1179656 | tf_op jit(solution)/shard_map/ppermute | solution.py:471
  20.8 0.0 copy-done.7
  20.8 0.5 convolution_add_fusion.normal
  21.3 3.3 %invert.1.inverse = f32[256,256]{1,0:T(8,128)S(1)} custom-call(f32[256,256]{1,0:T(8,128)S(1)} %convolution_add_fusion.normal), custom_call_target="tpu_custom_call" | custom-call | flops 2013265920 | bytes 524288 | tf_op jit(solution)/shard_map/invert/pallas_call | solution.py:361
  24.6 0.0 copy-start.1
  24.6 0.5 convolution_convert_fusion
  25.2 0.6 add_multiply_fusion
  25.7 0.0 collective-permute-done.refs_1_
  25.7 0.0 copy-done.1
  25.8 0.9 broadcast_select_fusion
  26.6 7.2 %collective-permute-start.3 = (bf16[2,2,4,128,128]{4,3,2,1,0:T(8,128)(2,1)}, bf16[2,2,4,128,128]{4,3,2,1,0:T(8,128)(2,1)S(1)}, u32[]{:S(2)}, u32[]{:S(2)}) collective-permute-start(bf16[2,2,4,128,128]{4,3,2,1,0:T(8,128)(2,1)} %broadcast_select_fusion), channel_id=1, source_target_pairs={{2,0},{4,2},{6,4},{8,6},{10,8},{12,10},{14,12},{16,14},{18,16},{20... | collective-permute-start | bytes 1572872 | tf_op jit(solution)/shard_map/ppermute | solution.py:498
  33.8 0.0 collective-permute-done.1.refs_3_
  33.8 0.8 slice_select_fusion.1
  34.6 3.4 %collective-permute-start.4 = (bf16[3,2,2,128,128]{4,3,2,1,0:T(8,128)(2,1)}, bf16[3,2,2,128,128]{4,3,2,1,0:T(8,128)(2,1)}, u32[]{:S(2)}, u32[]{:S(2)}) collective-permute-start(bf16[3,2,2,128,128]{4,3,2,1,0:T(8,128)(2,1)} %slice_select_fusion.1), channel_id=1, source_target_pairs={{2,0},{4,2},{6,4},{8,6},{10,8},{12,10},{14,12},{16,14},{18,16},{20... | collective-permute-start | bytes 1179656 | tf_op jit(solution)/shard_map/ppermute | solution.py:498
  38.1 8.3 %collective-permute-done.6.refs_3_ = bf16[3,2,2,128,128]{4,3,2,1,0:T(8,128)(2,1)S(1)} collective-permute-done((bf16[3,2,2,128,128]{4,3,2,1,0:T(8,128)(2,1)}, bf16[3,2,2,128,128]{4,3,2,1,0:T(8,128)(2,1)S(1)}, u32[]{:S(2)}, u32[]{:S(2)}) %collective-permute-start.6) | collective-permute-done | bytes 393248 | tf_op jit(solution)/shard_map/ppermute | solution.py:471
  46.3 0.8 slice_select_fusion
  47.1 6.5 %collective-permute-start.8 = (bf16[3,2,2,128,128]{4,3,2,1,0:T(8,128)(2,1)}, bf16[3,2,2,128,128]{4,3,2,1,0:T(8,128)(2,1)}, u32[]{:S(2)}, u32[]{:S(2)}) collective-permute-start(bf16[3,2,2,128,128]{4,3,2,1,0:T(8,128)(2,1)} %slice_select_fusion), channel_id=1, source_target_pairs={{2,0},{4,2},{6,4},{8,6},{10,8},{12,10},{14,12},{16,14},{18,16},{20... | collective-permute-start | bytes 1179656 | tf_op jit(solution)/shard_map/ppermute | solution.py:498
  53.6 0.5 iota_and_fusion.1
  54.2 0.8 copy.6
  55.0 1.1 reshape.175.mask
  56.1 0.0 collective-permute-done.2.refs_5_
  56.1 1.3 %collective-permute-start.7 = (bf16[3,2,1,128,128]{4,3,2,1,0:T(8,128)(2,1)}, bf16[3,2,1,128,128]{4,3,2,1,0:T(8,128)(2,1)S(1)}, u32[]{:S(2)}, u32[]{:S(2)}) collective-permute-start(bf16[3,2,1,128,128]{4,3,2,1,0:T(8,128)(2,1)} %copy-done.6), channel_id=1, source_target_pairs={{0,1},{1,0},{2,3},{3,2},{4,5},{5,4},{6,7},{7,6},{8,9},{9,8},{10,11... | collective-permute-start | bytes 589832 | tf_op jit(solution)/shard_map/ppermute | solution.py:471
  57.4 0.0 collective-permute-done.4.refs_7_
  57.4 0.3 collective-permute-start.9
  57.6 0.7 select_add_fusion
  58.4 0.0 collective-permute-done.3.refs_6_
  58.4 8.5 %shard_map.62.refs_8_.rest_0_ = f32[1,4,24,128]{3,2,1,0:T(8,128)S(1)} custom-call(s32[3]{0:T(128)S(1)} %pad_add_fusion.info, s32[1280]{0:T(1024)S(1)} %reshape.175.mask, bf16[2,2,4,128,128]{4,3,2,1,0:T(8,128)(2,1)S(1)} %get-tuple-element.20.rest_0_.refs_0_, bf16[2,2,4,128,128]{4,3,2,1,0:T(8,128)(2,1)S(1)} %collective-permute-done.refs_1_, ...), custom_call_target="tpu_custom_call" | custom-call | flops 10485760 | bytes 1310720 | tf_op jit(solution)/shard_map/pallas_call | solution.py:225
  66.9 1.3 %collective-permute-start.10 = (f32[1,4,24,128]{3,2,1,0:T(8,128)S(1)}, f32[1,4,24,128]{3,2,1,0:T(8,128)S(1)}, u32[]{:S(2)}, u32[]{:S(2)}) collective-permute-start(f32[1,4,24,128]{3,2,1,0:T(8,128)S(1)} %shard_map.62.refs_8_.rest_0_), channel_id=1, source_target_pairs={{0,1},{1,0},{2,3},{3,2},{4,5},{5,4},{6,7},{7,6},{8,9},{9,8},{10,11... | collective-permute-start | bytes 147464 | tf_op jit(solution)/shard_map/ppermute | solution.py:508
  68.2 0.0 collective-permute-done.5.refs_5_
  68.2 8.5 %shard_map.63.refs_8_.rest_1_ = f32[1,4,24,128]{3,2,1,0:T(8,128)S(1)} custom-call(s32[3]{0:T(128)S(1)} %pad_add_fusion.info, s32[1280]{0:T(1024)S(1)} %reshape.175.mask, bf16[2,2,4,128,128]{4,3,2,1,0:T(8,128)(2,1)S(1)} %get-tuple-element.20.rest_0_.refs_0_, bf16[2,2,4,128,128]{4,3,2,1,0:T(8,128)(2,1)S(1)} %collective-permute-done.refs_1_, ...), custom_call_target="tpu_custom_call" | custom-call | flops 10485760 | bytes 1310720 | tf_op jit(solution)/shard_map/pallas_call | solution.py:225
  76.7 0.0 copy-start.2
  76.7 0.3 collective-permute-start.11
  77.1 0.0 collective-permute-done.7.refs_5_
  77.1 0.0 collective-permute-done.8.refs_7_
  77.1 8.4 %shard_map.64.refs_8_.rest_2_ = f32[1,4,24,128]{3,2,1,0:T(8,128)S(1)} custom-call(s32[3]{0:T(128)S(1)} %pad_add_fusion.info, s32[1280]{0:T(1024)S(1)} %reshape.175.mask, bf16[2,2,4,128,128]{4,3,2,1,0:T(8,128)(2,1)S(1)} %get-tuple-element.20.rest_0_.refs_0_, bf16[2,2,4,128,128]{4,3,2,1,0:T(8,128)(2,1)S(1)} %collective-permute-done.refs_1_, ...), custom_call_target="tpu_custom_call" | custom-call | flops 10485760 | bytes 1310720 | tf_op jit(solution)/shard_map/pallas_call | solution.py:225
  85.4 1.3 %collective-permute-start.12 = (f32[1,4,24,128]{3,2,1,0:T(8,128)S(1)}, f32[1,4,24,128]{3,2,1,0:T(8,128)S(1)}, u32[]{:S(2)}, u32[]{:S(2)}) collective-permute-start(f32[1,4,24,128]{3,2,1,0:T(8,128)S(1)} %shard_map.64.refs_8_.rest_2_), channel_id=1, source_target_pairs={{0,1},{1,0},{2,3},{3,2},{4,5},{5,4},{6,7},{7,6},{8,9},{9,8},{10,11... | collective-permute-start | bytes 147464 | tf_op jit(solution)/shard_map/ppermute | solution.py:508
  86.7 0.0 collective-permute-done.9.refs_5_
  86.7 8.4 %shard_map.65.rest_3_ = f32[1,4,24,128]{3,2,1,0:T(8,128)S(1)} custom-call(s32[3]{0:T(128)S(1)} %pad_add_fusion.info, s32[1280]{0:T(1024)S(1)} %reshape.175.mask, bf16[2,2,4,128,128]{4,3,2,1,0:T(8,128)(2,1)S(1)} %get-tuple-element.20.rest_0_.refs_0_, bf16[2,2,4,128,128]{4,3,2,1,0:T(8,128)(2,1)S(1)} %collective-permute-done.refs_1_, ...), custom_call_target="tpu_custom_call" | custom-call | flops 10485760 | bytes 1310720 | tf_op jit(solution)/shard_map/pallas_call | solution.py:225
  95.1 0.3 collective-permute-start.13
  95.4 0.0 collective-permute-done.10.rest_4_
  95.4 0.0 collective-permute-done.11.rest_5_
  95.4 0.0 collective-permute-done.12.rest_6_
  95.4 2.7 %collective-permute-done.13.rest_7_ = f32[1,4,24,128]{3,2,1,0:T(8,128)S(1)} collective-permute-done((f32[1,4,24,128]{3,2,1,0:T(8,128)S(1)}, f32[1,4,24,128]{3,2,1,0:T(8,128)S(1)}, u32[]{:S(2)}, u32[]{:S(2)}) %collective-permute-start.13) | collective-permute-done | bytes 49184 | tf_op jit(solution)/shard_map/ppermute | solution.py:508
  98.1 2.9 %smooth.1 = f32[4,4,1,2,24,128]{5,4,3,2,1,0:T(8,128)S(1)} custom-call(s32[3]{0:T(128)S(1)} %pad_add_fusion.info, f32[1,4,24,128]{3,2,1,0:T(8,128)S(1)} %shard_map.62.refs_8_.rest_0_, f32[1,4,24,128]{3,2,1,0:T(8,128)S(1)} %shard_map.63.refs_8_.rest_1_, f32[1,4,24,128]{3,2,1,0:T(8,128)S(1)} %shard_map.64.refs_8_.rest_2_, ...), custom_call_target="tpu_custom_call" | custom-call | tf_op jit(solution)/shard_map/smooth/pallas_call | solution.py:305
  101.0 17.6 %all_to_all.5.got = f32[16,1,2,24,128]{4,3,2,1,0:T(8,128)S(1)} all-to-all(f32[16,1,2,24,128]{4,3,2,1,0:T(8,128)S(1)} %bitcast.9), channel_id=1, replica_groups=mesh['pairs'=4,'z'=4,'x'=2] {'pairs','z'}, dimensions={0} | all-to-all | bytes 786432 | tf_op jit(solution)/shard_map/all_to_all | solution.py:521
  118.5 0.0 copy-done.2
  118.5 1.2 series.1
  (7 shorter events, 0.0 us)
Async XLA Ops:
  0.7 2.2 %copy-start = (bf16[8,2,128,1024]{3,2,1,0:T(8,128)(2,1)S(1)}, bf16[8,2,128,1024]{3,2,1,0:T(8,128)(2,1)}, u32[]{:S(2)}) copy-start(bf16[8,2,128,1024]{3,2,1,0:T(8,128)(2,1)} %img.5) | copy-start | bytes 12582916
  2.9 0.7 copy-start.3
  3.6 0.7 copy-start.4
  7.1 18.6 %collective-permute-start = (bf16[2,2,4,128,128]{4,3,2,1,0:T(8,128)(2,1)}, bf16[2,2,4,128,128]{4,3,2,1,0:T(8,128)(2,1)S(1)}, u32[]{:S(2)}, u32[]{:S(2)}) collective-permute-start(bf16[2,2,4,128,128]{4,3,2,1,0:T(8,128)(2,1)} %get-tuple-element.21), channel_id=1, source_target_pairs={{0,1},{1,0},{2,3},{3,2},{4,5},{5,4},{6,7},{7,6},{8,9},{9,8},{10,11... | collective-permute-start | bytes 1572872 | tf_op jit(solution)/shard_map/ppermute | solution.py:471
  9.1 11.7 %copy-start.7 = (s32[1000,2]{0,1:T(2,128)S(1)}, s32[1000,2]{0,1:T(2,128)}, u32[]{:S(2)}) copy-start(s32[1000,2]{0,1:T(2,128)} %param.7) | copy-start | bytes 24004
  12.8 21.0 %collective-permute-start.1 = (bf16[3,2,2,128,128]{4,3,2,1,0:T(8,128)(2,1)}, bf16[3,2,2,128,128]{4,3,2,1,0:T(8,128)(2,1)}, u32[]{:S(2)}, u32[]{:S(2)}) collective-permute-start(bf16[3,2,2,128,128]{4,3,2,1,0:T(8,128)(2,1)} %get-tuple-element.23), channel_id=1, source_target_pairs={{0,1},{1,0},{2,3},{3,2},{4,5},{5,4},{6,7},{7,6},{8,9},{9,8},{10,11... | collective-permute-start | bytes 1179656 | tf_op jit(solution)/shard_map/ppermute | solution.py:471
  16.5 0.7 copy-start.5
  17.2 0.7 copy-start.6
  17.9 38.2 %collective-permute-start.2 = (bf16[3,2,1,128,128]{4,3,2,1,0:T(8,128)(2,1)}, bf16[3,2,1,128,128]{4,3,2,1,0:T(8,128)(2,1)}, u32[]{:S(2)}, u32[]{:S(2)}) collective-permute-start(bf16[3,2,1,128,128]{4,3,2,1,0:T(8,128)(2,1)} %get-tuple-element.25), channel_id=1, source_target_pairs={{0,1},{1,0},{2,3},{3,2},{4,5},{5,4},{6,7},{7,6},{8,9},{9,8},{10,11... | collective-permute-start | bytes 589832 | tf_op jit(solution)/shard_map/ppermute | solution.py:471
  19.4 48.8 %collective-permute-start.5 = (bf16[3,2,1,128,128]{4,3,2,1,0:T(8,128)(2,1)}, bf16[3,2,1,128,128]{4,3,2,1,0:T(8,128)(2,1)}, u32[]{:S(2)}, u32[]{:S(2)}) collective-permute-start(bf16[3,2,1,128,128]{4,3,2,1,0:T(8,128)(2,1)} %get-tuple-element.29), channel_id=1, source_target_pairs={{0,1},{1,0},{2,3},{3,2},{4,5},{5,4},{6,7},{7,6},{8,9},{9,8},{10,11... | collective-permute-start | bytes 589832 | tf_op jit(solution)/shard_map/ppermute | solution.py:471
  19.4 27.0 %collective-permute-start.6 = (bf16[3,2,2,128,128]{4,3,2,1,0:T(8,128)(2,1)}, bf16[3,2,2,128,128]{4,3,2,1,0:T(8,128)(2,1)S(1)}, u32[]{:S(2)}, u32[]{:S(2)}) collective-permute-start(bf16[3,2,2,128,128]{4,3,2,1,0:T(8,128)(2,1)} %get-tuple-element.30), channel_id=1, source_target_pairs={{0,1},{1,0},{2,3},{3,2},{4,5},{5,4},{6,7},{7,6},{8,9},{9,8},{10,11... | collective-permute-start | bytes 1179656 | tf_op jit(solution)/shard_map/ppermute | solution.py:471
  24.6 1.2 copy-start.1
  26.6 31.7 %collective-permute-start.3 = (bf16[2,2,4,128,128]{4,3,2,1,0:T(8,128)(2,1)}, bf16[2,2,4,128,128]{4,3,2,1,0:T(8,128)(2,1)S(1)}, u32[]{:S(2)}, u32[]{:S(2)}) collective-permute-start(bf16[2,2,4,128,128]{4,3,2,1,0:T(8,128)(2,1)} %broadcast_select_fusion), channel_id=1, source_target_pairs={{2,0},{4,2},{6,4},{8,6},{10,8},{12,10},{14,12},{16,14},{18,16},{20... | collective-permute-start | bytes 1572872 | tf_op jit(solution)/shard_map/ppermute | solution.py:498
  34.6 22.7 %collective-permute-start.4 = (bf16[3,2,2,128,128]{4,3,2,1,0:T(8,128)(2,1)}, bf16[3,2,2,128,128]{4,3,2,1,0:T(8,128)(2,1)}, u32[]{:S(2)}, u32[]{:S(2)}) collective-permute-start(bf16[3,2,2,128,128]{4,3,2,1,0:T(8,128)(2,1)} %slice_select_fusion.1), channel_id=1, source_target_pairs={{2,0},{4,2},{6,4},{8,6},{10,8},{12,10},{14,12},{16,14},{18,16},{20... | collective-permute-start | bytes 1179656 | tf_op jit(solution)/shard_map/ppermute | solution.py:498
  47.1 29.9 %collective-permute-start.8 = (bf16[3,2,2,128,128]{4,3,2,1,0:T(8,128)(2,1)}, bf16[3,2,2,128,128]{4,3,2,1,0:T(8,128)(2,1)}, u32[]{:S(2)}, u32[]{:S(2)}) collective-permute-start(bf16[3,2,2,128,128]{4,3,2,1,0:T(8,128)(2,1)} %slice_select_fusion), channel_id=1, source_target_pairs={{2,0},{4,2},{6,4},{8,6},{10,8},{12,10},{14,12},{16,14},{18,16},{20... | collective-permute-start | bytes 1179656 | tf_op jit(solution)/shard_map/ppermute | solution.py:498
  56.1 21.0 %collective-permute-start.7 = (bf16[3,2,1,128,128]{4,3,2,1,0:T(8,128)(2,1)}, bf16[3,2,1,128,128]{4,3,2,1,0:T(8,128)(2,1)S(1)}, u32[]{:S(2)}, u32[]{:S(2)}) collective-permute-start(bf16[3,2,1,128,128]{4,3,2,1,0:T(8,128)(2,1)} %copy-done.6), channel_id=1, source_target_pairs={{0,1},{1,0},{2,3},{3,2},{4,5},{5,4},{6,7},{7,6},{8,9},{9,8},{10,11... | collective-permute-start | bytes 589832 | tf_op jit(solution)/shard_map/ppermute | solution.py:471
  57.4 29.3 %collective-permute-start.9 = (bf16[3,2,1,128,128]{4,3,2,1,0:T(8,128)(2,1)}, bf16[3,2,1,128,128]{4,3,2,1,0:T(8,128)(2,1)S(1)}, u32[]{:S(2)}, u32[]{:S(2)}) collective-permute-start(bf16[3,2,1,128,128]{4,3,2,1,0:T(8,128)(2,1)} %copy-done.5), channel_id=1, source_target_pairs={{0,1},{1,0},{2,3},{3,2},{4,5},{5,4},{6,7},{7,6},{8,9},{9,8},{10,11... | collective-permute-start | bytes 589832 | tf_op jit(solution)/shard_map/ppermute | solution.py:471
  66.9 28.5 %collective-permute-start.10 = (f32[1,4,24,128]{3,2,1,0:T(8,128)S(1)}, f32[1,4,24,128]{3,2,1,0:T(8,128)S(1)}, u32[]{:S(2)}, u32[]{:S(2)}) collective-permute-start(f32[1,4,24,128]{3,2,1,0:T(8,128)S(1)} %shard_map.62.refs_8_.rest_0_), channel_id=1, source_target_pairs={{0,1},{1,0},{2,3},{3,2},{4,5},{5,4},{6,7},{7,6},{8,9},{9,8},{10,11... | collective-permute-start | bytes 147464 | tf_op jit(solution)/shard_map/ppermute | solution.py:508
  76.7 41.8 %copy-start.2 = (f32[256,256]{1,0:T(8,128)S(1)}, f32[256,256]{1,0:T(8,128)}, u32[]{:S(2)}) copy-start(f32[256,256]{1,0:T(8,128)} %copy-done.1) | copy-start | bytes 786436
  76.7 18.7 %collective-permute-start.11 = (f32[1,4,24,128]{3,2,1,0:T(8,128)S(1)}, f32[1,4,24,128]{3,2,1,0:T(8,128)S(1)}, u32[]{:S(2)}, u32[]{:S(2)}) collective-permute-start(f32[1,4,24,128]{3,2,1,0:T(8,128)S(1)} %shard_map.63.refs_8_.rest_1_), channel_id=1, source_target_pairs={{0,1},{1,0},{2,3},{3,2},{4,5},{5,4},{6,7},{7,6},{8,9},{9,8},{10,11... | collective-permute-start | bytes 147464 | tf_op jit(solution)/shard_map/ppermute | solution.py:508
  85.4 10.0 %collective-permute-start.12 = (f32[1,4,24,128]{3,2,1,0:T(8,128)S(1)}, f32[1,4,24,128]{3,2,1,0:T(8,128)S(1)}, u32[]{:S(2)}, u32[]{:S(2)}) collective-permute-start(f32[1,4,24,128]{3,2,1,0:T(8,128)S(1)} %shard_map.64.refs_8_.rest_2_), channel_id=1, source_target_pairs={{0,1},{1,0},{2,3},{3,2},{4,5},{5,4},{6,7},{7,6},{8,9},{9,8},{10,11... | collective-permute-start | bytes 147464 | tf_op jit(solution)/shard_map/ppermute | solution.py:508
  95.1 3.0 %collective-permute-start.13 = (f32[1,4,24,128]{3,2,1,0:T(8,128)S(1)}, f32[1,4,24,128]{3,2,1,0:T(8,128)S(1)}, u32[]{:S(2)}, u32[]{:S(2)}) collective-permute-start(f32[1,4,24,128]{3,2,1,0:T(8,128)S(1)} %shard_map.65.rest_3_), channel_id=1, source_target_pairs={{0,1},{1,0},{2,3},{3,2},{4,5},{5,4},{6,7},{7,6},{8,9},{9,8},{10,11... | collective-permute-start | bytes 147464 | tf_op jit(solution)/shard_map/ppermute | solution.py:508
where the time goes:
time: 121 us; the launch traced here: 120 us
  Pallas kernels  51.4 us (42%)
  starting transfers between devices  26.8 us (22%)
  blocking collectives  17.6 us (15%)
  waiting for transfers between devices  11 us (9%)
  local copies, waits for them, and re-layouts  6.83 us (6%)
  other arithmetic  4.42 us (4%)
    pallas_call x4, Pallas kernels, pair_sums(): pl.pallas_call(partial(pair_kernel, own, [p[0] for p in pieces], [f[0] fo...  33.8 us
    all_to_all x1, blocking collectives, local(): lax.all_to_all(outgoing, ('pairs', 'z'), split_axis=0, concat_axis=0, til...  17.6 us
    ppermute x3, starting transfers between devices, local(): lax.ppermute(v, ('pairs', 'z'), route)  17.1 us
    pallas_call x3, Pallas kernels, resample(): pl.pallas_call(partial(resample_kernel, first, per_stripe, chunks), grid_...  10.2 us
    ppermute x7, waiting for transfers between devices, local(): received.append(lax.ppermute(v, 'x', swap))  8.3 us
    ppermute x7, starting transfers between devices, local(): received.append(lax.ppermute(v, 'x', swap))  6.49 us
    unnamed x16, local copies, waits for them, and re-layouts  4.93 us
    pallas_call x1, Pallas kernels, invert(): pl.pallas_call(invert_kernel, in_specs=[vmem()], out_specs=vmem(), out_sh...  3.27 us
  transfers between devices with their start and end apart: 14, of which 2 were waited for; matrix products, arithmetic and copies ran while one was open for 6% of the time, Pallas kernels for 37%

commit v1 on v0

v1 whole, which is shorter than its diff:
```python
from functools import partial

import jax
import jax.numpy as jnp
from jax import lax
from jax.experimental import pallas as pl
from jax.experimental.pallas import tpu as pltpu
from jax.sharding import Mesh, PartitionSpec as P


MAXB = 5
LA = 4
LR = 16
MAXA = 8
FILTER_R = 3
LANES = 128
STRIPES = 4
GRANT = 16 << 20
WHOLE_GRANT = 60 << 20
damping = 0.5


def vmem():
    return pl.BlockSpec(memory_space=pltpu.VMEM)


def tap(k):
    sigma = FILTER_R / 2.0
    return jnp.exp(-jnp.float32(k * k) / jnp.float32(2.0 * sigma * sigma))


def resample_kernel(first, parts, info, az, rg, img, *rest):
    rest = rest[-4 - parts :]
    keep, sends = rest[0], rest[1 : 1 + parts]
    tiles_of, spread, shifted = rest[1 + parts :]
    lines, full = img.shape[2], img.shape[3]
    tiles = full // LANES
    groups = tiles // (2 * STRIPES)
    blocks = lines // (8 * LA)
    high = lines + 2 * MAXA
    span = STRIPES * LANES
    date = info[1] + first + pl.program_id(0)
    x = info[0]
    shift = rg[date]
    step = az[date]
    behind = shift < 0
    origin = jnp.where(behind, -1, 0)
    amount = shift - origin * LANES
    turn = lax.rem(LANES - amount, LANES)
    lane = lax.broadcasted_iota(jnp.int32, (lines, LANES), 1)
    own = lane + amount < LANES

    @pl.when(pl.program_id(0) == 0)
    def _():
        blank = jnp.zeros((MAXA, LANES), jnp.float32)
        for t in range(shifted.shape[0] // high):
            shifted[pl.ds(t * high, MAXA), :] = blank
            shifted[pl.ds(t * high + MAXA + lines, MAXA), :] = blank
        source = lax.broadcasted_iota(jnp.int32, (span, span), 0)
        target = lax.broadcasted_iota(jnp.int32, (1, span), 1)
        column, few = target & 7, (target >> 3) & 3
        stripe, many = (target >> 5) & 3, target >> 7
        wanted = stripe * LANES + column * LR + many * 4 + few
        spread[...] = jnp.where(source == wanted, 1.0, 0.0).astype(jnp.bfloat16)

    for c in range(2):

        def turned(t):
            place = jnp.clip(t + origin, 0, tiles - 1)
            tile = img[0, c, :, pl.ds(pl.multiple_of(place * LANES, LANES), LANES)]
            out = pltpu.roll(tile.astype(jnp.float32), turn, 1)
            if t == 0:
                out = jnp.where(behind, 0.0, out)
            if t == tiles:
                out = jnp.where(behind, out, 0.0)
            return out

        here = turned(0)
        for t in range(tiles):
            after = turned(t + 1)
            group, stripe, parity = t // 2 // STRIPES, t // 2 % STRIPES, t % 2
            tiles_of[
                group, pl.ds((c * 2 + parity) * lines, lines), pl.ds(stripe * LANES, LANES)
            ] = jnp.where(own, here, after).astype(jnp.bfloat16)
            here = after

    def slab(c, parity, group, many):
        return (((c * 2 + parity) * groups + group) * 4 + many) * high + MAXA

    for group in range(groups):
        for half in range(2):
            result = jnp.dot(
                tiles_of[group],
                spread[:, half * span // 2 : (half + 1) * span // 2],
                preferred_element_type=jnp.float32,
            )
            for c in range(2):
                for parity in range(2):
                    for k in range(2):
                        at = (c * 2 + parity) * lines
                        shifted[pl.ds(slab(c, parity, group, 2 * half + k), lines), :] = result[
                            at : at + lines, k * LANES : (k + 1) * LANES
                        ]

    def put(out, place, block, c, group, parity):
        for look in range(LA):
            for pair in range(2):
                both = [
                    shifted[
                        pl.ds(
                            slab(c, parity, group, 2 * pair + k) + step + 8 * LA * block + look,
                            8,
                            stride=LA,
                        ),
                        :,
                    ]
                    for k in range(2)
                ]
                out[0, c, place, group, pl.ds(32 * look + 16 * pair, 16), :] = jnp.concatenate(
                    both, 0
                ).astype(jnp.bfloat16)

    width = blocks // parts
    for c in range(2):
        for block in range(blocks):
            for group in range(groups):
                put(sends[block // width], block % width, block, c, group, 1 - x)
                put(keep, block, block, c, group, x)


def resample(images, az, rg, info, first, count, parts, earlier):
    lines, full = images.shape[2], images.shape[3]
    tiles = full // LANES
    groups = tiles // (2 * STRIPES)
    blocks = lines // (8 * LA)
    rows = 8 * LA * 4

    def block(width):
        return pl.BlockSpec(
            (1, 2, width, groups, rows, LANES), lambda i, *_: (i, 0, 0, 0, 0, 0)
        )

    def shape(width):
        return jax.ShapeDtypeStruct((count, 2, width, groups, rows, LANES), jnp.bfloat16)

    widths = [blocks] + [blocks // parts] * parts
    return pl.pallas_call(
        partial(resample_kernel, first, parts),
        grid_spec=pltpu.PrefetchScalarGridSpec(
            num_scalar_prefetch=3,
            grid=(count,),
            in_specs=[pl.BlockSpec((1, 2, lines, full), lambda i, *_: (i + first, 0, 0, 0))]
            + [pl.BlockSpec(memory_space=pl.ANY)] * len(earlier),
            out_specs=[block(w) for w in widths],
            scratch_shapes=[
                pltpu.VMEM((groups, 4 * lines, STRIPES * LANES), jnp.bfloat16),
                pltpu.VMEM((STRIPES * LANES, STRIPES * LANES), jnp.bfloat16),
                pltpu.VMEM((16 * groups * (lines + 2 * MAXA), LANES), jnp.float32),
            ],
        ),
        out_shape=[shape(w) for w in widths],
        compiler_params=pltpu.CompilerParams(vmem_limit_bytes=WHOLE_GRANT),
        cost_estimate=pl.CostEstimate(
            flops=count * lines * full * 4,
            transcendentals=0,
            bytes_accessed=count * lines * full * 8,
        ),
    )(info, az, rg, images, *earlier)


def merge(x, y, bit, distance):
    return jnp.where(
        bit, x + pltpu.roll(x, LANES - distance, 1), y + pltpu.roll(y, distance, 1)
    )


def pair_kernel(own, starts, reached, info, mask, *refs):
    count = len(starts)
    parts, following = refs[: 2 * count], refs[2 * count : 2 * count + len(reached)]
    right, images, products, sums = refs[-4:]
    block = 2 * own
    x = info[0]
    mine, other = x * own, (1 - x) * own
    for s, start in enumerate(starts):
        for where, ref in ((mine, parts[2 * s]), (other, parts[2 * s + 1])):
            for i in range(ref.shape[0]):
                images[where + start + i] = ref[i, :, 0, 0].astype(jnp.float32)
    for start, ref in zip(reached, following):
        for i in range(ref.shape[0]):
            images[block + start + i] = ref[i, :, 0, 0].astype(jnp.float32)
    sums[...] = jnp.zeros_like(sums)

    def multiply(d, carry):
        totals = [[None] * 2 for _ in range(MAXB)]
        for k in range(images.shape[2] // 8):
            at = pl.ds(8 * k, 8)
            a, b = images[d, 0, at, :], images[d, 1, at, :]
            for g in range(MAXB):
                c, e = images[d + g + 1, 0, at, :], images[d + g + 1, 1, at, :]
                terms = (a * c + b * e, b * c - a * e)
                for comp, term in enumerate(terms):
                    old = totals[g][comp]
                    totals[g][comp] = term if old is None else old + term
        for g in range(MAXB):
            for comp in range(2):
                at = ((d * MAXB + g) * 2 + comp) * 8
                products[pl.ds(pl.multiple_of(at, 8), 8), :] = totals[g][comp]
        return carry

    lax.fori_loop(0, block, multiply, 0)
    lane = lax.broadcasted_iota(jnp.int32, (8, LANES), 1)
    real = lane & 8 == 0
    place = lane >> 4

    def slot(d, g):
        at = (d * MAXB + g) * 16
        value = merge(
            products[pl.ds(pl.multiple_of(at, 8), 8), :],
            products[pl.ds(pl.multiple_of(at + 8, 8), 8), :],
            real,
            8,
        )
        value = value + pltpu.roll(value, LANES - 16, 1)
        value = (value * (1.0 / (LA * LR))).astype(jnp.bfloat16).astype(jnp.float32)
        return value * mask[(info[2] + d) * MAXB + g].astype(jnp.float32)

    step = 4 if block % 4 == 0 else 1

    def gather(i, carry):
        totals = [None] * (step + MAXB)

        def add(at, value):
            totals[at] = value if totals[at] is None else totals[at] + value

        for j in range(step):
            for g in range(MAXB):
                value = slot(i * step + j, g)
                add(j, value)
                add(j + g + 1, -value)
        for j, value in enumerate(totals):
            at = pl.ds(pl.multiple_of(8 * (i * step + j), 8), 8)
            sums[at, :] = sums[at, :] + value
        return carry

    lax.fori_loop(0, block // step, gather, 0)
    for group in range(right.shape[1] // 8):
        rows = [sums[pl.ds(64 * group + u, 8, stride=8), :] for u in range(8)]
        turned = []
        for s in range(8):
            joined = rows[s]
            for z in range(1, STRIPES):
                joined = jnp.where(place == 2 * z, rows[(s + 2 * z) % 8], joined)
            turned.append(pltpu.roll(joined, 16 * s, 1) if s else joined)
        for z in range(STRIPES):
            out = turned[0]
            for s in range(1, 8):
                out = jnp.where(place == (2 * z + s) % 8, turned[s], out)
            right[z, pl.ds(8 * group, 8), :] = out


def pair_sums(info, mask, pieces, following, earlier, chunk, chunks, own, deep):
    groups, lines = pieces[0][1].shape[3:5]

    def window(array, parts):
        offset = chunk % (chunks // parts)
        return pl.BlockSpec(
            (array.shape[0], 2, 1, 1, lines, LANES), lambda i, *_: (0, 0, offset, i, 0, 0)
        )

    operands, specs = [], []
    for _, keep, received in pieces:
        got = received[chunk * len(received) // chunks]
        operands += [keep, got]
        specs += [window(keep, 1), window(got, len(received))]
    for _, received in following:
        got = received[chunk * len(received) // chunks]
        operands.append(got)
        specs.append(window(got, len(received)))
    if earlier is not None:
        operands.append(earlier)
        specs.append(pl.BlockSpec(memory_space=pl.ANY))
    work = 2 * own * MAXB * lines * LANES * groups
    return pl.pallas_call(
        partial(pair_kernel, own, [p[0] for p in pieces], [f[0] for f in following]),
        grid_spec=pltpu.PrefetchScalarGridSpec(
            num_scalar_prefetch=2,
            grid=(groups,),
            in_specs=specs,
            out_specs=pl.BlockSpec((STRIPES, deep, LANES), lambda i, *_: (i, 0, 0)),
            scratch_shapes=[
                pltpu.VMEM((2 * own + MAXB, 2, lines, LANES), jnp.float32),
                pltpu.VMEM((2 * own * MAXB * 16, LANES), jnp.float32),
                pltpu.VMEM((8 * deep, LANES), jnp.float32),
            ],
        ),
        out_shape=jax.ShapeDtypeStruct((groups * STRIPES, deep, LANES), jnp.float32),
        compiler_params=pltpu.CompilerParams(vmem_limit_bytes=GRANT),
        cost_estimate=pl.CostEstimate(flops=work * 8, transcendentals=0, bytes_accessed=work),
    )(info, mask, *operands)


def filter_kernel(rows, info, *rest):
    own, partner = rest[:rows], rest[rows : 2 * rows]
    weight, out, along = rest[2 * rows :]
    tiles, deep = own[0].shape[:2]
    x = info[0]
    blank = jnp.zeros((rows, deep, LANES), jnp.float32)
    along[0] = blank
    along[2 * tiles + 1] = blank
    lane = lax.broadcasted_iota(jnp.int32, (deep, LANES), 1)
    place = lane & 7
    taps = [tap(k) for k in range(FILTER_R + 1)]

    def turn(v, k):
        return pltpu.roll(v, k % LANES, 1)

    for refs, side in ((partner, 1 - x), (own, x)):
        for i in range(tiles):
            values = [ref[i] for ref in refs]
            for r in range(rows):
                acc = values[r]
                for k in range(1, FILTER_R + 1):
                    reach = 16 * k
                    last = values[r - 1] if r > 0 else jnp.zeros_like(acc)
                    later = values[r + 1] if r + 1 < rows else jnp.zeros_like(acc)
                    up = turn(jnp.where(lane >= reach, values[r], later), -reach)
                    down = turn(jnp.where(lane < LANES - reach, values[r], last), reach)
                    acc = acc + taps[k] * (up + down)
                along[2 * i + side + 1, r] = acc

    for i in range(tiles):
        at = 2 * i + x + 1
        for r in range(rows):
            v, left, right = along[at, r], along[at - 1, r], along[at + 1, r]
            acc = v
            for k in range(1, FILTER_R + 1):
                near = jnp.where(place < 8 - k, turn(v, -k), turn(right, 8 - k)) + jnp.where(
                    place >= k, turn(v, k), turn(left, k - 8)
                )
                acc = acc + taps[k] * near
            out[r, i, 0] = own[r][i]
            out[r, i, 1] = acc * weight[i, r : r + 1, :]


def filtered(info, own, partner, weight):
    rows = len(own)
    tiles, deep = own[0].shape[:2]
    smem = pl.BlockSpec(memory_space=pltpu.SMEM)
    return pl.pallas_call(
        partial(filter_kernel, rows),
        in_specs=[smem] + [vmem()] * (2 * rows + 1),
        out_specs=vmem(),
        out_shape=jax.ShapeDtypeStruct((rows, tiles, 2, deep, LANES), jnp.float32),
        scratch_shapes=[pltpu.VMEM((2 * tiles + 2, rows, deep, LANES), jnp.float32)],
        name="smooth",
        compiler_params=pltpu.CompilerParams(vmem_limit_bytes=GRANT),
    )(info, *own, *partner, weight)


def edge_weights(positions, whole):
    total = jnp.zeros(positions.shape, jnp.float32)
    for k in range(-FILTER_R, FILTER_R + 1):
        at = positions + k
        total = total + jnp.where((at >= 0) & (at < whole), tap(k), 0.0)
    return total


def invert_kernel(normal, out):
    size = normal.shape[0]
    low, high = damping, damping + 4.0 * MAXB
    middle, spread = high + low, high - low
    peak = 2.0 * (middle / spread) ** 2 - 1.0
    row = lax.broadcasted_iota(jnp.int32, (size, size), 0)
    col = lax.broadcasted_iota(jnp.int32, (size, size), 1)
    unit = jnp.where(row == col, 1.0, 0.0).astype(jnp.float32)
    n = normal[...]
    guess = (8.0 * middle / spread**2 / peak) * unit - (8.0 / spread**2 / peak) * n
    whole = n.astype(jnp.bfloat16)

    def times_normal(value):
        total = None
        for _ in range(3):
            part = value.astype(jnp.bfloat16)
            value = value - part.astype(jnp.float32)
            term = jnp.dot(whole, part, preferred_element_type=jnp.float32)
            total = term if total is None else total + term
        return total

    error = 1.0 / peak
    while error > 1e-8:
        scale = 2.0 / (2.0 - error * error)
        residual = unit - times_normal(guess)
        precision = lax.Precision.HIGHEST if error < 0.1 else lax.Precision.DEFAULT
        change = jnp.dot(guess, residual, precision=precision, preferred_element_type=jnp.float32)
        guess = scale * (guess + change)
        error = error * error / (2.0 - error * error)
    out[...] = guess


def invert(normal):
    size = normal.shape[0]
    return pl.pallas_call(
        invert_kernel,
        in_specs=[vmem()],
        out_specs=vmem(),
        out_shape=jax.ShapeDtypeStruct((size, size), jnp.float32),
        name="invert",
        compiler_params=pltpu.CompilerParams(vmem_limit_bytes=GRANT),
        cost_estimate=pl.CostEstimate(
            flops=120 * size**3, transcendentals=0, bytes_accessed=8 * size * size
        ),
    )(normal)


def series_kernel(block, got, inverse, screen, motion, right):
    sources, _, deep = got.shape[:3]
    right[...] = jnp.zeros_like(right)
    for part in range(2):
        lanes = pl.ds(part * LANES, LANES)
        for s in range(sources):
            at = pl.ds(s * block, deep)
            right[at, lanes] = right[at, lanes] + got[s, part]
    result = jnp.dot(
        right[: inverse.shape[0], :].T,
        inverse[...],
        precision=lax.Precision.HIGHEST,
        preferred_element_type=jnp.float32,
    )
    for u in range(8):
        for comp in range(2):
            at = u * 16 + comp * 8
            first, second = result[at : at + 8], result[LANES + at : LANES + at + 8]
            screen[comp, u] = second
            motion[comp, u] = first - second


def invert_pixels(got, inverse, block):
    dates = inverse.shape[0]
    shape = jax.ShapeDtypeStruct((2, 8, 8, dates), jnp.float32)
    return pl.pallas_call(
        partial(series_kernel, block),
        in_specs=[vmem(), vmem()],
        out_specs=[vmem(), vmem()],
        out_shape=[shape, shape],
        scratch_shapes=[pltpu.VMEM((dates + got.shape[2] - block, 2 * LANES), jnp.float32)],
        name="series",
        compiler_params=pltpu.CompilerParams(vmem_limit_bytes=GRANT),
    )(got, inverse)


def local(images, az, rg, pair_list):
    own, _, lines, full = images.shape
    dates = az.shape[0]
    groups, along, _ = (lax.axis_size(name) for name in ("pairs", "z", "x"))
    blocks = groups * along
    block = 2 * own
    deep = -(-(block + MAXB) // 8) * 8
    rows = groups
    if full != 2 * along * LANES or along % STRIPES or lines != rows * 8 * LA:
        raise ValueError("unsupported shape")
    x = lax.axis_index("x")
    place = lax.axis_index(("pairs", "z"))
    info = jnp.stack([x, (2 * place + x) * own, place * block]).astype(jnp.int32)

    date_ids = jnp.arange(dates, dtype=jnp.int32)
    is_reference = date_ids[:, None] == pair_list[None, :, 0]
    is_secondary = date_ids[:, None] == pair_list[None, :, 1]
    design = (is_reference.astype(jnp.float32) - is_secondary.astype(jnp.float32)).astype(
        jnp.bfloat16
    )
    normal = jnp.dot(design, design.T, preferred_element_type=jnp.float32)
    normal = normal + damping * jnp.eye(dates, dtype=jnp.float32)
    gaps = pair_list[:, 1] - pair_list[:, 0]
    is_gap = gaps[:, None] == jnp.arange(1, MAXB + 1, dtype=jnp.int32)[None, :]
    mask = jnp.dot(
        is_reference.astype(jnp.bfloat16),
        is_gap.astype(jnp.bfloat16),
        preferred_element_type=jnp.float32,
    )
    mask = mask.astype(jnp.int32).reshape(-1)
    inverse = invert(normal)

    swap = [(0, 1), (1, 0)]
    cuts = [0, own] if own <= MAXB else [0, 2, MAXB, own]
    pieces, following = [], []
    left, turn = x == 0, 0
    for k, (start, end) in enumerate(zip(cuts, cuts[1:])):
        keep, *sends = resample(
            images, az, rg, info, start, end - start, min(rows, 2**k), [p[1] for p in pieces[-1:]]
        )
        received = []
        for v in sends:
            received.append(lax.ppermute(v, "x", swap))
            turn += 1
        pieces.append((start, keep, received))
        if start >= MAXB:
            continue
        hops = []
        for c, other in enumerate(pieces[-1][2]):
            tiles = other.shape[2]
            mine = lax.slice_in_dim(keep, c * tiles, (c + 1) * tiles, axis=2)
            lower, upper = mine, other
            if own < MAXB:
                lower = jnp.concatenate([mine, other], 0)[:MAXB]
                upper = jnp.concatenate([other, mine], 0)[:MAXB]
            hops.append(jnp.where(left, lower, upper))
            if end == own:
                continue
            waited = (left, hops[-1]) if following else (left, hops[-1], inverse)
            left, hops[-1], *waited = lax.optimization_barrier(waited)
            inverse = waited[0] if waited else inverse
        if own < MAXB:
            for hop in range(1, -(-MAXB // block) + 1):
                route = [(i + hop, i) for i in range(blocks - hop)]
                count = min(block, MAXB - (hop - 1) * block)
                going = [lax.ppermute(v[:count], ("pairs", "z"), route) for v in hops]
                following.append(((hop - 1) * block, going))
        else:
            route = [(i + 1, i) for i in range(blocks - 1)]
            following.append((start, [lax.ppermute(v, ("pairs", "z"), route) for v in hops]))

    sums = []
    for c in range(rows):
        earlier = sums[-1] if sums else None
        sums.append(pair_sums(info, mask, pieces, following, earlier, c, rows, own, deep))
    partner = [lax.ppermute(s, "x", swap) for s in sums]

    lane = jnp.arange(LANES, dtype=jnp.int32)
    row_at = jnp.arange(rows, dtype=jnp.int32)[:, None] * 8 + (lane // 16)[None, :]
    stripe = 2 * jnp.arange(along, dtype=jnp.int32) + x
    col_at = stripe[:, None] * 8 + (lane & 7)[None, :]
    row_weight = edge_weights(row_at, lines // LA)
    col_weight = edge_weights(col_at, full // LR)
    weight = 1.0 / (row_weight[None, :, :] * col_weight[:, None, :])

    outgoing = filtered(info, sums, partner, weight)
    outgoing = outgoing.reshape((rows * along,) + outgoing.shape[2:])
    got = lax.all_to_all(outgoing, ("pairs", "z"), split_axis=0, concat_axis=0, tiled=True)
    screen, motion = invert_pixels(got, inverse, block)
    return tuple(jnp.transpose(v, (3, 0, 1, 2)) for v in (screen, motion))


def solution(mesh):
    shape = (mesh.shape["pairs"], mesh.shape["stripe"] // 2, 2)
    if isinstance(mesh, Mesh):
        finer = Mesh(mesh.devices.reshape(shape), ("pairs", "z", "x"))
    else:
        finer = jax.sharding.AbstractMesh(shape, ("pairs", "z", "x"))
    placed = P(None, None, "pairs", ("z", "x"))

    return jax.shard_map(
        local,
        mesh=finer,
        in_specs=(P(("pairs", "z", "x"), None, None, None), P(), P(), P()),
        out_specs=(placed, placed),
        check_vma=False,
    )
```

time: 121 us -> 102 us (0.84)
  Pallas kernels: 51.4 us -> 37.2 us
  local copies, waits for them, and re-layouts: 6.83 us -> 1.93 us
    pallas_call x4, Pallas kernels: 33.8 us -> 16.9 us  [pair_sums(): pl.pallas_call(partial(pair_kernel, own, [p[0] for p in pieces], [f[0] fo...]
    unnamed x16 -> x14, local copies, waits for them, and re-layouts: 4.93 us -> 0.03 us
    pallas_call x4, Pallas kernels: 13.1 us -> 15.8 us  [the longest x3 14 us: resample(): pl.pallas_call(partial(resample_kernel, first, parts), grid_spec=pltpu.Pr...]
  transfers between devices with their start and end apart: 14 -> 14, of which waited for: 2 -> 2; matrix products, arithmetic and copies ran while one was open for 6% -> 7% of each run, Pallas kernels for 37% -> 30%
where the time goes in v1:
time: 102 us; the launch traced here: 101 us
  Pallas kernels  37.2 us (36%)
  starting transfers between devices  25.9 us (25%)
  blocking collectives  18.5 us (18%)
  waiting for transfers between devices  10.4 us (10%)
  other arithmetic  4.96 us (5%)
  local copies, waits for them, and re-layouts  1.93 us (2%)
  matrix products  1.02 us (1%)
    all_to_all x1, blocking collectives, local(): lax.all_to_all(outgoing, ('pairs', 'z'), split_axis=0, concat_axis=0, til...  18.5 us
    pallas_call x4, Pallas kernels, pair_sums(): pl.pallas_call(partial(pair_kernel, own, [p[0] for p in pieces], [f[0] fo...  16.9 us
    ppermute x3, starting transfers between devices, local(): lax.ppermute(v, ('pairs', 'z'), route)  16.2 us
    pallas_call x3, Pallas kernels, resample(): pl.pallas_call(partial(resample_kernel, first, parts), grid_spec=pltpu.Pr...  14 us
    ppermute x7, waiting for transfers between devices, local(): received.append(lax.ppermute(v, 'x', swap))  7.78 us
    ppermute x7, starting transfers between devices, local(): received.append(lax.ppermute(v, 'x', swap))  6.5 us
    pallas_call x1, Pallas kernels, invert(): pl.pallas_call(invert_kernel, in_specs=[vmem()], out_specs=vmem(), out_sh...  3.27 us
    ppermute x4, starting transfers between devices, local(): partner = [lax.ppermute(s, 'x', swap) for s in sums]  3.19 us
  transfers between devices with their start and end apart: 14, of which 2 were waited for; matrix products, arithmetic and copies ran while one was open for 7% of the time, Pallas kernels for 30%

profile of v1, /device:TPU:1, one launch (start us, length us, event | category | flops | bytes accessed | tf_op | source)
XLA Modules:
  0.0 100.8 jit_solution(14770724767794127499)
XLA Ops:
  0.6 0.6 pad_add_fusion.info
  1.2 3.9 %shard_map.59 = (bf16[2,2,4,1,128,128]{5,4,3,2,1,0:T(8,128)(2,1)}, bf16[2,2,4,1,128,128]{5,4,3,2,1,0:T(8,128)(2,1)}) custom-call(s32[3]{0:T(128)} %pad_add_fusion.info, s32[256]{0:T(256)} %az.5, s32[256]{0:T(256)} %rg.5, bf16[8,2,128,1024]{3,2,1,0:T(8,128)(2,1)} %img.5), custom_call_target="tpu_custom_call" | custom-call | flops 1048576 | bytes 2097152 | tf_op jit(solution)/shard_map/pallas_call | solution.py:147
  5.1 2.0 %collective-permute-start = (bf16[2,2,4,1,128,128]{5,4,3,2,1,0:T(8,128)(2,1)}, bf16[2,2,4,1,128,128]{5,4,3,2,1,0:T(8,128)(2,1)S(1)}, u32[]{:S(2)}, u32[]{:S(2)}) collective-permute-start(bf16[2,2,4,1,128,128]{5,4,3,2,1,0:T(8,128)(2,1)} %get-tuple-element.21), channel_id=1, source_target_pairs={{0,1},{1,0},{2,3},{3,2},{4,5},{5,4},{6,7},{7,6},{8,9},{9,8},{10,11... | collective-permute-start | bytes 1572872 | tf_op jit(solution)/shard_map/ppermute | solution.py:493
  7.1 0.0 copy-start.6
  7.1 5.1 %shard_map.60 = (bf16[3,2,4,1,128,128]{5,4,3,2,1,0:T(8,128)(2,1)}, bf16[3,2,2,1,128,128]{5,4,3,2,1,0:T(8,128)(2,1)}, bf16[3,2,2,1,128,128]{5,4,3,2,1,0:T(8,128)(2,1)}) custom-call(s32[3]{0:T(128)} %pad_add_fusion.info, s32[256]{0:T(256)} %az.5, s32[256]{0:T(256)} %rg.5, bf16[8,2,128,1024]{3,2,1,0:T(8,128)(2,1)} %img.5, ...), custom_call_target="tpu_custom_call" | custom-call | flops 1572864 | bytes 3145728 | tf_op jit(solution)/shard_map/pallas_call | solution.py:147
  12.3 0.0 collective-permute-start.1
  12.3 5.0 %shard_map.61 = (bf16[3,2,4,1,128,128]{5,4,3,2,1,0:T(8,128)(2,1)}, bf16[3,2,1,1,128,128]{5,4,3,2,1,0:T(8,128)(2,1)}, bf16[3,2,1,1,128,128]{5,4,3,2,1,0:T(8,128)(...) custom-call(s32[3]{0:T(128)} %pad_add_fusion.info, s32[256]{0:T(256)} %az.5, s32[256]{0:T(256)} %rg.5, ...), custom_call_target="tpu_custom_call" | custom-call | flops 1572864 | bytes 3145728 | tf_op jit(solution)/shard_map/pallas_call | solution.py:147
  17.3 1.5 %collective-permute-start.2 = (bf16[3,2,1,1,128,128]{5,4,3,2,1,0:T(8,128)(2,1)}, bf16[3,2,1,1,128,128]{5,4,3,2,1,0:T(8,128)(2,1)}, u32[]{:S(2)}, u32[]{:S(2)}) collective-permute-start(bf16[3,2,1,1,128,128]{5,4,3,2,1,0:T(8,128)(2,1)} %get-tuple-element.25), channel_id=1, source_target_pairs={{0,1},{1,0},{2,3},{3,2},{4,5},{5,4},{6,7},{7,6},{8,9},{9,8},{10,11... | collective-permute-start | bytes 589832 | tf_op jit(solution)/shard_map/ppermute | solution.py:493
  18.8 0.1 collective-permute-start.5
  18.8 1.4 %collective-permute-start.6 = (bf16[3,2,2,1,128,128]{5,4,3,2,1,0:T(8,128)(2,1)}, bf16[3,2,2,1,128,128]{5,4,3,2,1,0:T(8,128)(2,1)S(1)}, u32[]{:S(2)}, u32[]{:S(2)}) collective-permute-start(bf16[3,2,2,1,128,128]{5,4,3,2,1,0:T(8,128)(2,1)} %get-tuple-element.30), channel_id=1, source_target_pairs={{0,1},{1,0},{2,3},{3,2},{4,5},{5,4},{6,7},{7,6},{8,9},{9,8},{10,11... | collective-permute-start | bytes 1179656 | tf_op jit(solution)/shard_map/ppermute | solution.py:493
  20.2 0.0 copy-done.6
  20.2 0.5 convolution_add_fusion.normal
  20.7 0.0 copy-start.1
  20.7 0.0 copy-start
  20.8 0.0 copy-start.2
  20.8 0.0 copy-start.5
  20.8 3.3 %invert.1.inverse = f32[256,256]{1,0:T(8,128)S(1)} custom-call(f32[256,256]{1,0:T(8,128)S(1)} %convolution_add_fusion.normal), custom_call_target="tpu_custom_call" | custom-call | flops 2013265920 | bytes 524288 | tf_op jit(solution)/shard_map/invert/pallas_call | solution.py:402
  24.0 0.0 copy-start.3
  24.1 0.5 convolution_convert_fusion
  24.6 0.6 add_multiply_fusion
  25.2 0.0 collective-permute-done.refs_1_
  25.2 0.0 copy-done.3
  25.2 0.0 copy-done.1
  25.2 0.9 broadcast_select_fusion
  26.1 7.2 %collective-permute-start.3 = (bf16[2,2,4,1,128,128]{5,4,3,2,1,0:T(8,128)(2,1)}, bf16[2,2,4,1,128,128]{5,4,3,2,1,0:T(8,128)(2,1)S(1)}, u32[]{:S(2)}, u32[]{:S(2)}) collective-permute-start(bf16[2,2,4,1,128,128]{5,4,3,2,1,0:T(8,128)(2,1)} %broadcast_select_fusion), channel_id=1, source_target_pairs={{2,0},{4,2},{6,4},{8,6},{10,8},{12,10},{14,12},{16,14},{18,16},{20... | collective-permute-start | bytes 1572872 | tf_op jit(solution)/shard_map/ppermute | solution.py:520
  33.2 0.0 collective-permute-done.1.refs_3_
  33.3 0.0 copy-done
  33.3 0.8 slice_select_fusion.1
  34.1 2.4 %collective-permute-start.4 = (bf16[3,2,2,1,128,128]{5,4,3,2,1,0:T(8,128)(2,1)}, bf16[3,2,2,1,128,128]{5,4,3,2,1,0:T(8,128)(2,1)}, u32[]{:S(2)}, u32[]{:S(2)}) collective-permute-start(bf16[3,2,2,1,128,128]{5,4,3,2,1,0:T(8,128)(2,1)} %slice_select_fusion.1), channel_id=1, source_target_pairs={{2,0},{4,2},{6,4},{8,6},{10,8},{12,10},{14,12},{16,14},{18,16},{20... | collective-permute-start | bytes 1179656 | tf_op jit(solution)/shard_map/ppermute | solution.py:520
  36.5 7.8 %collective-permute-done.6.refs_3_ = bf16[3,2,2,1,128,128]{5,4,3,2,1,0:T(8,128)(2,1)S(1)} collective-permute-done((bf16[3,2,2,1,128,128]{5,4,3,2,1,0:T(8,128)(2,1)}, bf16[3,2,2,1,128,128]{5,4,3,2,1,0:T(8,128)(2,1)S(1)}, u32[]{:S(2)}, u32[]{:S(2)}) %collective-permute-start.6) | collective-permute-done | bytes 393248 | tf_op jit(solution)/shard_map/ppermute | solution.py:493
  44.3 0.8 slice_select_fusion
  45.1 6.6 %collective-permute-start.8 = (bf16[3,2,2,1,128,128]{5,4,3,2,1,0:T(8,128)(2,1)}, bf16[3,2,2,1,128,128]{5,4,3,2,1,0:T(8,128)(2,1)}, u32[]{:S(2)}, u32[]{:S(2)}) collective-permute-start(bf16[3,2,2,1,128,128]{5,4,3,2,1,0:T(8,128)(2,1)} %slice_select_fusion), channel_id=1, source_target_pairs={{2,0},{4,2},{6,4},{8,6},{10,8},{12,10},{14,12},{16,14},{18,16},{20... | collective-permute-start | bytes 1179656 | tf_op jit(solution)/shard_map/ppermute | solution.py:520
  51.7 0.5 and_select_fusion
  52.2 0.8 copy.6
  53.0 1.1 %reshape.175.mask = s32[1280]{0:T(1024)S(1)} reshape(s32[256,5]{1,0:T(8,128)} %copy.6) | data formatting | bytes 10240 | tf_op jit(solution)/shard_map/reshape | solution.py:480
  54.1 0.0 collective-permute-done.2.refs_5_
  54.1 1.3 %collective-permute-start.7 = (bf16[3,2,1,1,128,128]{5,4,3,2,1,0:T(8,128)(2,1)}, bf16[3,2,1,1,128,128]{5,4,3,2,1,0:T(8,128)(2,1)S(1)}, u32[]{:S(2)}, u32[]{:S(2)}) collective-permute-start(bf16[3,2,1,1,128,128]{5,4,3,2,1,0:T(8,128)(2,1)} %get-tuple-element.31), channel_id=1, source_target_pairs={{0,1},{1,0},{2,3},{3,2},{4,5},{5,4},{6,7},{7,6},{8,9},{9,8},{10,11... | collective-permute-start | bytes 589832 | tf_op jit(solution)/shard_map/ppermute | solution.py:493
  55.4 0.0 collective-permute-done.4.refs_7_
  55.4 0.3 collective-permute-start.9
  55.7 0.7 select_add_fusion
  56.4 0.0 collective-permute-done.3.refs_6_
  56.4 0.0 copy-done.2
  56.4 0.0 copy-done.5
  56.4 4.3 %shard_map.62.refs_8_.rest_0_ = f32[4,24,128]{2,1,0:T(8,128)S(1)} custom-call(s32[3]{0:T(128)S(1)} %copy-done.5, s32[1280]{0:T(1024)S(1)} %reshape.175.mask, bf16[2,2,4,1,128,128]{5,4,3,2,1,0:T(8,128)(2,1)S(1)} %copy-done.1, bf16[2,2,4,1,128,128]{5,4,3,2,1,0:T(8,128)(2,1)S(1)} %collective-permute-done.refs_1_, bf16[3,2,4,1,128,128]{5,4,3,2,1,0:T(8,128)(2,1)S(1)} %copy-done, ...), custom_call_target="tpu_custom_call" | custom-call | flops 10485760 | bytes 1310720 | tf_op jit(solution)/shard_map/pallas_call | solution.py:283
  60.7 1.3 %collective-permute-start.10 = (f32[4,24,128]{2,1,0:T(8,128)S(1)}, f32[4,24,128]{2,1,0:T(8,128)S(1)}, u32[]{:S(2)}, u32[]{:S(2)}) collective-permute-start(f32[4,24,128]{2,1,0:T(8,128)S(1)} %shard_map.62.refs_8_.rest_0_), channel_id=1, source_target_pairs={{0,1},{1,0},{2,3},{3,2},{4,5},{5,4},{6,7},{7,6},{8,9},{9,8},{10,11... | collective-permute-start | bytes 147464 | tf_op jit(solution)/shard_map/ppermute | solution.py:526
  62.0 0.0 collective-permute-done.5.refs_5_
  62.0 4.3 %shard_map.63.refs_8_.rest_1_ = f32[4,24,128]{2,1,0:T(8,128)S(1)} custom-call(s32[3]{0:T(128)S(1)} %copy-done.5, s32[1280]{0:T(1024)S(1)} %reshape.175.mask, bf16[2,2,4,1,128,128]{5,4,3,2,1,0:T(8,128)(2,1)S(1)} %copy-done.1, bf16[2,2,4,1,128,128]{5,4,3,2,1,0:T(8,128)(2,1)S(1)} %collective-permute-done.refs_1_, bf16[3,2,4,1,128,128]{5,4,3,2,1,0:T(8,128)(2,1)S(1)} %copy-done, ...), custom_call_target="tpu_custom_call" | custom-call | flops 10485760 | bytes 1310720 | tf_op jit(solution)/shard_map/pallas_call | solution.py:283
  66.3 0.0 copy-start.4
  66.3 0.3 collective-permute-start.11
  66.7 0.0 collective-permute-done.7.refs_5_
  66.7 0.0 collective-permute-done.8.refs_7_
  66.7 4.1 %shard_map.64.refs_8_.rest_2_ = f32[4,24,128]{2,1,0:T(8,128)S(1)} custom-call(s32[3]{0:T(128)S(1)} %copy-done.5, s32[1280]{0:T(1024)S(1)} %reshape.175.mask, bf16[2,2,4,1,128,128]{5,4,3,2,1,0:T(8,128)(2,1)S(1)} %copy-done.1, bf16[2,2,4,1,128,128]{5,4,3,2,1,0:T(8,128)(2,1)S(1)} %collective-permute-done.refs_1_, bf16[3,2,4,1,128,128]{5,4,3,2,1,0:T(8,128)(2,1)S(1)} %copy-done, ...), custom_call_target="tpu_custom_call" | custom-call | flops 10485760 | bytes 1310720 | tf_op jit(solution)/shard_map/pallas_call | solution.py:283
  70.8 1.3 %collective-permute-start.12 = (f32[4,24,128]{2,1,0:T(8,128)S(1)}, f32[4,24,128]{2,1,0:T(8,128)S(1)}, u32[]{:S(2)}, u32[]{:S(2)}) collective-permute-start(f32[4,24,128]{2,1,0:T(8,128)S(1)} %shard_map.64.refs_8_.rest_2_), channel_id=1, source_target_pairs={{0,1},{1,0},{2,3},{3,2},{4,5},{5,4},{6,7},{7,6},{8,9},{9,8},{10,11... | collective-permute-start | bytes 147464 | tf_op jit(solution)/shard_map/ppermute | solution.py:526
  72.1 0.0 collective-permute-done.9.refs_5_
  72.1 4.1 %shard_map.65.rest_3_ = f32[4,24,128]{2,1,0:T(8,128)S(1)} custom-call(s32[3]{0:T(128)S(1)} %copy-done.5, s32[1280]{0:T(1024)S(1)} %reshape.175.mask, bf16[2,2,4,1,128,128]{5,4,3,2,1,0:T(8,128)(2,1)S(1)} %copy-done.1, bf16[2,2,4,1,128,128]{5,4,3,2,1,0:T(8,128)(2,1)S(1)} %collective-permute-done.refs_1_, bf16[3,2,4,1,128,128]{5,4,3,2,1,0:T(8,128)(2,1)S(1)} %copy-done, ...), custom_call_target="tpu_custom_call" | custom-call | flops 10485760 | bytes 1310720 | tf_op jit(solution)/shard_map/pallas_call | solution.py:283
  76.2 0.3 collective-permute-start.13
  76.6 0.0 collective-permute-done.10.rest_4_
  76.6 0.0 collective-permute-done.11.rest_5_
  76.6 0.0 collective-permute-done.12.rest_6_
  76.6 2.6 %collective-permute-done.13.rest_7_ = f32[4,24,128]{2,1,0:T(8,128)S(1)} collective-permute-done((f32[4,24,128]{2,1,0:T(8,128)S(1)}, f32[4,24,128]{2,1,0:T(8,128)S(1)}, u32[]{:S(2)}, u32[]{:S(2)}) %collective-permute-start.13) | collective-permute-done | bytes 49184 | tf_op jit(solution)/shard_map/ppermute | solution.py:526
  79.3 1.8 %smooth.1 = f32[4,4,2,24,128]{4,3,2,1,0:T(8,128)S(1)} custom-call(s32[3]{0:T(128)S(1)} %copy-done.5, f32[4,24,128]{2,1,0:T(8,128)S(1)} %shard_map.62.refs_8_.rest_0_, f32[4,24,128]{2,1,0:T(8,128)S(1)} %shard_map.63.refs_8_.rest_1_, f32[4,24,128]{2,1,0:T(8,128)S(1)} %shard_map.64.refs_8_.rest_2_, f32[4,24,128]{2,1,0:T(8,128)S(1)} %shard_map.65.rest_3_, ...), custom_call_target="tpu_custom_call" | custom-call | tf_op jit(solution)/shard_map/smooth/pallas_call | solution.py:349
  81.1 18.5 %all_to_all.5.got = f32[16,2,24,128]{3,2,1,0:T(8,128)S(1)} all-to-all(f32[16,2,24,128]{3,2,1,0:T(8,128)S(1)} %bitcast.9), channel_id=1, replica_groups=mesh['pairs'=4,'z'=4,'x'=2] {'pairs','z'}, dimensions={0} | all-to-all | bytes 786432 | tf_op jit(solution)/shard_map/all_to_all | solution.py:538
  99.6 0.0 copy-done.4
  99.6 1.1 %series.1 = (f32[2,8,8,256]{3,2,1,0:T(8,128)}, f32[2,8,8,256]{3,2,1,0:T(8,128)}) custom-call(f32[16,2,24,128]{3,2,1,0:T(8,128)S(1)} %all_to_all.5.got, f32[256,256]{1,0:T(8,128)S(1)} %copy-done.4), custom_call_target="tpu_custom_call" | custom-call | tf_op jit(solution)/shard_map/series/pallas_call | solution.py:440
  (5 shorter events, 0.0 us)
Async XLA Ops:
  5.1 20.1 %collective-permute-start = (bf16[2,2,4,1,128,128]{5,4,3,2,1,0:T(8,128)(2,1)}, bf16[2,2,4,1,128,128]{5,4,3,2,1,0:T(8,128)(2,1)S(1)}, u32[]{:S(2)}, u32[]{:S(2)}) collective-permute-start(bf16[2,2,4,1,128,128]{5,4,3,2,1,0:T(8,128)(2,1)} %get-tuple-element.21), channel_id=1, source_target_pairs={{0,1},{1,0},{2,3},{3,2},{4,5},{5,4},{6,7},{7,6},{8,9},{9,8},{10,11... | collective-permute-start | bytes 1572872 | tf_op jit(solution)/shard_map/ppermute | solution.py:493
  7.1 13.1 %copy-start.6 = (s32[1000,2]{0,1:T(2,128)S(1)}, s32[1000,2]{0,1:T(2,128)}, u32[]{:S(2)}) copy-start(s32[1000,2]{0,1:T(2,128)} %param.7) | copy-start | bytes 24004
  12.3 21.0 %collective-permute-start.1 = (bf16[3,2,2,1,128,128]{5,4,3,2,1,0:T(8,128)(2,1)}, bf16[3,2,2,1,128,128]{5,4,3,2,1,0:T(8,128)(2,1)}, u32[]{:S(2)}, u32[]{:S(2)}) collective-permute-start(bf16[3,2,2,1,128,128]{5,4,3,2,1,0:T(8,128)(2,1)} %get-tuple-element.23), channel_id=1, source_target_pairs={{0,1},{1,0},{2,3},{3,2},{4,5},{5,4},{6,7},{7,6},{8,9},{9,8},{10,11... | collective-permute-start | bytes 1179656 | tf_op jit(solution)/shard_map/ppermute | solution.py:493
  17.3 36.8 %collective-permute-start.2 = (bf16[3,2,1,1,128,128]{5,4,3,2,1,0:T(8,128)(2,1)}, bf16[3,2,1,1,128,128]{5,4,3,2,1,0:T(8,128)(2,1)}, u32[]{:S(2)}, u32[]{:S(2)}) collective-permute-start(bf16[3,2,1,1,128,128]{5,4,3,2,1,0:T(8,128)(2,1)} %get-tuple-element.25), channel_id=1, source_target_pairs={{0,1},{1,0},{2,3},{3,2},{4,5},{5,4},{6,7},{7,6},{8,9},{9,8},{10,11... | collective-permute-start | bytes 589832 | tf_op jit(solution)/shard_map/ppermute | solution.py:493
  18.8 43.2 %collective-permute-start.5 = (bf16[3,2,1,1,128,128]{5,4,3,2,1,0:T(8,128)(2,1)}, bf16[3,2,1,1,128,128]{5,4,3,2,1,0:T(8,128)(2,1)}, u32[]{:S(2)}, u32[]{:S(2)}) collective-permute-start(bf16[3,2,1,1,128,128]{5,4,3,2,1,0:T(8,128)(2,1)} %get-tuple-element.29), channel_id=1, source_target_pairs={{0,1},{1,0},{2,3},{3,2},{4,5},{5,4},{6,7},{7,6},{8,9},{9,8},{10,11... | collective-permute-start | bytes 589832 | tf_op jit(solution)/shard_map/ppermute | solution.py:493
  18.8 25.4 %collective-permute-start.6 = (bf16[3,2,2,1,128,128]{5,4,3,2,1,0:T(8,128)(2,1)}, bf16[3,2,2,1,128,128]{5,4,3,2,1,0:T(8,128)(2,1)S(1)}, u32[]{:S(2)}, u32[]{:S(2)}) collective-permute-start(bf16[3,2,2,1,128,128]{5,4,3,2,1,0:T(8,128)(2,1)} %get-tuple-element.30), channel_id=1, source_target_pairs={{0,1},{1,0},{2,3},{3,2},{4,5},{5,4},{6,7},{7,6},{8,9},{9,8},{10,11... | collective-permute-start | bytes 1179656 | tf_op jit(solution)/shard_map/ppermute | solution.py:493
  20.7 4.5 %copy-start.1 = (bf16[2,2,4,1,128,128]{5,4,3,2,1,0:T(8,128)(2,1)S(1)}, bf16[2,2,4,1,128,128]{5,4,3,2,1,0:T(8,128)(2,1)}, u32[]{:S(2)}) copy-start(bf16[2,2,4,1,128,128]{5,4,3,2,1,0:T(8,128)(2,1)} %get-tuple-element.20.rest_0_.refs_0_) | copy-start | bytes 1572868
  20.7 12.5 %copy-start = (bf16[3,2,4,1,128,128]{5,4,3,2,1,0:T(8,128)(2,1)S(1)}, bf16[3,2,4,1,128,128]{5,4,3,2,1,0:T(8,128)(2,1)}, u32[]{:S(2)}) copy-start(bf16[3,2,4,1,128,128]{5,4,3,2,1,0:T(8,128)(2,1)} %get-tuple-element.22.rest_0_.refs_2_) | copy-start | bytes 2359300
  20.8 35.7 %copy-start.2 = (bf16[3,2,4,1,128,128]{5,4,3,2,1,0:T(8,128)(2,1)S(1)}, bf16[3,2,4,1,128,128]{5,4,3,2,1,0:T(8,128)(2,1)}, u32[]{:S(2)}) copy-start(bf16[3,2,4,1,128,128]{5,4,3,2,1,0:T(8,128)(2,1)} %get-tuple-element.24.refs_4_) | copy-start | bytes 2359300
  20.8 35.7 %copy-start.5 = (s32[3]{0:T(128)S(1)}, s32[3]{0:T(128)}, u32[]{:S(2)}) copy-start(s32[3]{0:T(128)} %pad_add_fusion.info) | copy-start | bytes 40
  24.0 1.2 %copy-start.3 = (f32[256,256]{1,0:T(8,128)}, f32[256,256]{1,0:T(8,128)S(1)}, u32[]{:S(2)}) copy-start(f32[256,256]{1,0:T(8,128)S(1)} %invert.1.inverse) | copy-start | bytes 786436
  26.1 30.3 %collective-permute-start.3 = (bf16[2,2,4,1,128,128]{5,4,3,2,1,0:T(8,128)(2,1)}, bf16[2,2,4,1,128,128]{5,4,3,2,1,0:T(8,128)(2,1)S(1)}, u32[]{:S(2)}, u32[]{:S(2)}) collective-permute-start(bf16[2,2,4,1,128,128]{5,4,3,2,1,0:T(8,128)(2,1)} %broadcast_select_fusion), channel_id=1, source_target_pairs={{2,0},{4,2},{6,4},{8,6},{10,8},{12,10},{14,12},{16,14},{18,16},{20... | collective-permute-start | bytes 1572872 | tf_op jit(solution)/shard_map/ppermute | solution.py:520
  34.1 21.3 %collective-permute-start.4 = (bf16[3,2,2,1,128,128]{5,4,3,2,1,0:T(8,128)(2,1)}, bf16[3,2,2,1,128,128]{5,4,3,2,1,0:T(8,128)(2,1)}, u32[]{:S(2)}, u32[]{:S(2)}) collective-permute-start(bf16[3,2,2,1,128,128]{5,4,3,2,1,0:T(8,128)(2,1)} %slice_select_fusion.1), channel_id=1, source_target_pairs={{2,0},{4,2},{6,4},{8,6},{10,8},{12,10},{14,12},{16,14},{18,16},{20... | collective-permute-start | bytes 1179656 | tf_op jit(solution)/shard_map/ppermute | solution.py:520
  45.1 21.6 %collective-permute-start.8 = (bf16[3,2,2,1,128,128]{5,4,3,2,1,0:T(8,128)(2,1)}, bf16[3,2,2,1,128,128]{5,4,3,2,1,0:T(8,128)(2,1)}, u32[]{:S(2)}, u32[]{:S(2)}) collective-permute-start(bf16[3,2,2,1,128,128]{5,4,3,2,1,0:T(8,128)(2,1)} %slice_select_fusion), channel_id=1, source_target_pairs={{2,0},{4,2},{6,4},{8,6},{10,8},{12,10},{14,12},{16,14},{18,16},{20... | collective-permute-start | bytes 1179656 | tf_op jit(solution)/shard_map/ppermute | solution.py:520
  54.1 12.6 %collective-permute-start.7 = (bf16[3,2,1,1,128,128]{5,4,3,2,1,0:T(8,128)(2,1)}, bf16[3,2,1,1,128,128]{5,4,3,2,1,0:T(8,128)(2,1)S(1)}, u32[]{:S(2)}, u32[]{:S(2)}) collective-permute-start(bf16[3,2,1,1,128,128]{5,4,3,2,1,0:T(8,128)(2,1)} %get-tuple-element.31), channel_id=1, source_target_pairs={{0,1},{1,0},{2,3},{3,2},{4,5},{5,4},{6,7},{7,6},{8,9},{9,8},{10,11... | collective-permute-start | bytes 589832 | tf_op jit(solution)/shard_map/ppermute | solution.py:493
  55.4 16.7 %collective-permute-start.9 = (bf16[3,2,1,1,128,128]{5,4,3,2,1,0:T(8,128)(2,1)}, bf16[3,2,1,1,128,128]{5,4,3,2,1,0:T(8,128)(2,1)S(1)}, u32[]{:S(2)}, u32[]{:S(2)}) collective-permute-start(bf16[3,2,1,1,128,128]{5,4,3,2,1,0:T(8,128)(2,1)} %get-tuple-element.34), channel_id=1, source_target_pairs={{0,1},{1,0},{2,3},{3,2},{4,5},{5,4},{6,7},{7,6},{8,9},{9,8},{10,11... | collective-permute-start | bytes 589832 | tf_op jit(solution)/shard_map/ppermute | solution.py:493
  60.7 15.9 %collective-permute-start.10 = (f32[4,24,128]{2,1,0:T(8,128)S(1)}, f32[4,24,128]{2,1,0:T(8,128)S(1)}, u32[]{:S(2)}, u32[]{:S(2)}) collective-permute-start(f32[4,24,128]{2,1,0:T(8,128)S(1)} %shard_map.62.refs_8_.rest_0_), channel_id=1, source_target_pairs={{0,1},{1,0},{2,3},{3,2},{4,5},{5,4},{6,7},{7,6},{8,9},{9,8},{10,11... | collective-permute-start | bytes 147464 | tf_op jit(solution)/shard_map/ppermute | solution.py:526
  66.3 33.3 %copy-start.4 = (f32[256,256]{1,0:T(8,128)S(1)}, f32[256,256]{1,0:T(8,128)}, u32[]{:S(2)}) copy-start(f32[256,256]{1,0:T(8,128)} %copy-done.3) | copy-start | bytes 786436
  66.3 10.3 %collective-permute-start.11 = (f32[4,24,128]{2,1,0:T(8,128)S(1)}, f32[4,24,128]{2,1,0:T(8,128)S(1)}, u32[]{:S(2)}, u32[]{:S(2)}) collective-permute-start(f32[4,24,128]{2,1,0:T(8,128)S(1)} %shard_map.63.refs_8_.rest_1_), channel_id=1, source_target_pairs={{0,1},{1,0},{2,3},{3,2},{4,5},{5,4},{6,7},{7,6},{8,9},{9,8},{10,11... | collective-permute-start | bytes 147464 | tf_op jit(solution)/shard_map/ppermute | solution.py:526
  70.8 5.8 %collective-permute-start.12 = (f32[4,24,128]{2,1,0:T(8,128)S(1)}, f32[4,24,128]{2,1,0:T(8,128)S(1)}, u32[]{:S(2)}, u32[]{:S(2)}) collective-permute-start(f32[4,24,128]{2,1,0:T(8,128)S(1)} %shard_map.64.refs_8_.rest_2_), channel_id=1, source_target_pairs={{0,1},{1,0},{2,3},{3,2},{4,5},{5,4},{6,7},{7,6},{8,9},{9,8},{10,11... | collective-permute-start | bytes 147464 | tf_op jit(solution)/shard_map/ppermute | solution.py:526
  76.2 3.0 %collective-permute-start.13 = (f32[4,24,128]{2,1,0:T(8,128)S(1)}, f32[4,24,128]{2,1,0:T(8,128)S(1)}, u32[]{:S(2)}, u32[]{:S(2)}) collective-permute-start(f32[4,24,128]{2,1,0:T(8,128)S(1)} %shard_map.65.rest_3_), channel_id=1, source_target_pairs={{0,1},{1,0},{2,3},{3,2},{4,5},{5,4},{6,7},{7,6},{8,9},{9,8},{10,11... | collective-permute-start | bytes 147464 | tf_op jit(solution)/shard_map/ppermute | solution.py:526

commit v2 on v1

--- a/solution.py
+++ b/solution.py
@@ -222,7 +222,7 @@
         )
         value = value + pltpu.roll(value, LANES - 16, 1)
         value = (value * (1.0 / (LA * LR))).astype(jnp.bfloat16).astype(jnp.float32)
-        return value * mask[(info[2] + d) * MAXB + g].astype(jnp.float32)
+        return value * mask[g, info[2] + d].astype(jnp.float32)
 
     step = 4 if block % 4 == 0 else 1
 
@@ -243,7 +243,7 @@
         return carry
 
     lax.fori_loop(0, block // step, gather, 0)
-    for group in range(right.shape[1] // 8):
+    for group in range(right.shape[2] // 8):
         rows = [sums[pl.ds(64 * group + u, 8, stride=8), :] for u in range(8)]
         turned = []
         for s in range(8):
@@ -255,7 +255,9 @@
             out = turned[0]
             for s in range(1, 8):
                 out = jnp.where(place == (2 * z + s) % 8, turned[s], out)
-            right[z, pl.ds(8 * group, 8), :] = out
+            right[right.shape[0] - 1, z, pl.ds(8 * group, 8), :] = out
+    if right.shape[0] > 1:
+        right[0] = refs[-5][0]
 
 
 def pair_sums(info, mask, pieces, following, earlier, chunk, chunks, own, deep):
@@ -276,9 +278,14 @@
         got = received[chunk * len(received) // chunks]
         operands.append(got)
         specs.append(window(got, len(received)))
+    joined = chunk == 1
     if earlier is not None:
         operands.append(earlier)
-        specs.append(pl.BlockSpec(memory_space=pl.ANY))
+        specs.append(
+            pl.BlockSpec((1, STRIPES, deep, LANES), lambda i, *_: (0, i, 0, 0))
+            if joined
+            else pl.BlockSpec(memory_space=pl.ANY)
+        )
     work = 2 * own * MAXB * lines * LANES * groups
     return pl.pallas_call(
         partial(pair_kernel, own, [p[0] for p in pieces], [f[0] for f in following]),
@@ -286,22 +293,26 @@
             num_scalar_prefetch=2,
             grid=(groups,),
             in_specs=specs,
-            out_specs=pl.BlockSpec((STRIPES, deep, LANES), lambda i, *_: (i, 0, 0)),
+            out_specs=pl.BlockSpec((1 + joined, STRIPES, deep, LANES), lambda i, *_: (0, i, 0, 0)),
             scratch_shapes=[
                 pltpu.VMEM((2 * own + MAXB, 2, lines, LANES), jnp.float32),
                 pltpu.VMEM((2 * own * MAXB * 16, LANES), jnp.float32),
                 pltpu.VMEM((8 * deep, LANES), jnp.float32),
             ],
         ),
-        out_shape=jax.ShapeDtypeStruct((groups * STRIPES, deep, LANES), jnp.float32),
+        out_shape=jax.ShapeDtypeStruct((1 + joined, groups * STRIPES, deep, LANES), jnp.float32),
         compiler_params=pltpu.CompilerParams(vmem_limit_bytes=GRANT),
         cost_estimate=pl.CostEstimate(flops=work * 8, transcendentals=0, bytes_accessed=work),
     )(info, mask, *operands)
 
 
-def filter_kernel(rows, info, *rest):
-    own, partner = rest[:rows], rest[rows : 2 * rows]
-    weight, out, along = rest[2 * rows :]
+def filter_kernel(count, info, *rest):
+    weight, out, along = rest[2 * count :]
+    own, partner = (
+        [ref.at[i] for ref in refs for i in range(ref.shape[0])]
+        for refs in (rest[:count], rest[count : 2 * count])
+    )
+    rows = len(own)
     tiles, deep = own[0].shape[:2]
     x = info[0]
     blank = jnp.zeros((rows, deep, LANES), jnp.float32)
@@ -343,12 +354,13 @@
 
 
 def filtered(info, own, partner, weight):
-    rows = len(own)
-    tiles, deep = own[0].shape[:2]
+    count = len(own)
+    rows = sum(v.shape[0] for v in own)
+    tiles, deep = own[0].shape[1:3]
     smem = pl.BlockSpec(memory_space=pltpu.SMEM)
     return pl.pallas_call(
-        partial(filter_kernel, rows),
-        in_specs=[smem] + [vmem()] * (2 * rows + 1),
+        partial(filter_kernel, count),
+        in_specs=[smem] + [vmem()] * (2 * count + 1),
         out_specs=vmem(),
         out_shape=jax.ShapeDtypeStruct((rows, tiles, 2, deep, LANES), jnp.float32),
         scratch_shapes=[pltpu.VMEM((2 * tiles + 2, rows, deep, LANES), jnp.float32)],
@@ -471,44 +483,32 @@
     normal = jnp.dot(design, design.T, preferred_element_type=jnp.float32)
     normal = normal + damping * jnp.eye(dates, dtype=jnp.float32)
     gaps = pair_list[:, 1] - pair_list[:, 0]
-    is_gap = gaps[:, None] == jnp.arange(1, MAXB + 1, dtype=jnp.int32)[None, :]
+    is_gap = jnp.arange(1, MAXB + 1, dtype=jnp.int32)[:, None] == gaps[None, :]
     mask = jnp.dot(
-        is_reference.astype(jnp.bfloat16),
         is_gap.astype(jnp.bfloat16),
+        is_reference.astype(jnp.bfloat16).T,
         preferred_element_type=jnp.float32,
     )
-    mask = mask.astype(jnp.int32).reshape(-1)
+    mask = mask.astype(jnp.int32)
     inverse = invert(normal)
 
     swap = [(0, 1), (1, 0)]
     cuts = [0, own] if own <= MAXB else [0, 2, MAXB, own]
     pieces, following = [], []
-    left, turn = x == 0, 0
-    for k, (start, end) in enumerate(zip(cuts, cuts[1:])):
-        keep, *sends = resample(
-            images, az, rg, info, start, end - start, min(rows, 2**k), [p[1] for p in pieces[-1:]]
-        )
-        received = []
-        for v in sends:
-            received.append(lax.ppermute(v, "x", swap))
-            turn += 1
-        pieces.append((start, keep, received))
-        if start >= MAXB:
-            continue
+    left, turn, leaving = x == 0, 0, None
+
+    def send_back(start, keep, received, left, inverse):
         hops = []
-        for c, other in enumerate(pieces[-1][2]):
-            tiles = other.shape[2]
-            mine = lax.slice_in_dim(keep, c * tiles, (c + 1) * tiles, axis=2)
+        for c, other in enumerate(received):
+            part = other.shape[2]
+            mine = lax.slice_in_dim(keep, c * part, (c + 1) * part, axis=2)
             lower, upper = mine, other
             if own < MAXB:
                 lower = jnp.concatenate([mine, other], 0)[:MAXB]
                 upper = jnp.concatenate([other, mine], 0)[:MAXB]
             hops.append(jnp.where(left, lower, upper))
-            if end == own:
-                continue
-            waited = (left, hops[-1]) if following else (left, hops[-1], inverse)
-            left, hops[-1], *waited = lax.optimization_barrier(waited)
-            inverse = waited[0] if waited else inverse
+            if own > MAXB:
+                left, hops[-1], inverse = lax.optimization_barrier((left, hops[-1], inverse))
         if own < MAXB:
             for hop in range(1, -(-MAXB // block) + 1):
                 route = [(i + hop, i) for i in range(blocks - hop)]
@@ -517,12 +517,34 @@
                 following.append(((hop - 1) * block, going))
         else:
             route = [(i + 1, i) for i in range(blocks - 1)]
-            following.append((start, [lax.ppermute(v, ("pairs", "z"), route) for v in hops]))
+            going = []
+            for v in hops:
+                going.append(lax.ppermute(v, ("pairs", "z"), route))
+            following.append((start, going))
+        return hops[0], left, inverse
+
+    for k, (start, end) in enumerate(zip(cuts, cuts[1:])):
+        after = [p[1] for p in pieces[-1:]] + [v for v in (leaving,) if v is not None]
+        keep, *sends = resample(
+            images, az, rg, info, start, end - start, min(rows, 2**k), after
+        )
+        received = []
+        for v in sends:
+            received.append(lax.ppermute(v, "x", swap))
+            turn += 1
+        pieces.append((start, keep, received))
+        if k > 0:
+            if k == len(cuts) - 2:
+                left, _ = lax.optimization_barrier((left, keep))
+            leaving, left, inverse = send_back(*pieces[k - 1], left, inverse)
+    if cuts[-2] < MAXB:
+        send_back(*pieces[-1], left, inverse)
 
     sums = []
     for c in range(rows):
         earlier = sums[-1] if sums else None
         sums.append(pair_sums(info, mask, pieces, following, earlier, c, rows, own, deep))
+    sums = sums[1:]
     partner = [lax.ppermute(s, "x", swap) for s in sums]
 
     lane = jnp.arange(LANES, dtype=jnp.int32)

time: 102 us -> 92.3 us (0.905)
  waiting for transfers between devices: 10.4 us -> 3.31 us
  blocking collectives: 18.5 us -> 22.6 us
  other arithmetic: 4.96 us -> 0.87 us
  Pallas kernels: 37.2 us -> 33.5 us
  starting transfers between devices: 25.9 us -> 28.1 us
    ppermute x7, waiting for transfers between devices: 7.78 us -> 1.24 us  [local(): received.append(lax.ppermute(v, 'x', swap))]
    all_to_all x1, blocking collectives: 18.5 us -> 22.6 us  [local(): lax.all_to_all(outgoing, ('pairs', 'z'), split_axis=0, concat_axis=0, til...]
    pallas_call x4, Pallas kernels: 16.9 us -> 13.1 us  [pair_sums(): pl.pallas_call(partial(pair_kernel, own, [p[0] for p in pieces], [f[0] fo...]
    select_n x3, other arithmetic: 2.5 us -> 0.14 us  [send_back(): hops.append(jnp.where(left, lower, upper))]
    ppermute x3, starting transfers between devices: 16.2 us -> 18 us  [send_back(): going.append(lax.ppermute(v, ('pairs', 'z'), route))]
    unnamed x14 -> x12, local copies, waits for them, and re-layouts: 0.03 us -> 1.15 us
    reshape x1 -> x0, local copies, waits for them, and re-layouts: 1.1 us -> none  [local(): mask = mask.astype(jnp.int32).reshape(-1)]
    ppermute x7, starting transfers between devices: 6.5 us -> 7.54 us  [local(): received.append(lax.ppermute(v, 'x', swap))]
  transfers between devices with their start and end apart: 14 -> 13, of which waited for: 2 -> 2; matrix products, arithmetic and copies ran while one was open for 7% -> 1% of each run, Pallas kernels for 30% -> 29%
where the time goes in v2:
time: 92.3 us; the launch traced here: 91.1 us
  Pallas kernels  33.5 us (36%)
  starting transfers between devices  28.1 us (30%)
  blocking collectives  22.6 us (24%)
  waiting for transfers between devices  3.31 us (4%)
  local copies, waits for them, and re-layouts  1.15 us (1%)
    all_to_all x1, blocking collectives, local(): lax.all_to_all(outgoing, ('pairs', 'z'), split_axis=0, concat_axis=0, til...  22.6 us
    ppermute x3, starting transfers between devices, send_back(): going.append(lax.ppermute(v, ('pairs', 'z'), route))  18 us
    pallas_call x3, Pallas kernels, resample(): pl.pallas_call(partial(resample_kernel, first, parts), grid_spec=pltpu.Pr...  14.2 us
    pallas_call x4, Pallas kernels, pair_sums(): pl.pallas_call(partial(pair_kernel, own, [p[0] for p in pieces], [f[0] fo...  13.1 us
    ppermute x7, starting transfers between devices, local(): received.append(lax.ppermute(v, 'x', swap))  7.54 us
    pallas_call x1, Pallas kernels, invert(): pl.pallas_call(invert_kernel, in_specs=[vmem()], out_specs=vmem(), out_sh...  3.26 us
    ppermute x3, starting transfers between devices, local(): partner = [lax.ppermute(s, 'x', swap) for s in sums]  2.53 us
    ppermute x3, waiting for transfers between devices, local(): partner = [lax.ppermute(s, 'x', swap) for s in sums]  2.07 us
  transfers between devices with their start and end apart: 13, of which 2 were waited for; matrix products, arithmetic and copies ran while one was open for 1% of the time, Pallas kernels for 29%

profile of v2, /device:TPU:1, one launch (start us, length us, event | category | flops | bytes accessed | tf_op | source)
XLA Modules:
  0.0 91.1 jit_solution(16681898107148056691)
XLA Ops:
  0.6 0.6 pad_add_fusion.info
  1.3 0.0 copy-start.5
  1.3 4.0 %shard_map.59 = (bf16[2,2,4,1,128,128]{5,4,3,2,1,0:T(8,128)(2,1)}, bf16[2,2,4,1,128,128]{5,4,3,2,1,0:T(8,128)(2,1)}) custom-call(s32[3]{0:T(128)} %pad_add_fusion.info, s32[256]{0:T(256)} %az.5, s32[256]{0:T(256)} %rg.5, bf16[8,2,128,1024]{3,2,1,0:T(8,128)(2,1)} %img.5), custom_call_target="tpu_custom_call" | custom-call | flops 1048576 | bytes 2097152 | tf_op jit(solution)/shard_map/pallas_call | solution.py:147
  5.3 2.1 %collective-permute-start = (bf16[2,2,4,1,128,128]{5,4,3,2,1,0:T(8,128)(2,1)}, bf16[2,2,4,1,128,128]{5,4,3,2,1,0:T(8,128)(2,1)S(1)}, u32[]{:S(2)}, u32[]{:S(2)}) collective-permute-start(bf16[2,2,4,1,128,128]{5,4,3,2,1,0:T(8,128)(2,1)} %get-tuple-element.24), channel_id=1, source_target_pairs={{0,1},{1,0},{2,3},{3,2},{4,5},{5,4},{6,7},{7,6},{8,9},{9,8},{10,11... | collective-permute-start | bytes 1572872 | tf_op jit(solution)/shard_map/ppermute | solution.py:533
  7.3 5.1 %shard_map.60 = (bf16[3,2,4,1,128,128]{5,4,3,2,1,0:T(8,128)(2,1)}, bf16[3,2,2,1,128,128]{5,4,3,2,1,0:T(8,128)(2,1)}, bf16[3,2,2,1,128,128]{5,4,3,2,1,0:T(8,128)(2,1)}) custom-call(s32[3]{0:T(128)} %pad_add_fusion.info, s32[256]{0:T(256)} %az.5, s32[256]{0:T(256)} %rg.5, bf16[8,2,128,1024]{3,2,1,0:T(8,128)(2,1)} %img.5, ...), custom_call_target="tpu_custom_call" | custom-call | flops 1572864 | bytes 3145728 | tf_op jit(solution)/shard_map/pallas_call | solution.py:147
  12.4 0.0 collective-permute-start.1
  12.4 1.5 %collective-permute-start.6 = (bf16[3,2,2,1,128,128]{5,4,3,2,1,0:T(8,128)(2,1)}, bf16[3,2,2,1,128,128]{5,4,3,2,1,0:T(8,128)(2,1)S(1)}, u32[]{:S(2)}, u32[]{:S(2)}) collective-permute-start(bf16[3,2,2,1,128,128]{5,4,3,2,1,0:T(8,128)(2,1)} %get-tuple-element.35), channel_id=1, source_target_pairs={{0,1},{1,0},{2,3},{3,2},{4,5},{5,4},{6,7},{7,6},{8,9},{9,8},{10,11... | collective-permute-start | bytes 1179656 | tf_op jit(solution)/shard_map/ppermute | solution.py:533
  13.9 0.0 copy-done.5
  13.9 0.5 convolution_add_fusion.normal
  14.4 0.0 copy-start.1
  14.4 3.3 %invert.1.inverse = f32[256,256]{1,0:T(8,128)S(1)} custom-call(f32[256,256]{1,0:T(8,128)S(1)} %convolution_add_fusion.normal), custom_call_target="tpu_custom_call" | custom-call | flops 2013265920 | bytes 524288 | tf_op jit(solution)/shard_map/invert/pallas_call | solution.py:414
  17.7 0.0 copy-start
  17.7 0.3 convolution_convert_fusion.mask
  18.0 1.2 %collective-permute-done.refs_1_ = bf16[2,2,4,1,128,128]{5,4,3,2,1,0:T(8,128)(2,1)S(1)} collective-permute-done((bf16[2,2,4,1,128,128]{5,4,3,2,1,0:T(8,128)(2,1)}, bf16[2,2,4,1,128,128]{5,4,3,2,1,0:T(8,128)(2,1)S(1)}, u32[]{:S(2)}, u32[]{:S(2)}) %collective-permute-start) | collective-permute-done | bytes 524320 | tf_op jit(solution)/shard_map/ppermute | solution.py:533
  19.2 0.0 copy-done.1
  19.2 0.1 broadcast_select_fusion.rest_1_
  19.3 0.0 copy-start.4
  19.3 0.0 copy-start.3
  19.3 7.7 %collective-permute-start.3 = (bf16[2,2,4,1,128,128]{5,4,3,2,1,0:T(8,128)(2,1)S(1)}, bf16[2,2,4,1,128,128]{5,4,3,2,1,0:T(8,128)(2,1)S(1)}, u32[]{:S(2)}, u32[]{:S(2)}) collective-permute-start(bf16[2,2,4,1,128,128]{5,4,3,2,1,0:T(8,128)(2,1)S(1)} %broadcast_select_fusion.rest_1_), channel_id=1, source_target_pairs={{2,0},{4,2},{6,4},{8,6},{10,8},{12,10},{14,12},{16,14},{18,16},{20... | collective-permute-start | bytes 1572872 | tf_op jit(solution)/shard_map/ppermute | solution.py:522
  27.0 0.0 copy-done.4
  27.0 5.1 %shard_map.61 = (bf16[3,2,4,1,128,128]{5,4,3,2,1,0:T(8,128)(2,1)}, bf16[3,2,1,1,128,128]{5,4,3,2,1,0:T(8,128)(2,1)}, bf16[3,2,1,1,128,128]{5,4,3,2,1,0:T(8,128)(...) custom-call(s32[3]{0:T(128)} %pad_add_fusion.info, s32[256]{0:T(256)} %az.5, s32[256]{0:T(256)} %rg.5, ...), custom_call_target="tpu_custom_call" | custom-call | flops 1572864 | bytes 3145728 | tf_op jit(solution)/shard_map/pallas_call | solution.py:147
  32.1 0.0 collective-permute-done.1.refs_3_
  32.1 0.0 copy-done
  32.1 3.2 %collective-permute-start.4 = (bf16[3,2,2,1,128,128]{5,4,3,2,1,0:T(8,128)(2,1)S(1)}, bf16[3,2,2,1,128,128]{5,4,3,2,1,0:T(8,128)(2,1)S(1)}, u32[]{:S(2)}, u32[]{:S(2)}) collective-permute-start(bf16[3,2,2,1,128,128]{5,4,3,2,1,0:T(8,128)(2,1)S(1)} %slice_select_fusion.1), channel_id=1, source_target_pairs={{2,0},{4,2},{6,4},{8,6},{10,8},{12,10},{14,12},{16,14},{18,16},{20... | collective-permute-start | bytes 1179656 | tf_op jit(solution)/shard_map/ppermute | solution.py:522
  35.4 1.3 %collective-permute-start.5 = (bf16[3,2,1,1,128,128]{5,4,3,2,1,0:T(8,128)(2,1)}, bf16[3,2,1,1,128,128]{5,4,3,2,1,0:T(8,128)(2,1)S(1)}, u32[]{:S(2)}, u32[]{:S(2)}) collective-permute-start(bf16[3,2,1,1,128,128]{5,4,3,2,1,0:T(8,128)(2,1)} %get-tuple-element.34), channel_id=1, source_target_pairs={{0,1},{1,0},{2,3},{3,2},{4,5},{5,4},{6,7},{7,6},{8,9},{9,8},{10,11... | collective-permute-start | bytes 589832 | tf_op jit(solution)/shard_map/ppermute | solution.py:533
  36.7 0.0 collective-permute-done.6.refs_3_
  36.7 7.1 %collective-permute-start.8 = (bf16[3,2,2,1,128,128]{5,4,3,2,1,0:T(8,128)(2,1)S(1)}, bf16[3,2,2,1,128,128]{5,4,3,2,1,0:T(8,128)(2,1)S(1)}, u32[]{:S(2)}, u32[]{:S(2)}) collective-permute-start(bf16[3,2,2,1,128,128]{5,4,3,2,1,0:T(8,128)(2,1)S(1)} %slice_select_fusion), channel_id=1, source_target_pairs={{2,0},{4,2},{6,4},{8,6},{10,8},{12,10},{14,12},{16,14},{18,16},{20... | collective-permute-start | bytes 1179656 | tf_op jit(solution)/shard_map/ppermute | solution.py:522
  43.8 1.3 %collective-permute-start.2 = (bf16[3,2,1,1,128,128]{5,4,3,2,1,0:T(8,128)(2,1)}, bf16[3,2,1,1,128,128]{5,4,3,2,1,0:T(8,128)(2,1)S(1)}, u32[]{:S(2)}, u32[]{:S(2)}) collective-permute-start(bf16[3,2,1,1,128,128]{5,4,3,2,1,0:T(8,128)(2,1)} %get-tuple-element.29), channel_id=1, source_target_pairs={{0,1},{1,0},{2,3},{3,2},{4,5},{5,4},{6,7},{7,6},{8,9},{9,8},{10,11... | collective-permute-start | bytes 589832 | tf_op jit(solution)/shard_map/ppermute | solution.py:533
  45.1 0.0 collective-permute-done.5.refs_5_
  45.1 0.3 collective-permute-start.7
  45.4 0.0 collective-permute-done.4.refs_7_
  45.4 1.2 %collective-permute-start.9 = (bf16[3,2,1,1,128,128]{5,4,3,2,1,0:T(8,128)(2,1)}, bf16[3,2,1,1,128,128]{5,4,3,2,1,0:T(8,128)(2,1)S(1)}, u32[]{:S(2)}, u32[]{:S(2)}) collective-permute-start(bf16[3,2,1,1,128,128]{5,4,3,2,1,0:T(8,128)(2,1)} %get-tuple-element.40), channel_id=1, source_target_pairs={{0,1},{1,0},{2,3},{3,2},{4,5},{5,4},{6,7},{7,6},{8,9},{9,8},{10,11... | collective-permute-start | bytes 589832 | tf_op jit(solution)/shard_map/ppermute | solution.py:533
  46.6 0.1 select_add_fusion
  46.7 0.0 collective-permute-done.3.refs_6_
  46.7 0.0 copy-done.3
  46.7 0.0 copy-start.2
  46.7 1.1 %copy-done.2 = bf16[3,2,4,1,128,128]{5,4,3,2,1,0:T(8,128)(2,1)S(1)} copy-done((bf16[3,2,4,1,128,128]{5,4,3,2,1,0:T(8,128)(2,1)S(1)}, bf16[3,2,4,1,128,128]{5,4,3,2,1,0:T(8,128)(2,1)}, u32[]{:S(2)}) %copy-start.2) | copy-done | bytes 786456
  47.8 3.3 %shard_map.62.refs_8_ = f32[1,4,24,128]{3,2,1,0:T(8,128)S(1)} custom-call(s32[3]{0:T(128)S(1)} %copy-done.3, s32[5,256]{1,0:T(8,128)S(1)} %convolution_convert_fusion.mask, bf16[2,2,4,1,128,128]{5,4,3,2,1,0:T(8,128)(2,1)S(1)} %copy-done.1, bf16[2,2,4,1,128,128]{5,4,3,2,1,0:T(8,128)(2,1)S(1)} %collective-permute-done.refs_1_, ...), custom_call_target="tpu_custom_call" | custom-call | flops 10485760 | bytes 1310720 | tf_op jit(solution)/shard_map/pallas_call | solution.py:290
  51.1 0.0 collective-permute-done.2.refs_5_
  51.1 3.3 %shard_map.63.refs_8_.rest_0_ = f32[2,4,24,128]{3,2,1,0:T(8,128)S(1)} custom-call(s32[3]{0:T(128)S(1)} %copy-done.3, s32[5,256]{1,0:T(8,128)S(1)} %convolution_convert_fusion.mask, bf16[2,2,4,1,128,128]{5,4,3,2,1,0:T(8,128)(2,1)S(1)} %copy-done.1, bf16[2,2,4,1,128,128]{5,4,3,2,1,0:T(8,128)(2,1)S(1)} %collective-permute-done.refs_1_, ...), custom_call_target="tpu_custom_call" | custom-call | flops 10485760 | bytes 1310720 | tf_op jit(solution)/shard_map/pallas_call | solution.py:290
  54.4 0.9 %collective-permute-start.10 = (f32[2,4,24,128]{3,2,1,0:T(8,128)S(1)}, f32[2,4,24,128]{3,2,1,0:T(8,128)S(1)}, u32[]{:S(2)}, u32[]{:S(2)}) collective-permute-start(f32[2,4,24,128]{3,2,1,0:T(8,128)S(1)} %shard_map.63.refs_8_.rest_0_), channel_id=1, source_target_pairs={{0,1},{1,0},{2,3},{3,2},{4,5},{5,4},{6,7},{7,6},{8,9},{9,8},{10,11... | collective-permute-start | bytes 294920 | tf_op jit(solution)/shard_map/ppermute | solution.py:548
  55.3 0.0 collective-permute-done.7.refs_5_
  55.3 0.0 collective-permute-done.8.refs_7_
  55.3 3.3 %shard_map.64.refs_8_.rest_1_ = f32[1,4,24,128]{3,2,1,0:T(8,128)S(1)} custom-call(s32[3]{0:T(128)S(1)} %copy-done.3, s32[5,256]{1,0:T(8,128)S(1)} %convolution_convert_fusion.mask, bf16[2,2,4,1,128,128]{5,4,3,2,1,0:T(8,128)(2,1)S(1)} %copy-done.1, bf16[2,2,4,1,128,128]{5,4,3,2,1,0:T(8,128)(2,1)S(1)} %collective-permute-done.refs_1_, ...), custom_call_target="tpu_custom_call" | custom-call | flops 10485760 | bytes 1310720 | tf_op jit(solution)/shard_map/pallas_call | solution.py:290
  58.6 0.7 collective-permute-start.11
  59.3 0.0 collective-permute-done.9.refs_5_
  59.3 3.3 %shard_map.65.rest_2_ = f32[1,4,24,128]{3,2,1,0:T(8,128)S(1)} custom-call(s32[3]{0:T(128)S(1)} %copy-done.3, s32[5,256]{1,0:T(8,128)S(1)} %convolution_convert_fusion.mask, bf16[2,2,4,1,128,128]{5,4,3,2,1,0:T(8,128)(2,1)S(1)} %copy-done.1, bf16[2,2,4,1,128,128]{5,4,3,2,1,0:T(8,128)(2,1)S(1)} %collective-permute-done.refs_1_, ...), custom_call_target="tpu_custom_call" | custom-call | flops 10485760 | bytes 1310720 | tf_op jit(solution)/shard_map/pallas_call | solution.py:290
  62.6 0.9 %collective-permute-start.12 = (f32[1,4,24,128]{3,2,1,0:T(8,128)S(1)}, f32[1,4,24,128]{3,2,1,0:T(8,128)S(1)}, u32[]{:S(2)}, u32[]{:S(2)}) collective-permute-start(f32[1,4,24,128]{3,2,1,0:T(8,128)S(1)} %shard_map.65.rest_2_), channel_id=1, source_target_pairs={{0,1},{1,0},{2,3},{3,2},{4,5},{5,4},{6,7},{7,6},{8,9},{9,8},{10,11... | collective-permute-start | bytes 147464 | tf_op jit(solution)/shard_map/ppermute | solution.py:548
  63.5 0.0 collective-permute-done.11.rest_4_
  63.5 2.1 %collective-permute-done.12.rest_5_ = f32[1,4,24,128]{3,2,1,0:T(8,128)S(1)} collective-permute-done((f32[1,4,24,128]{3,2,1,0:T(8,128)S(1)}, f32[1,4,24,128]{3,2,1,0:T(8,128)S(1)}, u32[]{:S(2)}, u32[]{:S(2)}) %collective-permute-start.12) | collective-permute-done | bytes 49184 | tf_op jit(solution)/shard_map/ppermute | solution.py:548
  65.6 0.0 collective-permute-done.10.rest_3_
  65.6 1.8 %smooth.1 = f32[4,4,2,24,128]{4,3,2,1,0:T(8,128)S(1)} custom-call(s32[3]{0:T(128)S(1)} %copy-done.3, f32[2,4,24,128]{3,2,1,0:T(8,128)S(1)} %shard_map.63.refs_8_.rest_0_, f32[1,4,24,128]{3,2,1,0:T(8,128)S(1)} %shard_map.64.refs_8_.rest_1_, f32[1,4,24,128]{3,2,1,0:T(8,128)S(1)} %shard_map.65.rest_2_, f32[2,4,24,128]{3,2,1,0:T(8,128)S(1)} %collective-permute-done.10.rest_3_, ...), custom_call_target="tpu_custom_call" | custom-call | tf_op jit(solution)/shard_map/smooth/pallas_call | solution.py:361
  67.4 22.6 %all_to_all.5.got = f32[16,2,24,128]{3,2,1,0:T(8,128)S(1)} all-to-all(f32[16,2,24,128]{3,2,1,0:T(8,128)S(1)} %bitcast.8), channel_id=1, replica_groups=mesh['pairs'=4,'z'=4,'x'=2] {'pairs','z'}, dimensions={0} | all-to-all | bytes 786432 | tf_op jit(solution)/shard_map/all_to_all | solution.py:560
  90.0 1.1 %series.1 = (f32[2,8,8,256]{3,2,1,0:T(8,128)}, f32[2,8,8,256]{3,2,1,0:T(8,128)}) custom-call(f32[16,2,24,128]{3,2,1,0:T(8,128)S(1)} %all_to_all.5.got, f32[256,256]{1,0:T(8,128)S(1)} %invert.1.inverse), custom_call_target="tpu_custom_call" | custom-call | tf_op jit(solution)/shard_map/series/pallas_call | solution.py:452
  (10 shorter events, 0.1 us)
Async XLA Ops:
  1.3 12.6 %copy-start.5 = (s32[1000,2]{0,1:T(2,128)S(1)}, s32[1000,2]{0,1:T(2,128)}, u32[]{:S(2)}) copy-start(s32[1000,2]{0,1:T(2,128)} %param.7) | copy-start | bytes 24004
  5.3 13.9 %collective-permute-start = (bf16[2,2,4,1,128,128]{5,4,3,2,1,0:T(8,128)(2,1)}, bf16[2,2,4,1,128,128]{5,4,3,2,1,0:T(8,128)(2,1)S(1)}, u32[]{:S(2)}, u32[]{:S(2)}) collective-permute-start(bf16[2,2,4,1,128,128]{5,4,3,2,1,0:T(8,128)(2,1)} %get-tuple-element.24), channel_id=1, source_target_pairs={{0,1},{1,0},{2,3},{3,2},{4,5},{5,4},{6,7},{7,6},{8,9},{9,8},{10,11... | collective-permute-start | bytes 1572872 | tf_op jit(solution)/shard_map/ppermute | solution.py:533
  12.4 19.7 %collective-permute-start.1 = (bf16[3,2,2,1,128,128]{5,4,3,2,1,0:T(8,128)(2,1)}, bf16[3,2,2,1,128,128]{5,4,3,2,1,0:T(8,128)(2,1)S(1)}, u32[]{:S(2)}, u32[]{:S(2)}) collective-permute-start(bf16[3,2,2,1,128,128]{5,4,3,2,1,0:T(8,128)(2,1)} %get-tuple-element.26), channel_id=1, source_target_pairs={{0,1},{1,0},{2,3},{3,2},{4,5},{5,4},{6,7},{7,6},{8,9},{9,8},{10,11... | collective-permute-start | bytes 1179656 | tf_op jit(solution)/shard_map/ppermute | solution.py:533
  12.4 24.3 %collective-permute-start.6 = (bf16[3,2,2,1,128,128]{5,4,3,2,1,0:T(8,128)(2,1)}, bf16[3,2,2,1,128,128]{5,4,3,2,1,0:T(8,128)(2,1)S(1)}, u32[]{:S(2)}, u32[]{:S(2)}) collective-permute-start(bf16[3,2,2,1,128,128]{5,4,3,2,1,0:T(8,128)(2,1)} %get-tuple-element.35), channel_id=1, source_target_pairs={{0,1},{1,0},{2,3},{3,2},{4,5},{5,4},{6,7},{7,6},{8,9},{9,8},{10,11... | collective-permute-start | bytes 1179656 | tf_op jit(solution)/shard_map/ppermute | solution.py:533
  14.4 4.8 %copy-start.1 = (bf16[2,2,4,1,128,128]{5,4,3,2,1,0:T(8,128)(2,1)S(1)}, bf16[2,2,4,1,128,128]{5,4,3,2,1,0:T(8,128)(2,1)}, u32[]{:S(2)}) copy-start(bf16[2,2,4,1,128,128]{5,4,3,2,1,0:T(8,128)(2,1)} %get-tuple-element.23.rest_0_.refs_0_) | copy-start | bytes 1572868
  17.7 14.4 %copy-start = (bf16[3,2,4,1,128,128]{5,4,3,2,1,0:T(8,128)(2,1)S(1)}, bf16[3,2,4,1,128,128]{5,4,3,2,1,0:T(8,128)(2,1)}, u32[]{:S(2)}) copy-start(bf16[3,2,4,1,128,128]{5,4,3,2,1,0:T(8,128)(2,1)} %get-tuple-element.25.rest_0_.refs_2_) | copy-start | bytes 2359300
  19.3 7.7 %copy-start.4 = (bf16[2,2,4,1,128,128]{5,4,3,2,1,0:T(8,128)(2,1)}, bf16[2,2,4,1,128,128]{5,4,3,2,1,0:T(8,128)(2,1)S(1)}, u32[]{:S(2)}) copy-start(bf16[2,2,4,1,128,128]{5,4,3,2,1,0:T(8,128)(2,1)S(1)} %broadcast_select_fusion.rest_1_) | copy-start | bytes 1572868
  19.3 27.4 %copy-start.3 = (s32[3]{0:T(128)S(1)}, s32[3]{0:T(128)}, u32[]{:S(2)}) copy-start(s32[3]{0:T(128)} %pad_add_fusion.info) | copy-start | bytes 40
  19.3 27.4 %collective-permute-start.3 = (bf16[2,2,4,1,128,128]{5,4,3,2,1,0:T(8,128)(2,1)S(1)}, bf16[2,2,4,1,128,128]{5,4,3,2,1,0:T(8,128)(2,1)S(1)}, u32[]{:S(2)}, u32[]{:S(2)}) collective-permute-start(bf16[2,2,4,1,128,128]{5,4,3,2,1,0:T(8,128)(2,1)S(1)} %broadcast_select_fusion.rest_1_), channel_id=1, source_target_pairs={{2,0},{4,2},{6,4},{8,6},{10,8},{12,10},{14,12},{16,14},{18,16},{20... | collective-permute-start | bytes 1572872 | tf_op jit(solution)/shard_map/ppermute | solution.py:522
  32.1 13.2 %collective-permute-start.4 = (bf16[3,2,2,1,128,128]{5,4,3,2,1,0:T(8,128)(2,1)S(1)}, bf16[3,2,2,1,128,128]{5,4,3,2,1,0:T(8,128)(2,1)S(1)}, u32[]{:S(2)}, u32[]{:S(2)}) collective-permute-start(bf16[3,2,2,1,128,128]{5,4,3,2,1,0:T(8,128)(2,1)S(1)} %slice_select_fusion.1), channel_id=1, source_target_pairs={{2,0},{4,2},{6,4},{8,6},{10,8},{12,10},{14,12},{16,14},{18,16},{20... | collective-permute-start | bytes 1179656 | tf_op jit(solution)/shard_map/ppermute | solution.py:522
  35.4 9.7 %collective-permute-start.5 = (bf16[3,2,1,1,128,128]{5,4,3,2,1,0:T(8,128)(2,1)}, bf16[3,2,1,1,128,128]{5,4,3,2,1,0:T(8,128)(2,1)S(1)}, u32[]{:S(2)}, u32[]{:S(2)}) collective-permute-start(bf16[3,2,1,1,128,128]{5,4,3,2,1,0:T(8,128)(2,1)} %get-tuple-element.34), channel_id=1, source_target_pairs={{0,1},{1,0},{2,3},{3,2},{4,5},{5,4},{6,7},{7,6},{8,9},{9,8},{10,11... | collective-permute-start | bytes 589832 | tf_op jit(solution)/shard_map/ppermute | solution.py:533
  36.7 18.6 %collective-permute-start.8 = (bf16[3,2,2,1,128,128]{5,4,3,2,1,0:T(8,128)(2,1)S(1)}, bf16[3,2,2,1,128,128]{5,4,3,2,1,0:T(8,128)(2,1)S(1)}, u32[]{:S(2)}, u32[]{:S(2)}) collective-permute-start(bf16[3,2,2,1,128,128]{5,4,3,2,1,0:T(8,128)(2,1)S(1)} %slice_select_fusion), channel_id=1, source_target_pairs={{2,0},{4,2},{6,4},{8,6},{10,8},{12,10},{14,12},{16,14},{18,16},{20... | collective-permute-start | bytes 1179656 | tf_op jit(solution)/shard_map/ppermute | solution.py:522
  43.8 7.3 %collective-permute-start.2 = (bf16[3,2,1,1,128,128]{5,4,3,2,1,0:T(8,128)(2,1)}, bf16[3,2,1,1,128,128]{5,4,3,2,1,0:T(8,128)(2,1)S(1)}, u32[]{:S(2)}, u32[]{:S(2)}) collective-permute-start(bf16[3,2,1,1,128,128]{5,4,3,2,1,0:T(8,128)(2,1)} %get-tuple-element.29), channel_id=1, source_target_pairs={{0,1},{1,0},{2,3},{3,2},{4,5},{5,4},{6,7},{7,6},{8,9},{9,8},{10,11... | collective-permute-start | bytes 589832 | tf_op jit(solution)/shard_map/ppermute | solution.py:533
  45.1 10.2 %collective-permute-start.7 = (bf16[3,2,1,1,128,128]{5,4,3,2,1,0:T(8,128)(2,1)}, bf16[3,2,1,1,128,128]{5,4,3,2,1,0:T(8,128)(2,1)S(1)}, u32[]{:S(2)}, u32[]{:S(2)}) collective-permute-start(bf16[3,2,1,1,128,128]{5,4,3,2,1,0:T(8,128)(2,1)} %get-tuple-element.36), channel_id=1, source_target_pairs={{0,1},{1,0},{2,3},{3,2},{4,5},{5,4},{6,7},{7,6},{8,9},{9,8},{10,11... | collective-permute-start | bytes 589832 | tf_op jit(solution)/shard_map/ppermute | solution.py:533
  45.4 13.9 %collective-permute-start.9 = (bf16[3,2,1,1,128,128]{5,4,3,2,1,0:T(8,128)(2,1)}, bf16[3,2,1,1,128,128]{5,4,3,2,1,0:T(8,128)(2,1)S(1)}, u32[]{:S(2)}, u32[]{:S(2)}) collective-permute-start(bf16[3,2,1,1,128,128]{5,4,3,2,1,0:T(8,128)(2,1)} %get-tuple-element.40), channel_id=1, source_target_pairs={{0,1},{1,0},{2,3},{3,2},{4,5},{5,4},{6,7},{7,6},{8,9},{9,8},{10,11... | collective-permute-start | bytes 589832 | tf_op jit(solution)/shard_map/ppermute | solution.py:533
  46.7 1.1 %copy-start.2 = (bf16[3,2,4,1,128,128]{5,4,3,2,1,0:T(8,128)(2,1)S(1)}, bf16[3,2,4,1,128,128]{5,4,3,2,1,0:T(8,128)(2,1)}, u32[]{:S(2)}) copy-start(bf16[3,2,4,1,128,128]{5,4,3,2,1,0:T(8,128)(2,1)} %get-tuple-element.28.refs_4_) | copy-start | bytes 2359300
  54.4 11.2 %collective-permute-start.10 = (f32[2,4,24,128]{3,2,1,0:T(8,128)S(1)}, f32[2,4,24,128]{3,2,1,0:T(8,128)S(1)}, u32[]{:S(2)}, u32[]{:S(2)}) collective-permute-start(f32[2,4,24,128]{3,2,1,0:T(8,128)S(1)} %shard_map.63.refs_8_.rest_0_), channel_id=1, source_target_pairs={{0,1},{1,0},{2,3},{3,2},{4,5},{5,4},{6,7},{7,6},{8,9},{9,8},{10,11... | collective-permute-start | bytes 294920 | tf_op jit(solution)/shard_map/ppermute | solution.py:548
  58.6 4.9 %collective-permute-start.11 = (f32[1,4,24,128]{3,2,1,0:T(8,128)S(1)}, f32[1,4,24,128]{3,2,1,0:T(8,128)S(1)}, u32[]{:S(2)}, u32[]{:S(2)}) collective-permute-start(f32[1,4,24,128]{3,2,1,0:T(8,128)S(1)} %shard_map.64.refs_8_.rest_1_), channel_id=1, source_target_pairs={{0,1},{1,0},{2,3},{3,2},{4,5},{5,4},{6,7},{7,6},{8,9},{9,8},{10,11... | collective-permute-start | bytes 147464 | tf_op jit(solution)/shard_map/ppermute | solution.py:548
  62.6 3.0 %collective-permute-start.12 = (f32[1,4,24,128]{3,2,1,0:T(8,128)S(1)}, f32[1,4,24,128]{3,2,1,0:T(8,128)S(1)}, u32[]{:S(2)}, u32[]{:S(2)}) collective-permute-start(f32[1,4,24,128]{3,2,1,0:T(8,128)S(1)} %shard_map.65.rest_2_), channel_id=1, source_target_pairs={{0,1},{1,0},{2,3},{3,2},{4,5},{5,4},{6,7},{7,6},{8,9},{9,8},{10,11... | collective-permute-start | bytes 147464 | tf_op jit(solution)/shard_map/ppermute | solution.py:548

commit v3 on v2

--- a/solution.py
+++ b/solution.py
@@ -493,11 +493,13 @@
     inverse = invert(normal)
 
     swap = [(0, 1), (1, 0)]
-    cuts = [0, own] if own <= MAXB else [0, 2, MAXB, own]
+    cuts, parts = [0, own], [1]
+    if own > MAXB:
+        cuts, parts = [0, 1, 2, MAXB, own], [1, 1, min(rows, 2), rows]
     pieces, following = [], []
-    left, turn, leaving = x == 0, 0, None
-
-    def send_back(start, keep, received, left, inverse):
+    left, turn = x == 0, 0
+
+    def send_back(start, keep, received, left):
         hops = []
         for c, other in enumerate(received):
             part = other.shape[2]
@@ -508,7 +510,7 @@
                 upper = jnp.concatenate([other, mine], 0)[:MAXB]
             hops.append(jnp.where(left, lower, upper))
             if own > MAXB:
-                left, hops[-1], inverse = lax.optimization_barrier((left, hops[-1], inverse))
+                left, hops[-1] = lax.optimization_barrier((left, hops[-1]))
         if own < MAXB:
             for hop in range(1, -(-MAXB // block) + 1):
                 route = [(i + hop, i) for i in range(blocks - hop)]
@@ -521,24 +523,19 @@
             for v in hops:
                 going.append(lax.ppermute(v, ("pairs", "z"), route))
             following.append((start, going))
-        return hops[0], left, inverse
-
-    for k, (start, end) in enumerate(zip(cuts, cuts[1:])):
-        after = [p[1] for p in pieces[-1:]] + [v for v in (leaving,) if v is not None]
-        keep, *sends = resample(
-            images, az, rg, info, start, end - start, min(rows, 2**k), after
-        )
+        return left
+
+    for start, end, count in zip(cuts, cuts[1:], parts):
+        after = [p[1] for p in pieces[-1:]]
+        keep, *sends = resample(images, az, rg, info, start, end - start, count, after)
         received = []
         for v in sends:
             received.append(lax.ppermute(v, "x", swap))
             turn += 1
         pieces.append((start, keep, received))
-        if k > 0:
-            if k == len(cuts) - 2:
-                left, _ = lax.optimization_barrier((left, keep))
-            leaving, left, inverse = send_back(*pieces[k - 1], left, inverse)
-    if cuts[-2] < MAXB:
-        send_back(*pieces[-1], left, inverse)
+    for start, keep, received in pieces:
+        if start < MAXB:
+            left = send_back(start, keep, received, left)
 
     sums = []
     for c in range(rows):

time: 92.3 us -> 95 us (1.029)
  blocking collectives: 22.6 us -> 0 us
  waiting for transfers between devices: 3.31 us -> 14.5 us
  starting transfers between devices: 28.1 us -> 39.1 us
  Pallas kernels: 33.5 us -> 37.6 us
  local copies, waits for them, and re-layouts: 1.15 us -> 0.03 us
    all_to_all x1 -> x0, blocking collectives: 22.6 us -> none  [local(): lax.all_to_all(outgoing, ('pairs', 'z'), split_axis=0, concat_axis=0, til...]
    all_to_all x0 -> x1, starting transfers between devices: none -> 10.1 us  [local(): lax.all_to_all(outgoing, ('pairs', 'z'), split_axis=0, concat_axis=0, til...]
    all_to_all x0 -> x1, waiting for transfers between devices: none -> 8.37 us  [local(): lax.all_to_all(outgoing, ('pairs', 'z'), split_axis=0, concat_axis=0, til...]
    ppermute x7 -> x8, waiting for transfers between devices: 1.24 us -> 4.07 us  [local(): received.append(lax.ppermute(v, 'x', swap))]
    pallas_call x3 -> x4, Pallas kernels: 14.2 us -> 16.6 us  [resample(): pl.pallas_call(partial(resample_kernel, first, parts), grid_spec=pltpu.Pr...]
    unnamed x12, local copies, waits for them, and re-layouts: 1.15 us -> 0.02 us
    ppermute x3 -> x4, starting transfers between devices: 18 us -> 18.5 us  [send_back(): going.append(lax.ppermute(v, ('pairs', 'z'), route))]
    ppermute x7 -> x8, starting transfers between devices: 7.54 us -> 7.72 us  [local(): received.append(lax.ppermute(v, 'x', swap))]
  transfers between devices with their start and end apart: 13 -> 16, of which waited for: 2 -> 4; matrix products, arithmetic and copies ran while one was open for 1% -> 1% of each run, Pallas kernels for 29% -> 33%
where the time goes in v3:
time: 95 us; the launch traced here: 93.7 us
  starting transfers between devices  39.1 us (41%)
  Pallas kernels  37.6 us (40%)
  waiting for transfers between devices  14.5 us (15%)
    ppermute x4, starting transfers between devices, send_back(): going.append(lax.ppermute(v, ('pairs', 'z'), route))  18.5 us
    pallas_call x4, Pallas kernels, resample(): pl.pallas_call(partial(resample_kernel, first, parts), grid_spec=pltpu.Pr...  16.6 us
    pallas_call x4, Pallas kernels, pair_sums(): pl.pallas_call(partial(pair_kernel, own, [p[0] for p in pieces], [f[0] fo...  14 us
    all_to_all x1, starting transfers between devices, local(): lax.all_to_all(outgoing, ('pairs', 'z'), split_axis=0, concat_axis=0, til...  10.1 us
    all_to_all x1, waiting for transfers between devices, local(): lax.all_to_all(outgoing, ('pairs', 'z'), split_axis=0, concat_axis=0, til...  8.37 us
    ppermute x8, starting transfers between devices, local(): received.append(lax.ppermute(v, 'x', swap))  7.72 us
    ppermute x8, waiting for transfers between devices, local(): received.append(lax.ppermute(v, 'x', swap))  4.07 us
    pallas_call x1, Pallas kernels, invert(): pl.pallas_call(invert_kernel, in_specs=[vmem()], out_specs=vmem(), out_sh...  3.27 us
  transfers between devices with their start and end apart: 16, of which 4 were waited for; matrix products, arithmetic and copies ran while one was open for 1% of the time, Pallas kernels for 33%

profile of v3, /device:TPU:1, one launch (start us, length us, event | category | flops | bytes accessed | tf_op | source)
XLA Modules:
  0.0 93.7 jit_solution(1561407094500080789)
XLA Ops:
  0.6 0.6 pad_add_fusion.info
  1.2 3.2 %shard_map.59 = (bf16[1,2,4,1,128,128]{5,4,3,2,1,0:T(8,128)(2,1)}, bf16[1,2,4,1,128,128]{5,4,3,2,1,0:T(8,128)(2,1)}) custom-call(s32[3]{0:T(128)} %pad_add_fusion.info, s32[256]{0:T(256)} %az.7, s32[256]{0:T(256)} %rg.7, bf16[8,2,128,1024]{3,2,1,0:T(8,128)(2,1)} %img.7), custom_call_target="tpu_custom_call" | custom-call | flops 524288 | bytes 1048576 | tf_op jit(solution)/shard_map/pallas_call | solution.py:147
  4.4 2.0 %collective-permute-start = (bf16[1,2,4,1,128,128]{5,4,3,2,1,0:T(8,128)(2,1)}, bf16[1,2,4,1,128,128]{5,4,3,2,1,0:T(8,128)(2,1)S(1)}, u32[]{:S(2)}, u32[]{:S(2)}) collective-permute-start(bf16[1,2,4,1,128,128]{5,4,3,2,1,0:T(8,128)(2,1)} %get-tuple-element.24), channel_id=1, source_target_pairs={{0,1},{1,0},{2,3},{3,2},{4,5},{5,4},{6,7},{7,6},{8,9},{9,8},{10,11... | collective-permute-start | bytes 786440 | tf_op jit(solution)/shard_map/ppermute | solution.py:533
  6.4 3.2 %shard_map.60 = (bf16[1,2,4,1,128,128]{5,4,3,2,1,0:T(8,128)(2,1)}, bf16[1,2,4,1,128,128]{5,4,3,2,1,0:T(8,128)(2,1)}) custom-call(s32[3]{0:T(128)} %pad_add_fusion.info, s32[256]{0:T(256)} %az.7, s32[256]{0:T(256)} %rg.7, bf16[8,2,128,1024]{3,2,1,0:T(8,128)(2,1)} %img.7, bf16[1,2,4,1,128,128]{5,4,3,2,1,0:T(8,128)(2,1)} %get-tuple-element.23.rest_0_.refs_0_), custom_call_target="tpu_custom_call" | custom-call | flops 524288 | bytes 1048576 | tf_op jit(solution)/shard_map/pallas_call | solution.py:147
  9.6 0.0 collective-permute-start.1
  9.6 0.0 copy-start.5
  9.6 0.0 copy-start.2
  9.6 0.0 copy-start.3
  9.6 5.1 %shard_map.61 = (bf16[3,2,4,1,128,128]{5,4,3,2,1,0:T(8,128)(2,1)}, bf16[3,2,2,1,128,128]{5,4,3,2,1,0:T(8,128)(2,1)}, bf16[3,2,2,1,128,128]{5,4,3,2,1,0:T(8,128)(2,1)}) custom-call(s32[3]{0:T(128)} %pad_add_fusion.info, s32[256]{0:T(256)} %az.7, s32[256]{0:T(256)} %rg.7, bf16[8,2,128,1024]{3,2,1,0:T(8,128)(2,1)} %img.7, ...), custom_call_target="tpu_custom_call" | custom-call | flops 1572864 | bytes 3145728 | tf_op jit(solution)/shard_map/pallas_call | solution.py:147
  14.7 0.0 copy-start
  14.7 1.4 %collective-permute-start.2 = (bf16[3,2,2,1,128,128]{5,4,3,2,1,0:T(8,128)(2,1)}, bf16[3,2,2,1,128,128]{5,4,3,2,1,0:T(8,128)(2,1)S(1)}, u32[]{:S(2)}, u32[]{:S(2)}) collective-permute-start(bf16[3,2,2,1,128,128]{5,4,3,2,1,0:T(8,128)(2,1)} %get-tuple-element.28), channel_id=1, source_target_pairs={{0,1},{1,0},{2,3},{3,2},{4,5},{5,4},{6,7},{7,6},{8,9},{9,8},{10,11... | collective-permute-start | bytes 1179656 | tf_op jit(solution)/shard_map/ppermute | solution.py:533
  16.2 0.0 copy-start.4
  16.2 5.1 %shard_map.62 = (bf16[3,2,4,1,128,128]{5,4,3,2,1,0:T(8,128)(2,1)}, bf16[3,2,1,1,128,128]{5,4,3,2,1,0:T(8,128)(2,1)}, bf16[3,2,1,1,128,128]{5,4,3,2,1,0:T(8,128)(...) custom-call(s32[3]{0:T(128)} %pad_add_fusion.info, s32[256]{0:T(256)} %az.7, s32[256]{0:T(256)} %rg.7, ...), custom_call_target="tpu_custom_call" | custom-call | flops 1572864 | bytes 3145728 | tf_op jit(solution)/shard_map/pallas_call | solution.py:147
  21.3 0.0 copy-start.1
  21.3 0.1 collective-permute-start.7
  21.3 1.4 %collective-permute-start.8 = (bf16[3,2,2,1,128,128]{5,4,3,2,1,0:T(8,128)(2,1)}, bf16[3,2,2,1,128,128]{5,4,3,2,1,0:T(8,128)(2,1)S(1)}, u32[]{:S(2)}, u32[]{:S(2)}) collective-permute-start(bf16[3,2,2,1,128,128]{5,4,3,2,1,0:T(8,128)(2,1)} %get-tuple-element.37), channel_id=1, source_target_pairs={{0,1},{1,0},{2,3},{3,2},{4,5},{5,4},{6,7},{7,6},{8,9},{9,8},{10,11... | collective-permute-start | bytes 1179656 | tf_op jit(solution)/shard_map/ppermute | solution.py:533
  22.8 0.0 copy-done.5
  22.8 0.3 convolution_convert_fusion.mask
  23.1 0.0 collective-permute-done.refs_1_
  23.1 0.0 copy-done.2
  23.2 7.2 %collective-permute-start.4 = (bf16[1,2,4,1,128,128]{5,4,3,2,1,0:T(8,128)(2,1)S(1)}, bf16[1,2,4,1,128,128]{5,4,3,2,1,0:T(8,128)(2,1)S(1)}, u32[]{:S(2)}, u32[]{:S(2)}) collective-permute-start(bf16[1,2,4,1,128,128]{5,4,3,2,1,0:T(8,128)(2,1)S(1)} %broadcast_select_fusion.1), channel_id=1, source_target_pairs={{2,0},{4,2},{6,4},{8,6},{10,8},{12,10},{14,12},{16,14},{18,16},{20... | collective-permute-start | bytes 786440 | tf_op jit(solution)/shard_map/ppermute | solution.py:524
  30.4 0.0 collective-permute-done.1.refs_3_
  30.4 0.0 copy-done.3
  30.4 2.4 %collective-permute-start.5 = (bf16[1,2,4,1,128,128]{5,4,3,2,1,0:T(8,128)(2,1)S(1)}, bf16[1,2,4,1,128,128]{5,4,3,2,1,0:T(8,128)(2,1)S(1)}, u32[]{:S(2)}, u32[]{:S(2)}) collective-permute-start(bf16[1,2,4,1,128,128]{5,4,3,2,1,0:T(8,128)(2,1)S(1)} %broadcast_select_fusion), channel_id=1, source_target_pairs={{2,0},{4,2},{6,4},{8,6},{10,8},{12,10},{14,12},{16,14},{18,16},{20... | collective-permute-start | bytes 786440 | tf_op jit(solution)/shard_map/ppermute | solution.py:524
  32.8 0.0 collective-permute-done.2.refs_5_
  32.8 0.0 copy-done
  32.9 2.4 %collective-permute-start.6 = (bf16[3,2,2,1,128,128]{5,4,3,2,1,0:T(8,128)(2,1)S(1)}, bf16[3,2,2,1,128,128]{5,4,3,2,1,0:T(8,128)(2,1)S(1)}, u32[]{:S(2)}, u32[]{:S(2)}) collective-permute-start(bf16[3,2,2,1,128,128]{5,4,3,2,1,0:T(8,128)(2,1)S(1)} %slice_select_fusion.1), channel_id=1, source_target_pairs={{2,0},{4,2},{6,4},{8,6},{10,8},{12,10},{14,12},{16,14},{18,16},{20... | collective-permute-start | bytes 1179656 | tf_op jit(solution)/shard_map/ppermute | solution.py:524
  35.2 4.1 %collective-permute-done.8.refs_5_ = bf16[3,2,2,1,128,128]{5,4,3,2,1,0:T(8,128)(2,1)S(1)} collective-permute-done((bf16[3,2,2,1,128,128]{5,4,3,2,1,0:T(8,128)(2,1)}, bf16[3,2,2,1,128,128]{5,4,3,2,1,0:T(8,128)(2,1)S(1)}, u32[]{:S(2)}, u32[]{:S(2)}) %collective-permute-start.8) | collective-permute-done | bytes 393248 | tf_op jit(solution)/shard_map/ppermute | solution.py:533
  39.3 6.6 %collective-permute-start.10 = (bf16[3,2,2,1,128,128]{5,4,3,2,1,0:T(8,128)(2,1)S(1)}, bf16[3,2,2,1,128,128]{5,4,3,2,1,0:T(8,128)(2,1)S(1)}, u32[]{:S(2)}, u32[]{:S(2)}) collective-permute-start(bf16[3,2,2,1,128,128]{5,4,3,2,1,0:T(8,128)(2,1)S(1)} %slice_select_fusion), channel_id=1, source_target_pairs={{2,0},{4,2},{6,4},{8,6},{10,8},{12,10},{14,12},{16,14},{18,16},{20... | collective-permute-start | bytes 1179656 | tf_op jit(solution)/shard_map/ppermute | solution.py:524
  46.0 0.0 collective-permute-done.7.refs_7_
  46.0 1.3 %collective-permute-start.3 = (bf16[3,2,1,1,128,128]{5,4,3,2,1,0:T(8,128)(2,1)}, bf16[3,2,1,1,128,128]{5,4,3,2,1,0:T(8,128)(2,1)S(1)}, u32[]{:S(2)}, u32[]{:S(2)}) collective-permute-start(bf16[3,2,1,1,128,128]{5,4,3,2,1,0:T(8,128)(2,1)} %get-tuple-element.30), channel_id=1, source_target_pairs={{0,1},{1,0},{2,3},{3,2},{4,5},{5,4},{6,7},{7,6},{8,9},{9,8},{10,11... | collective-permute-start | bytes 589832 | tf_op jit(solution)/shard_map/ppermute | solution.py:533
  47.3 0.0 collective-permute-done.4.refs_8_
  47.3 0.3 collective-permute-start.9
  47.5 0.0 collective-permute-done.5.refs_9_
  47.5 1.2 %collective-permute-start.11 = (bf16[3,2,1,1,128,128]{5,4,3,2,1,0:T(8,128)(2,1)}, bf16[3,2,1,1,128,128]{5,4,3,2,1,0:T(8,128)(2,1)S(1)}, u32[]{:S(2)}, u32[]{:S(2)}) collective-permute-start(bf16[3,2,1,1,128,128]{5,4,3,2,1,0:T(8,128)(2,1)} %get-tuple-element.41), channel_id=1, source_target_pairs={{0,1},{1,0},{2,3},{3,2},{4,5},{5,4},{6,7},{7,6},{8,9},{9,8},{10,11... | collective-permute-start | bytes 589832 | tf_op jit(solution)/shard_map/ppermute | solution.py:533
  48.7 0.1 select_add_fusion
  48.8 0.2 collective-permute-done.6.refs_10_
  49.1 0.0 copy-done.4
  49.1 0.0 copy-done.1
  49.1 4.2 %shard_map.63.refs_11_ = f32[1,4,24,128]{3,2,1,0:T(8,128)S(1)} custom-call(s32[3]{0:T(128)S(1)} %copy-done.4, s32[5,256]{1,0:T(8,128)S(1)} %convolution_convert_fusion.mask, bf16[1,2,4,1,128,128]{5,4,3,2,1,0:T(8,128)(2,1)S(1)} %copy-done.2, bf16[1,2,4,1,128,128]{5,4,3,2,1,0:T(8,128)(2,1)S(1)} %collective-permute-done.refs_1_, ...), custom_call_target="tpu_custom_call" | custom-call | flops 10485760 | bytes 1310720 | tf_op jit(solution)/shard_map/pallas_call | solution.py:290
  53.3 0.0 collective-permute-done.3.refs_7_
  53.3 3.3 %shard_map.64.refs_11_.rest_0_ = f32[2,4,24,128]{3,2,1,0:T(8,128)S(1)} custom-call(s32[3]{0:T(128)S(1)} %copy-done.4, s32[5,256]{1,0:T(8,128)S(1)} %convolution_convert_fusion.mask, bf16[1,2,4,1,128,128]{5,4,3,2,1,0:T(8,128)(2,1)S(1)} %copy-done.2, bf16[1,2,4,1,128,128]{5,4,3,2,1,0:T(8,128)(2,1)S(1)} %collective-permute-done.refs_1_, ...), custom_call_target="tpu_custom_call" | custom-call | flops 10485760 | bytes 1310720 | tf_op jit(solution)/shard_map/pallas_call | solution.py:290
  56.6 1.2 %collective-permute-start.12 = (f32[2,4,24,128]{3,2,1,0:T(8,128)S(1)}, f32[2,4,24,128]{3,2,1,0:T(8,128)S(1)}, u32[]{:S(2)}, u32[]{:S(2)}) collective-permute-start(f32[2,4,24,128]{3,2,1,0:T(8,128)S(1)} %shard_map.64.refs_11_.rest_0_), channel_id=1, source_target_pairs={{0,1},{1,0},{2,3},{3,2},{4,5},{5,4},{6,7},{7,6},{8,9},{9,8},{10,11... | collective-permute-start | bytes 294920 | tf_op jit(solution)/shard_map/ppermute | solution.py:545
  57.7 0.0 collective-permute-done.9.refs_7_
  57.8 0.0 collective-permute-done.10.refs_10_
  57.8 3.3 %shard_map.65.refs_11_.rest_1_ = f32[1,4,24,128]{3,2,1,0:T(8,128)S(1)} custom-call(s32[3]{0:T(128)S(1)} %copy-done.4, s32[5,256]{1,0:T(8,128)S(1)} %convolution_convert_fusion.mask, bf16[1,2,4,1,128,128]{5,4,3,2,1,0:T(8,128)(2,1)S(1)} %copy-done.2, bf16[1,2,4,1,128,128]{5,4,3,2,1,0:T(8,128)(2,1)S(1)} %collective-permute-done.refs_1_, ...), custom_call_target="tpu_custom_call" | custom-call | flops 10485760 | bytes 1310720 | tf_op jit(solution)/shard_map/pallas_call | solution.py:290
  61.0 0.4 collective-permute-start.13
  61.5 0.0 collective-permute-done.11.refs_7_
  61.5 3.3 %shard_map.66.rest_2_ = f32[1,4,24,128]{3,2,1,0:T(8,128)S(1)} custom-call(s32[3]{0:T(128)S(1)} %copy-done.4, s32[5,256]{1,0:T(8,128)S(1)} %convolution_convert_fusion.mask, bf16[1,2,4,1,128,128]{5,4,3,2,1,0:T(8,128)(2,1)S(1)} %copy-done.2, bf16[1,2,4,1,128,128]{5,4,3,2,1,0:T(8,128)(2,1)S(1)} %collective-permute-done.refs_1_, ...), custom_call_target="tpu_custom_call" | custom-call | flops 10485760 | bytes 1310720 | tf_op jit(solution)/shard_map/pallas_call | solution.py:290
  64.7 1.2 %collective-permute-start.14 = (f32[1,4,24,128]{3,2,1,0:T(8,128)S(1)}, f32[1,4,24,128]{3,2,1,0:T(8,128)S(1)}, u32[]{:S(2)}, u32[]{:S(2)}) collective-permute-start(f32[1,4,24,128]{3,2,1,0:T(8,128)S(1)} %shard_map.66.rest_2_), channel_id=1, source_target_pairs={{0,1},{1,0},{2,3},{3,2},{4,5},{5,4},{6,7},{7,6},{8,9},{9,8},{10,11... | collective-permute-start | bytes 147464 | tf_op jit(solution)/shard_map/ppermute | solution.py:545
  65.9 0.0 collective-permute-done.13.rest_4_
  65.9 1.8 %collective-permute-done.14.rest_5_ = f32[1,4,24,128]{3,2,1,0:T(8,128)S(1)} collective-permute-done((f32[1,4,24,128]{3,2,1,0:T(8,128)S(1)}, f32[1,4,24,128]{3,2,1,0:T(8,128)S(1)}, u32[]{:S(2)}, u32[]{:S(2)}) %collective-permute-start.14) | collective-permute-done | bytes 49184 | tf_op jit(solution)/shard_map/ppermute | solution.py:545
  67.8 0.0 collective-permute-done.12.rest_3_
  67.8 2.6 %smooth.1 = f32[4,4,2,24,128]{4,3,2,1,0:T(8,128)} custom-call(s32[3]{0:T(128)S(1)} %copy-done.4, f32[2,4,24,128]{3,2,1,0:T(8,128)S(1)} %shard_map.64.refs_11_.rest_0_, f32[1,4,24,128]{3,2,1,0:T(8,128)S(1)} %shard_map.65.refs_11_.rest_1_, f32[1,4,24,128]{3,2,1,0:T(8,128)S(1)} %shard_map.66.rest_2_, f32[2,4,24,128]{3,2,1,0:T(8,128)S(1)} %collective-permute-done.12.rest_3_, ...), custom_call_target="tpu_custom_call" | custom-call | tf_op jit(solution)/shard_map/smooth/pallas_call | solution.py:361
  70.3 10.1 %all-to-all-start = ((f32[16,2,24,128]{3,2,1,0:T(8,128)}), f32[16,2,24,128]{3,2,1,0:T(8,128)S(1)}, u32[]{:S(2)}, u32[]{:S(2)}) async-start(f32[16,2,24,128]{3,2,1,0:T(8,128)} %bitcast.5), calls=%async_computation | async-start | bytes 786432 | tf_op jit(solution)/shard_map/all_to_all | solution.py:557
  80.4 0.5 convolution_add_fusion.normal
  80.9 3.3 %invert.1.inverse = f32[256,256]{1,0:T(8,128)S(1)} custom-call(f32[256,256]{1,0:T(8,128)S(1)} %convolution_add_fusion.normal), custom_call_target="tpu_custom_call" | custom-call | flops 2013265920 | bytes 524288 | tf_op jit(solution)/shard_map/invert/pallas_call | solution.py:414
  84.2 8.4 %all-to-all-done.got = f32[16,2,24,128]{3,2,1,0:T(8,128)S(1)} async-done(((f32[16,2,24,128]{3,2,1,0:T(8,128)}), f32[16,2,24,128]{3,2,1,0:T(8,128)S(1)}, u32[]{:S(2)}, u32[]{:S(2)}) %all-to-all-start) | async-done | bytes 393248 | tf_op jit(solution)/shard_map/all_to_all | solution.py:557
  92.5 1.1 %series.1 = (f32[2,8,8,256]{3,2,1,0:T(8,128)}, f32[2,8,8,256]{3,2,1,0:T(8,128)}) custom-call(f32[16,2,24,128]{3,2,1,0:T(8,128)S(1)} %all-to-all-done.got, f32[256,256]{1,0:T(8,128)S(1)} %invert.1.inverse), custom_call_target="tpu_custom_call" | custom-call | tf_op jit(solution)/shard_map/series/pallas_call | solution.py:452
  (12 shorter events, 0.2 us)
Async XLA Ops:
  4.4 18.8 %collective-permute-start = (bf16[1,2,4,1,128,128]{5,4,3,2,1,0:T(8,128)(2,1)}, bf16[1,2,4,1,128,128]{5,4,3,2,1,0:T(8,128)(2,1)S(1)}, u32[]{:S(2)}, u32[]{:S(2)}) collective-permute-start(bf16[1,2,4,1,128,128]{5,4,3,2,1,0:T(8,128)(2,1)} %get-tuple-element.24), channel_id=1, source_target_pairs={{0,1},{1,0},{2,3},{3,2},{4,5},{5,4},{6,7},{7,6},{8,9},{9,8},{10,11... | collective-permute-start | bytes 786440 | tf_op jit(solution)/shard_map/ppermute | solution.py:533
  9.6 20.8 %collective-permute-start.1 = (bf16[1,2,4,1,128,128]{5,4,3,2,1,0:T(8,128)(2,1)}, bf16[1,2,4,1,128,128]{5,4,3,2,1,0:T(8,128)(2,1)S(1)}, u32[]{:S(2)}, u32[]{:S(2)}) collective-permute-start(bf16[1,2,4,1,128,128]{5,4,3,2,1,0:T(8,128)(2,1)} %get-tuple-element.26), channel_id=1, source_target_pairs={{0,1},{1,0},{2,3},{3,2},{4,5},{5,4},{6,7},{7,6},{8,9},{9,8},{10,11... | collective-permute-start | bytes 786440 | tf_op jit(solution)/shard_map/ppermute | solution.py:533
  9.6 13.2 %copy-start.5 = (s32[1000,2]{0,1:T(2,128)S(1)}, s32[1000,2]{0,1:T(2,128)}, u32[]{:S(2)}) copy-start(s32[1000,2]{0,1:T(2,128)} %param.7) | copy-start | bytes 24004
  9.6 13.6 %copy-start.2 = (bf16[1,2,4,1,128,128]{5,4,3,2,1,0:T(8,128)(2,1)S(1)}, bf16[1,2,4,1,128,128]{5,4,3,2,1,0:T(8,128)(2,1)}, u32[]{:S(2)}) copy-start(bf16[1,2,4,1,128,128]{5,4,3,2,1,0:T(8,128)(2,1)} %get-tuple-element.23.rest_0_.refs_0_) | copy-start | bytes 786436
  9.6 20.8 %copy-start.3 = (bf16[1,2,4,1,128,128]{5,4,3,2,1,0:T(8,128)(2,1)S(1)}, bf16[1,2,4,1,128,128]{5,4,3,2,1,0:T(8,128)(2,1)}, u32[]{:S(2)}) copy-start(bf16[1,2,4,1,128,128]{5,4,3,2,1,0:T(8,128)(2,1)} %get-tuple-element.25.rest_0_.refs_2_) | copy-start | bytes 786436
  14.7 18.1 %copy-start = (bf16[3,2,4,1,128,128]{5,4,3,2,1,0:T(8,128)(2,1)S(1)}, bf16[3,2,4,1,128,128]{5,4,3,2,1,0:T(8,128)(2,1)}, u32[]{:S(2)}) copy-start(bf16[3,2,4,1,128,128]{5,4,3,2,1,0:T(8,128)(2,1)} %get-tuple-element.27.rest_0_.refs_4_) | copy-start | bytes 2359300
  14.7 18.1 %collective-permute-start.2 = (bf16[3,2,2,1,128,128]{5,4,3,2,1,0:T(8,128)(2,1)}, bf16[3,2,2,1,128,128]{5,4,3,2,1,0:T(8,128)(2,1)S(1)}, u32[]{:S(2)}, u32[]{:S(2)}) collective-permute-start(bf16[3,2,2,1,128,128]{5,4,3,2,1,0:T(8,128)(2,1)} %get-tuple-element.28), channel_id=1, source_target_pairs={{0,1},{1,0},{2,3},{3,2},{4,5},{5,4},{6,7},{7,6},{8,9},{9,8},{10,11... | collective-permute-start | bytes 1179656 | tf_op jit(solution)/shard_map/ppermute | solution.py:533
  16.2 32.9 %copy-start.4 = (s32[3]{0:T(128)S(1)}, s32[3]{0:T(128)}, u32[]{:S(2)}) copy-start(s32[3]{0:T(128)} %pad_add_fusion.info) | copy-start | bytes 40
  21.3 27.8 %copy-start.1 = (bf16[3,2,4,1,128,128]{5,4,3,2,1,0:T(8,128)(2,1)S(1)}, bf16[3,2,4,1,128,128]{5,4,3,2,1,0:T(8,128)(2,1)}, u32[]{:S(2)}) copy-start(bf16[3,2,4,1,128,128]{5,4,3,2,1,0:T(8,128)(2,1)} %get-tuple-element.29.refs_6_) | copy-start | bytes 2359300
  21.3 24.7 %collective-permute-start.7 = (bf16[3,2,1,1,128,128]{5,4,3,2,1,0:T(8,128)(2,1)}, bf16[3,2,1,1,128,128]{5,4,3,2,1,0:T(8,128)(2,1)}, u32[]{:S(2)}, u32[]{:S(2)}) collective-permute-start(bf16[3,2,1,1,128,128]{5,4,3,2,1,0:T(8,128)(2,1)} %get-tuple-element.36), channel_id=1, source_target_pairs={{0,1},{1,0},{2,3},{3,2},{4,5},{5,4},{6,7},{7,6},{8,9},{9,8},{10,11... | collective-permute-start | bytes 589832 | tf_op jit(solution)/shard_map/ppermute | solution.py:533
  21.3 18.0 %collective-permute-start.8 = (bf16[3,2,2,1,128,128]{5,4,3,2,1,0:T(8,128)(2,1)}, bf16[3,2,2,1,128,128]{5,4,3,2,1,0:T(8,128)(2,1)S(1)}, u32[]{:S(2)}, u32[]{:S(2)}) collective-permute-start(bf16[3,2,2,1,128,128]{5,4,3,2,1,0:T(8,128)(2,1)} %get-tuple-element.37), channel_id=1, source_target_pairs={{0,1},{1,0},{2,3},{3,2},{4,5},{5,4},{6,7},{7,6},{8,9},{9,8},{10,11... | collective-permute-start | bytes 1179656 | tf_op jit(solution)/shard_map/ppermute | solution.py:533
  23.2 24.1 %collective-permute-start.4 = (bf16[1,2,4,1,128,128]{5,4,3,2,1,0:T(8,128)(2,1)S(1)}, bf16[1,2,4,1,128,128]{5,4,3,2,1,0:T(8,128)(2,1)S(1)}, u32[]{:S(2)}, u32[]{:S(2)}) collective-permute-start(bf16[1,2,4,1,128,128]{5,4,3,2,1,0:T(8,128)(2,1)S(1)} %broadcast_select_fusion.1), channel_id=1, source_target_pairs={{2,0},{4,2},{6,4},{8,6},{10,8},{12,10},{14,12},{16,14},{18,16},{20... | collective-permute-start | bytes 786440 | tf_op jit(solution)/shard_map/ppermute | solution.py:524
  30.4 17.1 %collective-permute-start.5 = (bf16[1,2,4,1,128,128]{5,4,3,2,1,0:T(8,128)(2,1)S(1)}, bf16[1,2,4,1,128,128]{5,4,3,2,1,0:T(8,128)(2,1)S(1)}, u32[]{:S(2)}, u32[]{:S(2)}) collective-permute-start(bf16[1,2,4,1,128,128]{5,4,3,2,1,0:T(8,128)(2,1)S(1)} %broadcast_select_fusion), channel_id=1, source_target_pairs={{2,0},{4,2},{6,4},{8,6},{10,8},{12,10},{14,12},{16,14},{18,16},{20... | collective-permute-start | bytes 786440 | tf_op jit(solution)/shard_map/ppermute | solution.py:524
  32.9 16.2 %collective-permute-start.6 = (bf16[3,2,2,1,128,128]{5,4,3,2,1,0:T(8,128)(2,1)S(1)}, bf16[3,2,2,1,128,128]{5,4,3,2,1,0:T(8,128)(2,1)S(1)}, u32[]{:S(2)}, u32[]{:S(2)}) collective-permute-start(bf16[3,2,2,1,128,128]{5,4,3,2,1,0:T(8,128)(2,1)S(1)} %slice_select_fusion.1), channel_id=1, source_target_pairs={{2,0},{4,2},{6,4},{8,6},{10,8},{12,10},{14,12},{16,14},{18,16},{20... | collective-permute-start | bytes 1179656 | tf_op jit(solution)/shard_map/ppermute | solution.py:524
  39.3 18.4 %collective-permute-start.10 = (bf16[3,2,2,1,128,128]{5,4,3,2,1,0:T(8,128)(2,1)S(1)}, bf16[3,2,2,1,128,128]{5,4,3,2,1,0:T(8,128)(2,1)S(1)}, u32[]{:S(2)}, u32[]{:S(2)}) collective-permute-start(bf16[3,2,2,1,128,128]{5,4,3,2,1,0:T(8,128)(2,1)S(1)} %slice_select_fusion), channel_id=1, source_target_pairs={{2,0},{4,2},{6,4},{8,6},{10,8},{12,10},{14,12},{16,14},{18,16},{20... | collective-permute-start | bytes 1179656 | tf_op jit(solution)/shard_map/ppermute | solution.py:524
  46.0 7.3 %collective-permute-start.3 = (bf16[3,2,1,1,128,128]{5,4,3,2,1,0:T(8,128)(2,1)}, bf16[3,2,1,1,128,128]{5,4,3,2,1,0:T(8,128)(2,1)S(1)}, u32[]{:S(2)}, u32[]{:S(2)}) collective-permute-start(bf16[3,2,1,1,128,128]{5,4,3,2,1,0:T(8,128)(2,1)} %get-tuple-element.30), channel_id=1, source_target_pairs={{0,1},{1,0},{2,3},{3,2},{4,5},{5,4},{6,7},{7,6},{8,9},{9,8},{10,11... | collective-permute-start | bytes 589832 | tf_op jit(solution)/shard_map/ppermute | solution.py:533
  47.3 10.5 %collective-permute-start.9 = (bf16[3,2,1,1,128,128]{5,4,3,2,1,0:T(8,128)(2,1)}, bf16[3,2,1,1,128,128]{5,4,3,2,1,0:T(8,128)(2,1)S(1)}, u32[]{:S(2)}, u32[]{:S(2)}) collective-permute-start(bf16[3,2,1,1,128,128]{5,4,3,2,1,0:T(8,128)(2,1)} %get-tuple-element.38), channel_id=1, source_target_pairs={{0,1},{1,0},{2,3},{3,2},{4,5},{5,4},{6,7},{7,6},{8,9},{9,8},{10,11... | collective-permute-start | bytes 589832 | tf_op jit(solution)/shard_map/ppermute | solution.py:533
  47.5 13.9 %collective-permute-start.11 = (bf16[3,2,1,1,128,128]{5,4,3,2,1,0:T(8,128)(2,1)}, bf16[3,2,1,1,128,128]{5,4,3,2,1,0:T(8,128)(2,1)S(1)}, u32[]{:S(2)}, u32[]{:S(2)}) collective-permute-start(bf16[3,2,1,1,128,128]{5,4,3,2,1,0:T(8,128)(2,1)} %get-tuple-element.41), channel_id=1, source_target_pairs={{0,1},{1,0},{2,3},{3,2},{4,5},{5,4},{6,7},{7,6},{8,9},{9,8},{10,11... | collective-permute-start | bytes 589832 | tf_op jit(solution)/shard_map/ppermute | solution.py:533
  56.6 11.2 %collective-permute-start.12 = (f32[2,4,24,128]{3,2,1,0:T(8,128)S(1)}, f32[2,4,24,128]{3,2,1,0:T(8,128)S(1)}, u32[]{:S(2)}, u32[]{:S(2)}) collective-permute-start(f32[2,4,24,128]{3,2,1,0:T(8,128)S(1)} %shard_map.64.refs_11_.rest_0_), channel_id=1, source_target_pairs={{0,1},{1,0},{2,3},{3,2},{4,5},{5,4},{6,7},{7,6},{8,9},{9,8},{10,11... | collective-permute-start | bytes 294920 | tf_op jit(solution)/shard_map/ppermute | solution.py:545
  61.0 4.9 %collective-permute-start.13 = (f32[1,4,24,128]{3,2,1,0:T(8,128)S(1)}, f32[1,4,24,128]{3,2,1,0:T(8,128)S(1)}, u32[]{:S(2)}, u32[]{:S(2)}) collective-permute-start(f32[1,4,24,128]{3,2,1,0:T(8,128)S(1)} %shard_map.65.refs_11_.rest_1_), channel_id=1, source_target_pairs={{0,1},{1,0},{2,3},{3,2},{4,5},{5,4},{6,7},{7,6},{8,9},{9,8},{10,11... | collective-permute-start | bytes 147464 | tf_op jit(solution)/shard_map/ppermute | solution.py:545
  64.7 3.0 %collective-permute-start.14 = (f32[1,4,24,128]{3,2,1,0:T(8,128)S(1)}, f32[1,4,24,128]{3,2,1,0:T(8,128)S(1)}, u32[]{:S(2)}, u32[]{:S(2)}) collective-permute-start(f32[1,4,24,128]{3,2,1,0:T(8,128)S(1)} %shard_map.66.rest_2_), channel_id=1, source_target_pairs={{0,1},{1,0},{2,3},{3,2},{4,5},{5,4},{6,7},{7,6},{8,9},{9,8},{10,11... | collective-permute-start | bytes 147464 | tf_op jit(solution)/shard_map/ppermute | solution.py:545
  70.3 22.2 %all-to-all-start = ((f32[16,2,24,128]{3,2,1,0:T(8,128)}), f32[16,2,24,128]{3,2,1,0:T(8,128)S(1)}, u32[]{:S(2)}, u32[]{:S(2)}) async-start(f32[16,2,24,128]{3,2,1,0:T(8,128)} %bitcast.5), calls=%async_computation | async-start | bytes 786432 | tf_op jit(solution)/shard_map/all_to_all | solution.py:557

commit v4 on v3

--- a/solution.py
+++ b/solution.py
@@ -321,6 +321,18 @@
     lane = lax.broadcasted_iota(jnp.int32, (deep, LANES), 1)
     place = lane & 7
     taps = [tap(k) for k in range(FILTER_R + 1)]
+    most = jnp.zeros((deep, LANES), jnp.float32)
+    for ref in own + partner:
+        for i in range(tiles):
+            most = jnp.maximum(most, jnp.abs(ref[i]))
+    most = jnp.full((8, LANES), jnp.maximum(jnp.max(most), 1e-30))
+    power = jnp.ceil(jnp.log2(most) + 0.001)
+    scale = jnp.exp2(15.0 - power)[:1]
+    code = power[:1]
+    last_row = lax.broadcasted_iota(jnp.int32, (deep, LANES), 0) == deep - 1
+
+    def coded(value):
+        return jnp.where(last_row, code, value * scale)
 
     def turn(v, k):
         return pltpu.roll(v, k % LANES, 1)
@@ -349,8 +361,8 @@
                     place >= k, turn(v, k), turn(left, k - 8)
                 )
                 acc = acc + taps[k] * near
-            out[r, i, 0] = own[r][i]
-            out[r, i, 1] = acc * weight[i, r : r + 1, :]
+            out[r, i, 0] = coded(own[r][i])
+            out[r, i, 1] = coded(acc * weight[i, r : r + 1, :])
 
 
 def filtered(info, own, partner, weight):
@@ -427,11 +439,14 @@
 def series_kernel(block, got, inverse, screen, motion, right):
     sources, _, deep = got.shape[:3]
     right[...] = jnp.zeros_like(right)
-    for part in range(2):
-        lanes = pl.ds(part * LANES, LANES)
-        for s in range(sources):
+    used = lax.broadcasted_iota(jnp.int32, (deep, LANES), 0) < block + MAXB
+    for s in range(sources):
+        for part in range(2):
+            lanes = pl.ds(part * LANES, LANES)
             at = pl.ds(s * block, deep)
-            right[at, lanes] = right[at, lanes] + got[s, part]
+            values = got[s, part]
+            scale = jnp.exp2(values[deep - 1 :] - 15.0)
+            right[at, lanes] = right[at, lanes] + jnp.where(used, values * scale, 0.0)
     result = jnp.dot(
         right[: inverse.shape[0], :].T,
         inverse[...],
@@ -466,7 +481,7 @@
     groups, along, _ = (lax.axis_size(name) for name in ("pairs", "z", "x"))
     blocks = groups * along
     block = 2 * own
-    deep = -(-(block + MAXB) // 8) * 8
+    deep = -(-(block + MAXB + 1) // 8) * 8
     rows = groups
     if full != 2 * along * LANES or along % STRIPES or lines != rows * 8 * LA:
         raise ValueError("unsupported shape")
@@ -553,8 +568,9 @@
     weight = 1.0 / (row_weight[None, :, :] * col_weight[:, None, :])
 
     outgoing = filtered(info, sums, partner, weight)
-    outgoing = outgoing.reshape((rows * along,) + outgoing.shape[2:])
+    outgoing = outgoing.reshape((rows * along,) + outgoing.shape[2:]).astype(jnp.float16)
     got = lax.all_to_all(outgoing, ("pairs", "z"), split_axis=0, concat_axis=0, tiled=True)
+    got = got.astype(jnp.float32)
     screen, motion = invert_pixels(got, inverse, block)
     return tuple(jnp.transpose(v, (3, 0, 1, 2)) for v in (screen, motion))
 

time: 95 us -> 90.2 us (0.949)
  waiting for transfers between devices: 14.5 us -> 10.2 us
    all_to_all x1, waiting for transfers between devices: 8.37 us -> 4.08 us  [local(): lax.all_to_all(outgoing, ('pairs', 'z'), split_axis=0, concat_axis=0, til...]
  transfers between devices with their start and end apart: 16 -> 16, of which waited for: 4 -> 4; matrix products, arithmetic and copies ran while one was open for 1% -> 1% of each run, Pallas kernels for 33% -> 34%
where the time goes in v4:
time: 90.2 us; the launch traced here: 89.4 us
  starting transfers between devices  39.1 us (43%)
  Pallas kernels  36.8 us (41%)
  waiting for transfers between devices  10.2 us (11%)
  other arithmetic  1.57 us (2%)
    ppermute x4, starting transfers between devices, send_back(): going.append(lax.ppermute(v, ('pairs', 'z'), route))  18.5 us
    pallas_call x4, Pallas kernels, resample(): pl.pallas_call(partial(resample_kernel, first, parts), grid_spec=pltpu.Pr...  16.6 us
    pallas_call x4, Pallas kernels, pair_sums(): pl.pallas_call(partial(pair_kernel, own, [p[0] for p in pieces], [f[0] fo...  14 us
    all_to_all x1, starting transfers between devices, local(): lax.all_to_all(outgoing, ('pairs', 'z'), split_axis=0, concat_axis=0, til...  10.1 us
    ppermute x8, starting transfers between devices, local(): received.append(lax.ppermute(v, 'x', swap))  7.72 us
    all_to_all x1, waiting for transfers between devices, local(): lax.all_to_all(outgoing, ('pairs', 'z'), split_axis=0, concat_axis=0, til...  4.08 us
    ppermute x8, waiting for transfers between devices, local(): received.append(lax.ppermute(v, 'x', swap))  4.07 us
    pallas_call x1, Pallas kernels, invert(): pl.pallas_call(invert_kernel, in_specs=[vmem()], out_specs=vmem(), out_sh...  3.27 us
  transfers between devices with their start and end apart: 16, of which 4 were waited for; matrix products, arithmetic and copies ran while one was open for 1% of the time, Pallas kernels for 34%

profile of v4, /device:TPU:1, one launch (start us, length us, event | category | flops | bytes accessed | tf_op | source)
XLA Modules:
  0.0 89.4 jit_solution(827575127244074093)
XLA Ops:
  0.6 0.6 pad_add_fusion.info
  1.2 3.2 %shard_map.59 = (bf16[1,2,4,1,128,128]{5,4,3,2,1,0:T(8,128)(2,1)}, bf16[1,2,4,1,128,128]{5,4,3,2,1,0:T(8,128)(2,1)}) custom-call(s32[3]{0:T(128)} %pad_add_fusion.info, s32[256]{0:T(256)} %az.7, s32[256]{0:T(256)} %rg.7, bf16[8,2,128,1024]{3,2,1,0:T(8,128)(2,1)} %img.7), custom_call_target="tpu_custom_call" | custom-call | flops 524288 | bytes 1048576 | tf_op jit(solution)/shard_map/pallas_call | solution.py:147
  4.4 2.0 %collective-permute-start = (bf16[1,2,4,1,128,128]{5,4,3,2,1,0:T(8,128)(2,1)}, bf16[1,2,4,1,128,128]{5,4,3,2,1,0:T(8,128)(2,1)S(1)}, u32[]{:S(2)}, u32[]{:S(2)}) collective-permute-start(bf16[1,2,4,1,128,128]{5,4,3,2,1,0:T(8,128)(2,1)} %get-tuple-element.24), channel_id=1, source_target_pairs={{0,1},{1,0},{2,3},{3,2},{4,5},{5,4},{6,7},{7,6},{8,9},{9,8},{10,11... | collective-permute-start | bytes 786440 | tf_op jit(solution)/shard_map/ppermute | solution.py:548
  6.4 3.2 %shard_map.60 = (bf16[1,2,4,1,128,128]{5,4,3,2,1,0:T(8,128)(2,1)}, bf16[1,2,4,1,128,128]{5,4,3,2,1,0:T(8,128)(2,1)}) custom-call(s32[3]{0:T(128)} %pad_add_fusion.info, s32[256]{0:T(256)} %az.7, s32[256]{0:T(256)} %rg.7, bf16[8,2,128,1024]{3,2,1,0:T(8,128)(2,1)} %img.7, bf16[1,2,4,1,128,128]{5,4,3,2,1,0:T(8,128)(2,1)} %get-tuple-element.23.rest_0_.refs_0_), custom_call_target="tpu_custom_call" | custom-call | flops 524288 | bytes 1048576 | tf_op jit(solution)/shard_map/pallas_call | solution.py:147
  9.6 0.0 collective-permute-start.1
  9.6 0.0 copy-start.5
  9.6 0.0 copy-start.2
  9.6 0.0 copy-start.3
  9.6 5.1 %shard_map.61 = (bf16[3,2,4,1,128,128]{5,4,3,2,1,0:T(8,128)(2,1)}, bf16[3,2,2,1,128,128]{5,4,3,2,1,0:T(8,128)(2,1)}, bf16[3,2,2,1,128,128]{5,4,3,2,1,0:T(8,128)(2,1)}) custom-call(s32[3]{0:T(128)} %pad_add_fusion.info, s32[256]{0:T(256)} %az.7, s32[256]{0:T(256)} %rg.7, bf16[8,2,128,1024]{3,2,1,0:T(8,128)(2,1)} %img.7, ...), custom_call_target="tpu_custom_call" | custom-call | flops 1572864 | bytes 3145728 | tf_op jit(solution)/shard_map/pallas_call | solution.py:147
  14.7 0.0 copy-start
  14.7 1.4 %collective-permute-start.2 = (bf16[3,2,2,1,128,128]{5,4,3,2,1,0:T(8,128)(2,1)}, bf16[3,2,2,1,128,128]{5,4,3,2,1,0:T(8,128)(2,1)S(1)}, u32[]{:S(2)}, u32[]{:S(2)}) collective-permute-start(bf16[3,2,2,1,128,128]{5,4,3,2,1,0:T(8,128)(2,1)} %get-tuple-element.28), channel_id=1, source_target_pairs={{0,1},{1,0},{2,3},{3,2},{4,5},{5,4},{6,7},{7,6},{8,9},{9,8},{10,11... | collective-permute-start | bytes 1179656 | tf_op jit(solution)/shard_map/ppermute | solution.py:548
  16.2 0.0 copy-start.4
  16.2 5.1 %shard_map.62 = (bf16[3,2,4,1,128,128]{5,4,3,2,1,0:T(8,128)(2,1)}, bf16[3,2,1,1,128,128]{5,4,3,2,1,0:T(8,128)(2,1)}, bf16[3,2,1,1,128,128]{5,4,3,2,1,0:T(8,128)(...) custom-call(s32[3]{0:T(128)} %pad_add_fusion.info, s32[256]{0:T(256)} %az.7, s32[256]{0:T(256)} %rg.7, ...), custom_call_target="tpu_custom_call" | custom-call | flops 1572864 | bytes 3145728 | tf_op jit(solution)/shard_map/pallas_call | solution.py:147
  21.3 0.0 copy-start.1
  21.3 0.1 collective-permute-start.7
  21.3 1.4 %collective-permute-start.8 = (bf16[3,2,2,1,128,128]{5,4,3,2,1,0:T(8,128)(2,1)}, bf16[3,2,2,1,128,128]{5,4,3,2,1,0:T(8,128)(2,1)S(1)}, u32[]{:S(2)}, u32[]{:S(2)}) collective-permute-start(bf16[3,2,2,1,128,128]{5,4,3,2,1,0:T(8,128)(2,1)} %get-tuple-element.37), channel_id=1, source_target_pairs={{0,1},{1,0},{2,3},{3,2},{4,5},{5,4},{6,7},{7,6},{8,9},{9,8},{10,11... | collective-permute-start | bytes 1179656 | tf_op jit(solution)/shard_map/ppermute | solution.py:548
  22.8 0.0 copy-done.5
  22.8 0.3 convolution_convert_fusion.mask
  23.1 0.0 collective-permute-done.refs_1_
  23.1 0.0 copy-done.2
  23.2 7.2 %collective-permute-start.4 = (bf16[1,2,4,1,128,128]{5,4,3,2,1,0:T(8,128)(2,1)S(1)}, bf16[1,2,4,1,128,128]{5,4,3,2,1,0:T(8,128)(2,1)S(1)}, u32[]{:S(2)}, u32[]{:S(2)}) collective-permute-start(bf16[1,2,4,1,128,128]{5,4,3,2,1,0:T(8,128)(2,1)S(1)} %broadcast_select_fusion.1), channel_id=1, source_target_pairs={{2,0},{4,2},{6,4},{8,6},{10,8},{12,10},{14,12},{16,14},{18,16},{20... | collective-permute-start | bytes 786440 | tf_op jit(solution)/shard_map/ppermute | solution.py:539
  30.4 0.0 collective-permute-done.1.refs_3_
  30.4 0.0 copy-done.3
  30.4 2.4 %collective-permute-start.5 = (bf16[1,2,4,1,128,128]{5,4,3,2,1,0:T(8,128)(2,1)S(1)}, bf16[1,2,4,1,128,128]{5,4,3,2,1,0:T(8,128)(2,1)S(1)}, u32[]{:S(2)}, u32[]{:S(2)}) collective-permute-start(bf16[1,2,4,1,128,128]{5,4,3,2,1,0:T(8,128)(2,1)S(1)} %broadcast_select_fusion), channel_id=1, source_target_pairs={{2,0},{4,2},{6,4},{8,6},{10,8},{12,10},{14,12},{16,14},{18,16},{20... | collective-permute-start | bytes 786440 | tf_op jit(solution)/shard_map/ppermute | solution.py:539
  32.8 0.0 collective-permute-done.2.refs_5_
  32.8 0.0 copy-done
  32.9 2.4 %collective-permute-start.6 = (bf16[3,2,2,1,128,128]{5,4,3,2,1,0:T(8,128)(2,1)S(1)}, bf16[3,2,2,1,128,128]{5,4,3,2,1,0:T(8,128)(2,1)S(1)}, u32[]{:S(2)}, u32[]{:S(2)}) collective-permute-start(bf16[3,2,2,1,128,128]{5,4,3,2,1,0:T(8,128)(2,1)S(1)} %slice_select_fusion.1), channel_id=1, source_target_pairs={{2,0},{4,2},{6,4},{8,6},{10,8},{12,10},{14,12},{16,14},{18,16},{20... | collective-permute-start | bytes 1179656 | tf_op jit(solution)/shard_map/ppermute | solution.py:539
  35.2 4.1 %collective-permute-done.8.refs_5_ = bf16[3,2,2,1,128,128]{5,4,3,2,1,0:T(8,128)(2,1)S(1)} collective-permute-done((bf16[3,2,2,1,128,128]{5,4,3,2,1,0:T(8,128)(2,1)}, bf16[3,2,2,1,128,128]{5,4,3,2,1,0:T(8,128)(2,1)S(1)}, u32[]{:S(2)}, u32[]{:S(2)}) %collective-permute-start.8) | collective-permute-done | bytes 393248 | tf_op jit(solution)/shard_map/ppermute | solution.py:548
  39.3 6.6 %collective-permute-start.10 = (bf16[3,2,2,1,128,128]{5,4,3,2,1,0:T(8,128)(2,1)S(1)}, bf16[3,2,2,1,128,128]{5,4,3,2,1,0:T(8,128)(2,1)S(1)}, u32[]{:S(2)}, u32[]{:S(2)}) collective-permute-start(bf16[3,2,2,1,128,128]{5,4,3,2,1,0:T(8,128)(2,1)S(1)} %slice_select_fusion), channel_id=1, source_target_pairs={{2,0},{4,2},{6,4},{8,6},{10,8},{12,10},{14,12},{16,14},{18,16},{20... | collective-permute-start | bytes 1179656 | tf_op jit(solution)/shard_map/ppermute | solution.py:539
  46.0 0.0 collective-permute-done.7.refs_7_
  46.0 1.3 %collective-permute-start.3 = (bf16[3,2,1,1,128,128]{5,4,3,2,1,0:T(8,128)(2,1)}, bf16[3,2,1,1,128,128]{5,4,3,2,1,0:T(8,128)(2,1)S(1)}, u32[]{:S(2)}, u32[]{:S(2)}) collective-permute-start(bf16[3,2,1,1,128,128]{5,4,3,2,1,0:T(8,128)(2,1)} %get-tuple-element.30), channel_id=1, source_target_pairs={{0,1},{1,0},{2,3},{3,2},{4,5},{5,4},{6,7},{7,6},{8,9},{9,8},{10,11... | collective-permute-start | bytes 589832 | tf_op jit(solution)/shard_map/ppermute | solution.py:548
  47.3 0.0 collective-permute-done.4.refs_8_
  47.3 0.3 collective-permute-start.9
  47.5 0.0 collective-permute-done.5.refs_9_
  47.5 1.2 %collective-permute-start.11 = (bf16[3,2,1,1,128,128]{5,4,3,2,1,0:T(8,128)(2,1)}, bf16[3,2,1,1,128,128]{5,4,3,2,1,0:T(8,128)(2,1)S(1)}, u32[]{:S(2)}, u32[]{:S(2)}) collective-permute-start(bf16[3,2,1,1,128,128]{5,4,3,2,1,0:T(8,128)(2,1)} %get-tuple-element.41), channel_id=1, source_target_pairs={{0,1},{1,0},{2,3},{3,2},{4,5},{5,4},{6,7},{7,6},{8,9},{9,8},{10,11... | collective-permute-start | bytes 589832 | tf_op jit(solution)/shard_map/ppermute | solution.py:548
  48.7 0.1 select_add_fusion
  48.8 0.2 collective-permute-done.6.refs_10_
  49.1 0.0 copy-done.4
  49.1 0.0 copy-done.1
  49.1 4.2 %shard_map.63.refs_11_ = f32[1,4,24,128]{3,2,1,0:T(8,128)S(1)} custom-call(s32[3]{0:T(128)S(1)} %copy-done.4, s32[5,256]{1,0:T(8,128)S(1)} %convolution_convert_fusion.mask, bf16[1,2,4,1,128,128]{5,4,3,2,1,0:T(8,128)(2,1)S(1)} %copy-done.2, bf16[1,2,4,1,128,128]{5,4,3,2,1,0:T(8,128)(2,1)S(1)} %collective-permute-done.refs_1_, ...), custom_call_target="tpu_custom_call" | custom-call | flops 10485760 | bytes 1310720 | tf_op jit(solution)/shard_map/pallas_call | solution.py:290
  53.3 0.0 collective-permute-done.3.refs_7_
  53.3 3.3 %shard_map.64.refs_11_.rest_0_ = f32[2,4,24,128]{3,2,1,0:T(8,128)S(1)} custom-call(s32[3]{0:T(128)S(1)} %copy-done.4, s32[5,256]{1,0:T(8,128)S(1)} %convolution_convert_fusion.mask, bf16[1,2,4,1,128,128]{5,4,3,2,1,0:T(8,128)(2,1)S(1)} %copy-done.2, bf16[1,2,4,1,128,128]{5,4,3,2,1,0:T(8,128)(2,1)S(1)} %collective-permute-done.refs_1_, ...), custom_call_target="tpu_custom_call" | custom-call | flops 10485760 | bytes 1310720 | tf_op jit(solution)/shard_map/pallas_call | solution.py:290
  56.6 1.2 %collective-permute-start.12 = (f32[2,4,24,128]{3,2,1,0:T(8,128)S(1)}, f32[2,4,24,128]{3,2,1,0:T(8,128)S(1)}, u32[]{:S(2)}, u32[]{:S(2)}) collective-permute-start(f32[2,4,24,128]{3,2,1,0:T(8,128)S(1)} %shard_map.64.refs_11_.rest_0_), channel_id=1, source_target_pairs={{0,1},{1,0},{2,3},{3,2},{4,5},{5,4},{6,7},{7,6},{8,9},{9,8},{10,11... | collective-permute-start | bytes 294920 | tf_op jit(solution)/shard_map/ppermute | solution.py:560
  57.7 0.0 collective-permute-done.9.refs_7_
  57.8 0.0 collective-permute-done.10.refs_10_
  57.8 3.3 %shard_map.65.refs_11_.rest_1_ = f32[1,4,24,128]{3,2,1,0:T(8,128)S(1)} custom-call(s32[3]{0:T(128)S(1)} %copy-done.4, s32[5,256]{1,0:T(8,128)S(1)} %convolution_convert_fusion.mask, bf16[1,2,4,1,128,128]{5,4,3,2,1,0:T(8,128)(2,1)S(1)} %copy-done.2, bf16[1,2,4,1,128,128]{5,4,3,2,1,0:T(8,128)(2,1)S(1)} %collective-permute-done.refs_1_, ...), custom_call_target="tpu_custom_call" | custom-call | flops 10485760 | bytes 1310720 | tf_op jit(solution)/shard_map/pallas_call | solution.py:290
  61.0 0.4 collective-permute-start.13
  61.5 0.0 collective-permute-done.11.refs_7_
  61.5 3.3 %shard_map.66.rest_2_ = f32[1,4,24,128]{3,2,1,0:T(8,128)S(1)} custom-call(s32[3]{0:T(128)S(1)} %copy-done.4, s32[5,256]{1,0:T(8,128)S(1)} %convolution_convert_fusion.mask, bf16[1,2,4,1,128,128]{5,4,3,2,1,0:T(8,128)(2,1)S(1)} %copy-done.2, bf16[1,2,4,1,128,128]{5,4,3,2,1,0:T(8,128)(2,1)S(1)} %collective-permute-done.refs_1_, ...), custom_call_target="tpu_custom_call" | custom-call | flops 10485760 | bytes 1310720 | tf_op jit(solution)/shard_map/pallas_call | solution.py:290
  64.7 1.2 %collective-permute-start.14 = (f32[1,4,24,128]{3,2,1,0:T(8,128)S(1)}, f32[1,4,24,128]{3,2,1,0:T(8,128)S(1)}, u32[]{:S(2)}, u32[]{:S(2)}) collective-permute-start(f32[1,4,24,128]{3,2,1,0:T(8,128)S(1)} %shard_map.66.rest_2_), channel_id=1, source_target_pairs={{0,1},{1,0},{2,3},{3,2},{4,5},{5,4},{6,7},{7,6},{8,9},{9,8},{10,11... | collective-permute-start | bytes 147464 | tf_op jit(solution)/shard_map/ppermute | solution.py:560
  65.9 0.0 collective-permute-done.13.rest_4_
  65.9 1.8 %collective-permute-done.14.rest_5_ = f32[1,4,24,128]{3,2,1,0:T(8,128)S(1)} collective-permute-done((f32[1,4,24,128]{3,2,1,0:T(8,128)S(1)}, f32[1,4,24,128]{3,2,1,0:T(8,128)S(1)}, u32[]{:S(2)}, u32[]{:S(2)}) %collective-permute-start.14) | collective-permute-done | bytes 49184 | tf_op jit(solution)/shard_map/ppermute | solution.py:560
  67.8 0.0 collective-permute-done.12.rest_3_
  67.8 1.9 %smooth.1 = f32[4,4,2,24,128]{4,3,2,1,0:T(8,128)S(1)} custom-call(s32[3]{0:T(128)S(1)} %copy-done.4, f32[2,4,24,128]{3,2,1,0:T(8,128)S(1)} %shard_map.64.refs_11_.rest_0_, f32[1,4,24,128]{3,2,1,0:T(8,128)S(1)} %shard_map.65.refs_11_.rest_1_, f32[1,4,24,128]{3,2,1,0:T(8,128)S(1)} %shard_map.66.rest_2_, f32[2,4,24,128]{3,2,1,0:T(8,128)S(1)} %collective-permute-done.12.rest_3_, ...), custom_call_target="tpu_custom_call" | custom-call | tf_op jit(solution)/shard_map/smooth/pallas_call | solution.py:373
  69.6 0.7 convert_element_type.25
  70.3 10.1 %all-to-all-start = ((f16[16,2,24,128]{3,2,1,0:T(8,128)(2,1)}), f16[16,2,24,128]{3,2,1,0:T(8,128)(2,1)S(1)}, u32[]{:S(2)}, u32[]{:S(2)}) async-start(f16[16,2,24,128]{3,2,1,0:T(8,128)(2,1)} %bitcast.5), calls=%async_computation | async-start | bytes 393216 | tf_op jit(solution)/shard_map/all_to_all | solution.py:572
  80.4 0.5 convolution_add_fusion.normal
  80.9 3.3 %invert.1.inverse = f32[256,256]{1,0:T(8,128)S(1)} custom-call(f32[256,256]{1,0:T(8,128)S(1)} %convolution_add_fusion.normal), custom_call_target="tpu_custom_call" | custom-call | flops 2013265920 | bytes 524288 | tf_op jit(solution)/shard_map/invert/pallas_call | solution.py:426
  84.2 4.1 %all-to-all-done = f16[16,2,24,128]{3,2,1,0:T(8,128)(2,1)S(1)} async-done(((f16[16,2,24,128]{3,2,1,0:T(8,128)(2,1)}), f16[16,2,24,128]{3,2,1,0:T(8,128)(2,1)S(1)}, u32[]{:S(2)}, u32[]{:S(2)}) %all-to-all-start) | async-done | bytes 196640 | tf_op jit(solution)/shard_map/all_to_all | solution.py:572
  88.3 1.1 %series.1 = (f32[2,8,8,256]{3,2,1,0:T(8,128)}, f32[2,8,8,256]{3,2,1,0:T(8,128)}) custom-call(f32[16,2,24,128]{3,2,1,0:T(8,128)S(1)} %convert_element_type.27.got, f32[256,256]{1,0:T(8,128)S(1)} %invert.1.inverse), custom_call_target="tpu_custom_call" | custom-call | tf_op jit(solution)/shard_map/series/pallas_call | solution.py:467
  (13 shorter events, 0.2 us)
Async XLA Ops:
  4.4 18.8 %collective-permute-start = (bf16[1,2,4,1,128,128]{5,4,3,2,1,0:T(8,128)(2,1)}, bf16[1,2,4,1,128,128]{5,4,3,2,1,0:T(8,128)(2,1)S(1)}, u32[]{:S(2)}, u32[]{:S(2)}) collective-permute-start(bf16[1,2,4,1,128,128]{5,4,3,2,1,0:T(8,128)(2,1)} %get-tuple-element.24), channel_id=1, source_target_pairs={{0,1},{1,0},{2,3},{3,2},{4,5},{5,4},{6,7},{7,6},{8,9},{9,8},{10,11... | collective-permute-start | bytes 786440 | tf_op jit(solution)/shard_map/ppermute | solution.py:548
  9.6 20.8 %collective-permute-start.1 = (bf16[1,2,4,1,128,128]{5,4,3,2,1,0:T(8,128)(2,1)}, bf16[1,2,4,1,128,128]{5,4,3,2,1,0:T(8,128)(2,1)S(1)}, u32[]{:S(2)}, u32[]{:S(2)}) collective-permute-start(bf16[1,2,4,1,128,128]{5,4,3,2,1,0:T(8,128)(2,1)} %get-tuple-element.26), channel_id=1, source_target_pairs={{0,1},{1,0},{2,3},{3,2},{4,5},{5,4},{6,7},{7,6},{8,9},{9,8},{10,11... | collective-permute-start | bytes 786440 | tf_op jit(solution)/shard_map/ppermute | solution.py:548
  9.6 13.2 %copy-start.5 = (s32[1000,2]{0,1:T(2,128)S(1)}, s32[1000,2]{0,1:T(2,128)}, u32[]{:S(2)}) copy-start(s32[1000,2]{0,1:T(2,128)} %param.7) | copy-start | bytes 24004
  9.6 13.6 %copy-start.2 = (bf16[1,2,4,1,128,128]{5,4,3,2,1,0:T(8,128)(2,1)S(1)}, bf16[1,2,4,1,128,128]{5,4,3,2,1,0:T(8,128)(2,1)}, u32[]{:S(2)}) copy-start(bf16[1,2,4,1,128,128]{5,4,3,2,1,0:T(8,128)(2,1)} %get-tuple-element.23.rest_0_.refs_0_) | copy-start | bytes 786436
  9.6 20.8 %copy-start.3 = (bf16[1,2,4,1,128,128]{5,4,3,2,1,0:T(8,128)(2,1)S(1)}, bf16[1,2,4,1,128,128]{5,4,3,2,1,0:T(8,128)(2,1)}, u32[]{:S(2)}) copy-start(bf16[1,2,4,1,128,128]{5,4,3,2,1,0:T(8,128)(2,1)} %get-tuple-element.25.rest_0_.refs_2_) | copy-start | bytes 786436
  14.7 18.1 %copy-start = (bf16[3,2,4,1,128,128]{5,4,3,2,1,0:T(8,128)(2,1)S(1)}, bf16[3,2,4,1,128,128]{5,4,3,2,1,0:T(8,128)(2,1)}, u32[]{:S(2)}) copy-start(bf16[3,2,4,1,128,128]{5,4,3,2,1,0:T(8,128)(2,1)} %get-tuple-element.27.rest_0_.refs_4_) | copy-start | bytes 2359300
  14.7 18.1 %collective-permute-start.2 = (bf16[3,2,2,1,128,128]{5,4,3,2,1,0:T(8,128)(2,1)}, bf16[3,2,2,1,128,128]{5,4,3,2,1,0:T(8,128)(2,1)S(1)}, u32[]{:S(2)}, u32[]{:S(2)}) collective-permute-start(bf16[3,2,2,1,128,128]{5,4,3,2,1,0:T(8,128)(2,1)} %get-tuple-element.28), channel_id=1, source_target_pairs={{0,1},{1,0},{2,3},{3,2},{4,5},{5,4},{6,7},{7,6},{8,9},{9,8},{10,11... | collective-permute-start | bytes 1179656 | tf_op jit(solution)/shard_map/ppermute | solution.py:548
  16.2 32.9 %copy-start.4 = (s32[3]{0:T(128)S(1)}, s32[3]{0:T(128)}, u32[]{:S(2)}) copy-start(s32[3]{0:T(128)} %pad_add_fusion.info) | copy-start | bytes 40
  21.3 27.8 %copy-start.1 = (bf16[3,2,4,1,128,128]{5,4,3,2,1,0:T(8,128)(2,1)S(1)}, bf16[3,2,4,1,128,128]{5,4,3,2,1,0:T(8,128)(2,1)}, u32[]{:S(2)}) copy-start(bf16[3,2,4,1,128,128]{5,4,3,2,1,0:T(8,128)(2,1)} %get-tuple-element.29.refs_6_) | copy-start | bytes 2359300
  21.3 24.7 %collective-permute-start.7 = (bf16[3,2,1,1,128,128]{5,4,3,2,1,0:T(8,128)(2,1)}, bf16[3,2,1,1,128,128]{5,4,3,2,1,0:T(8,128)(2,1)}, u32[]{:S(2)}, u32[]{:S(2)}) collective-permute-start(bf16[3,2,1,1,128,128]{5,4,3,2,1,0:T(8,128)(2,1)} %get-tuple-element.36), channel_id=1, source_target_pairs={{0,1},{1,0},{2,3},{3,2},{4,5},{5,4},{6,7},{7,6},{8,9},{9,8},{10,11... | collective-permute-start | bytes 589832 | tf_op jit(solution)/shard_map/ppermute | solution.py:548
  21.3 18.0 %collective-permute-start.8 = (bf16[3,2,2,1,128,128]{5,4,3,2,1,0:T(8,128)(2,1)}, bf16[3,2,2,1,128,128]{5,4,3,2,1,0:T(8,128)(2,1)S(1)}, u32[]{:S(2)}, u32[]{:S(2)}) collective-permute-start(bf16[3,2,2,1,128,128]{5,4,3,2,1,0:T(8,128)(2,1)} %get-tuple-element.37), channel_id=1, source_target_pairs={{0,1},{1,0},{2,3},{3,2},{4,5},{5,4},{6,7},{7,6},{8,9},{9,8},{10,11... | collective-permute-start | bytes 1179656 | tf_op jit(solution)/shard_map/ppermute | solution.py:548
  23.2 24.1 %collective-permute-start.4 = (bf16[1,2,4,1,128,128]{5,4,3,2,1,0:T(8,128)(2,1)S(1)}, bf16[1,2,4,1,128,128]{5,4,3,2,1,0:T(8,128)(2,1)S(1)}, u32[]{:S(2)}, u32[]{:S(2)}) collective-permute-start(bf16[1,2,4,1,128,128]{5,4,3,2,1,0:T(8,128)(2,1)S(1)} %broadcast_select_fusion.1), channel_id=1, source_target_pairs={{2,0},{4,2},{6,4},{8,6},{10,8},{12,10},{14,12},{16,14},{18,16},{20... | collective-permute-start | bytes 786440 | tf_op jit(solution)/shard_map/ppermute | solution.py:539
  30.4 17.1 %collective-permute-start.5 = (bf16[1,2,4,1,128,128]{5,4,3,2,1,0:T(8,128)(2,1)S(1)}, bf16[1,2,4,1,128,128]{5,4,3,2,1,0:T(8,128)(2,1)S(1)}, u32[]{:S(2)}, u32[]{:S(2)}) collective-permute-start(bf16[1,2,4,1,128,128]{5,4,3,2,1,0:T(8,128)(2,1)S(1)} %broadcast_select_fusion), channel_id=1, source_target_pairs={{2,0},{4,2},{6,4},{8,6},{10,8},{12,10},{14,12},{16,14},{18,16},{20... | collective-permute-start | bytes 786440 | tf_op jit(solution)/shard_map/ppermute | solution.py:539
  32.9 16.2 %collective-permute-start.6 = (bf16[3,2,2,1,128,128]{5,4,3,2,1,0:T(8,128)(2,1)S(1)}, bf16[3,2,2,1,128,128]{5,4,3,2,1,0:T(8,128)(2,1)S(1)}, u32[]{:S(2)}, u32[]{:S(2)}) collective-permute-start(bf16[3,2,2,1,128,128]{5,4,3,2,1,0:T(8,128)(2,1)S(1)} %slice_select_fusion.1), channel_id=1, source_target_pairs={{2,0},{4,2},{6,4},{8,6},{10,8},{12,10},{14,12},{16,14},{18,16},{20... | collective-permute-start | bytes 1179656 | tf_op jit(solution)/shard_map/ppermute | solution.py:539
  39.3 18.4 %collective-permute-start.10 = (bf16[3,2,2,1,128,128]{5,4,3,2,1,0:T(8,128)(2,1)S(1)}, bf16[3,2,2,1,128,128]{5,4,3,2,1,0:T(8,128)(2,1)S(1)}, u32[]{:S(2)}, u32[]{:S(2)}) collective-permute-start(bf16[3,2,2,1,128,128]{5,4,3,2,1,0:T(8,128)(2,1)S(1)} %slice_select_fusion), channel_id=1, source_target_pairs={{2,0},{4,2},{6,4},{8,6},{10,8},{12,10},{14,12},{16,14},{18,16},{20... | collective-permute-start | bytes 1179656 | tf_op jit(solution)/shard_map/ppermute | solution.py:539
  46.0 7.3 %collective-permute-start.3 = (bf16[3,2,1,1,128,128]{5,4,3,2,1,0:T(8,128)(2,1)}, bf16[3,2,1,1,128,128]{5,4,3,2,1,0:T(8,128)(2,1)S(1)}, u32[]{:S(2)}, u32[]{:S(2)}) collective-permute-start(bf16[3,2,1,1,128,128]{5,4,3,2,1,0:T(8,128)(2,1)} %get-tuple-element.30), channel_id=1, source_target_pairs={{0,1},{1,0},{2,3},{3,2},{4,5},{5,4},{6,7},{7,6},{8,9},{9,8},{10,11... | collective-permute-start | bytes 589832 | tf_op jit(solution)/shard_map/ppermute | solution.py:548
  47.3 10.5 %collective-permute-start.9 = (bf16[3,2,1,1,128,128]{5,4,3,2,1,0:T(8,128)(2,1)}, bf16[3,2,1,1,128,128]{5,4,3,2,1,0:T(8,128)(2,1)S(1)}, u32[]{:S(2)}, u32[]{:S(2)}) collective-permute-start(bf16[3,2,1,1,128,128]{5,4,3,2,1,0:T(8,128)(2,1)} %get-tuple-element.38), channel_id=1, source_target_pairs={{0,1},{1,0},{2,3},{3,2},{4,5},{5,4},{6,7},{7,6},{8,9},{9,8},{10,11... | collective-permute-start | bytes 589832 | tf_op jit(solution)/shard_map/ppermute | solution.py:548
  47.5 13.9 %collective-permute-start.11 = (bf16[3,2,1,1,128,128]{5,4,3,2,1,0:T(8,128)(2,1)}, bf16[3,2,1,1,128,128]{5,4,3,2,1,0:T(8,128)(2,1)S(1)}, u32[]{:S(2)}, u32[]{:S(2)}) collective-permute-start(bf16[3,2,1,1,128,128]{5,4,3,2,1,0:T(8,128)(2,1)} %get-tuple-element.41), channel_id=1, source_target_pairs={{0,1},{1,0},{2,3},{3,2},{4,5},{5,4},{6,7},{7,6},{8,9},{9,8},{10,11... | collective-permute-start | bytes 589832 | tf_op jit(solution)/shard_map/ppermute | solution.py:548
  56.6 11.2 %collective-permute-start.12 = (f32[2,4,24,128]{3,2,1,0:T(8,128)S(1)}, f32[2,4,24,128]{3,2,1,0:T(8,128)S(1)}, u32[]{:S(2)}, u32[]{:S(2)}) collective-permute-start(f32[2,4,24,128]{3,2,1,0:T(8,128)S(1)} %shard_map.64.refs_11_.rest_0_), channel_id=1, source_target_pairs={{0,1},{1,0},{2,3},{3,2},{4,5},{5,4},{6,7},{7,6},{8,9},{9,8},{10,11... | collective-permute-start | bytes 294920 | tf_op jit(solution)/shard_map/ppermute | solution.py:560
  61.0 4.9 %collective-permute-start.13 = (f32[1,4,24,128]{3,2,1,0:T(8,128)S(1)}, f32[1,4,24,128]{3,2,1,0:T(8,128)S(1)}, u32[]{:S(2)}, u32[]{:S(2)}) collective-permute-start(f32[1,4,24,128]{3,2,1,0:T(8,128)S(1)} %shard_map.65.refs_11_.rest_1_), channel_id=1, source_target_pairs={{0,1},{1,0},{2,3},{3,2},{4,5},{5,4},{6,7},{7,6},{8,9},{9,8},{10,11... | collective-permute-start | bytes 147464 | tf_op jit(solution)/shard_map/ppermute | solution.py:560
  64.7 3.0 %collective-permute-start.14 = (f32[1,4,24,128]{3,2,1,0:T(8,128)S(1)}, f32[1,4,24,128]{3,2,1,0:T(8,128)S(1)}, u32[]{:S(2)}, u32[]{:S(2)}) collective-permute-start(f32[1,4,24,128]{3,2,1,0:T(8,128)S(1)} %shard_map.66.rest_2_), channel_id=1, source_target_pairs={{0,1},{1,0},{2,3},{3,2},{4,5},{5,4},{6,7},{7,6},{8,9},{9,8},{10,11... | collective-permute-start | bytes 147464 | tf_op jit(solution)/shard_map/ppermute | solution.py:560
  70.3 17.9 %all-to-all-start = ((f16[16,2,24,128]{3,2,1,0:T(8,128)(2,1)}), f16[16,2,24,128]{3,2,1,0:T(8,128)(2,1)S(1)}, u32[]{:S(2)}, u32[]{:S(2)}) async-start(f16[16,2,24,128]{3,2,1,0:T(8,128)(2,1)} %bitcast.5), calls=%async_computation | async-start | bytes 393216 | tf_op jit(solution)/shard_map/all_to_all | solution.py:572

commit v5 on v4

--- a/solution.py
+++ b/solution.py
@@ -29,7 +29,13 @@
     return jnp.exp(-jnp.float32(k * k) / jnp.float32(2.0 * sigma * sigma))
 
 
-def resample_kernel(first, parts, info, az, rg, img, *rest):
+def position(own):
+    x = lax.axis_index("x")
+    place = lax.axis_index("pairs") * lax.axis_size("z") + lax.axis_index("z")
+    return x, (2 * place + x) * own, 2 * place * own
+
+
+def resample_kernel(own_dates, first, parts, az, rg, img, *rest):
     rest = rest[-4 - parts :]
     keep, sends = rest[0], rest[1 : 1 + parts]
     tiles_of, spread, shifted = rest[1 + parts :]
@@ -39,8 +45,8 @@
     blocks = lines // (8 * LA)
     high = lines + 2 * MAXA
     span = STRIPES * LANES
-    date = info[1] + first + pl.program_id(0)
-    x = info[0]
+    x, base, _ = position(own_dates)
+    date = base + first + pl.program_id(0)
     shift = rg[date]
     step = az[date]
     behind = shift < 0
@@ -128,7 +134,7 @@
                 put(keep, block, block, c, group, x)
 
 
-def resample(images, az, rg, info, first, count, parts, earlier):
+def resample(images, az, rg, first, count, parts, earlier):
     lines, full = images.shape[2], images.shape[3]
     tiles = full // LANES
     groups = tiles // (2 * STRIPES)
@@ -145,9 +151,9 @@
 
     widths = [blocks] + [blocks // parts] * parts
     return pl.pallas_call(
-        partial(resample_kernel, first, parts),
+        partial(resample_kernel, images.shape[0], first, parts),
         grid_spec=pltpu.PrefetchScalarGridSpec(
-            num_scalar_prefetch=3,
+            num_scalar_prefetch=2,
             grid=(count,),
             in_specs=[pl.BlockSpec((1, 2, lines, full), lambda i, *_: (i + first, 0, 0, 0))]
             + [pl.BlockSpec(memory_space=pl.ANY)] * len(earlier),
@@ -165,7 +171,7 @@
             transcendentals=0,
             bytes_accessed=count * lines * full * 8,
         ),
-    )(info, az, rg, images, *earlier)
+    )(az, rg, images, *earlier)
 
 
 def merge(x, y, bit, distance):
@@ -174,12 +180,12 @@
     )
 
 
-def pair_kernel(own, starts, reached, info, mask, *refs):
+def pair_kernel(own, starts, reached, mask, *refs):
     count = len(starts)
     parts, following = refs[: 2 * count], refs[2 * count : 2 * count + len(reached)]
     right, images, products, sums = refs[-4:]
     block = 2 * own
-    x = info[0]
+    x, _, date0 = position(own)
     mine, other = x * own, (1 - x) * own
     for s, start in enumerate(starts):
         for where, ref in ((mine, parts[2 * s]), (other, parts[2 * s + 1])):
@@ -222,7 +228,7 @@
         )
         value = value + pltpu.roll(value, LANES - 16, 1)
         value = (value * (1.0 / (LA * LR))).astype(jnp.bfloat16).astype(jnp.float32)
-        return value * mask[g, info[2] + d].astype(jnp.float32)
+        return value * mask[g, date0 + d].astype(jnp.float32)
 
     step = 4 if block % 4 == 0 else 1
 
@@ -260,7 +266,7 @@
         right[0] = refs[-5][0]
 
 
-def pair_sums(info, mask, pieces, following, earlier, chunk, chunks, own, deep):
+def pair_sums(mask, pieces, following, earlier, chunk, chunks, own, deep):
     groups, lines = pieces[0][1].shape[3:5]
 
     def window(array, parts):
@@ -290,7 +296,7 @@
     return pl.pallas_call(
         partial(pair_kernel, own, [p[0] for p in pieces], [f[0] for f in following]),
         grid_spec=pltpu.PrefetchScalarGridSpec(
-            num_scalar_prefetch=2,
+            num_scalar_prefetch=1,
             grid=(groups,),
             in_specs=specs,
             out_specs=pl.BlockSpec((1 + joined, STRIPES, deep, LANES), lambda i, *_: (0, i, 0, 0)),
@@ -303,10 +309,10 @@
         out_shape=jax.ShapeDtypeStruct((1 + joined, groups * STRIPES, deep, LANES), jnp.float32),
         compiler_params=pltpu.CompilerParams(vmem_limit_bytes=GRANT),
         cost_estimate=pl.CostEstimate(flops=work * 8, transcendentals=0, bytes_accessed=work),
-    )(info, mask, *operands)
-
-
-def filter_kernel(count, info, *rest):
+    )(mask, *operands)
+
+
+def filter_kernel(count, *rest):
     weight, out, along = rest[2 * count :]
     own, partner = (
         [ref.at[i] for ref in refs for i in range(ref.shape[0])]
@@ -314,7 +320,7 @@
     )
     rows = len(own)
     tiles, deep = own[0].shape[:2]
-    x = info[0]
+    x = lax.axis_index("x")
     blank = jnp.zeros((rows, deep, LANES), jnp.float32)
     along[0] = blank
     along[2 * tiles + 1] = blank
@@ -365,20 +371,19 @@
             out[r, i, 1] = coded(acc * weight[i, r : r + 1, :])
 
 
-def filtered(info, own, partner, weight):
+def filtered(own, partner, weight):
     count = len(own)
     rows = sum(v.shape[0] for v in own)
     tiles, deep = own[0].shape[1:3]
-    smem = pl.BlockSpec(memory_space=pltpu.SMEM)
     return pl.pallas_call(
         partial(filter_kernel, count),
-        in_specs=[smem] + [vmem()] * (2 * count + 1),
+        in_specs=[vmem()] * (2 * count + 1),
         out_specs=vmem(),
         out_shape=jax.ShapeDtypeStruct((rows, tiles, 2, deep, LANES), jnp.float32),
         scratch_shapes=[pltpu.VMEM((2 * tiles + 2, rows, deep, LANES), jnp.float32)],
         name="smooth",
         compiler_params=pltpu.CompilerParams(vmem_limit_bytes=GRANT),
-    )(info, *own, *partner, weight)
+    )(*own, *partner, weight)
 
 
 def edge_weights(positions, whole):
@@ -486,8 +491,6 @@
     if full != 2 * along * LANES or along % STRIPES or lines != rows * 8 * LA:
         raise ValueError("unsupported shape")
     x = lax.axis_index("x")
-    place = lax.axis_index(("pairs", "z"))
-    info = jnp.stack([x, (2 * place + x) * own, place * block]).astype(jnp.int32)
 
     date_ids = jnp.arange(dates, dtype=jnp.int32)
     is_reference = date_ids[:, None] == pair_list[None, :, 0]
@@ -542,7 +545,7 @@
 
     for start, end, count in zip(cuts, cuts[1:], parts):
         after = [p[1] for p in pieces[-1:]]
-        keep, *sends = resample(images, az, rg, info, start, end - start, count, after)
+        keep, *sends = resample(images, az, rg, start, end - start, count, after)
         received = []
         for v in sends:
             received.append(lax.ppermute(v, "x", swap))
@@ -555,7 +558,7 @@
     sums = []
     for c in range(rows):
         earlier = sums[-1] if sums else None
-        sums.append(pair_sums(info, mask, pieces, following, earlier, c, rows, own, deep))
+        sums.append(pair_sums(mask, pieces, following, earlier, c, rows, own, deep))
     sums = sums[1:]
     partner = [lax.ppermute(s, "x", swap) for s in sums]
 
@@ -567,7 +570,7 @@
     col_weight = edge_weights(col_at, full // LR)
     weight = 1.0 / (row_weight[None, :, :] * col_weight[:, None, :])
 
-    outgoing = filtered(info, sums, partner, weight)
+    outgoing = filtered(sums, partner, weight)
     outgoing = outgoing.reshape((rows * along,) + outgoing.shape[2:]).astype(jnp.float16)
     got = lax.all_to_all(outgoing, ("pairs", "z"), split_axis=0, concat_axis=0, tiled=True)
     got = got.astype(jnp.float32)

time: 90.2 us -> 89.1 us (0.988)
  transfers between devices with their start and end apart: 16 -> 16, of which waited for: 4 -> 4; matrix products, arithmetic and copies ran while one was open for 1% -> 1% of each run, Pallas kernels for 34% -> 35%
where the time goes in v5:
time: 89.1 us; the launch traced here: 88.3 us
  starting transfers between devices  39.2 us (44%)
  Pallas kernels  36.3 us (41%)
  waiting for transfers between devices  10.2 us (11%)
  other arithmetic  1.02 us (1%)
    ppermute x4, starting transfers between devices, send_back(): going.append(lax.ppermute(v, ('pairs', 'z'), route))  18.5 us
    pallas_call x4, Pallas kernels, resample(): pl.pallas_call(partial(resample_kernel, images.shape[0], first, parts), g...  16.5 us
    pallas_call x4, Pallas kernels, pair_sums(): pl.pallas_call(partial(pair_kernel, own, [p[0] for p in pieces], [f[0] fo...  14 us
    all_to_all x1, starting transfers between devices, local(): lax.all_to_all(outgoing, ('pairs', 'z'), split_axis=0, concat_axis=0, til...  10.1 us
    ppermute x8, starting transfers between devices, local(): received.append(lax.ppermute(v, 'x', swap))  7.76 us
    ppermute x8, waiting for transfers between devices, local(): received.append(lax.ppermute(v, 'x', swap))  4.11 us
    all_to_all x1, waiting for transfers between devices, local(): lax.all_to_all(outgoing, ('pairs', 'z'), split_axis=0, concat_axis=0, til...  4.09 us
    pallas_call x1, Pallas kernels, invert(): pl.pallas_call(invert_kernel, in_specs=[vmem()], out_specs=vmem(), out_sh...  3.26 us
  transfers between devices with their start and end apart: 16, of which 4 were waited for; matrix products, arithmetic and copies ran while one was open for 1% of the time, Pallas kernels for 35%

profile of v5, /device:TPU:1, one launch (start us, length us, event | category | flops | bytes accessed | tf_op | source)
XLA Modules:
  0.0 88.3 jit_solution(9818976695092800994)
XLA Ops:
  0.6 3.2 %shard_map.59 = (bf16[1,2,4,1,128,128]{5,4,3,2,1,0:T(8,128)(2,1)}, bf16[1,2,4,1,128,128]{5,4,3,2,1,0:T(8,128)(2,1)}) custom-call(s32[256]{0:T(256)} %az.7, s32[256]{0:T(256)} %rg.7, bf16[8,2,128,1024]{3,2,1,0:T(8,128)(2,1)} %img.7), custom_call_target="tpu_custom_call" | custom-call | flops 524288 | bytes 1048576 | tf_op jit(solution)/shard_map/pallas_call | solution.py:153
  3.8 2.0 %collective-permute-start = (bf16[1,2,4,1,128,128]{5,4,3,2,1,0:T(8,128)(2,1)}, bf16[1,2,4,1,128,128]{5,4,3,2,1,0:T(8,128)(2,1)S(1)}, u32[]{:S(2)}, u32[]{:S(2)}) collective-permute-start(bf16[1,2,4,1,128,128]{5,4,3,2,1,0:T(8,128)(2,1)} %get-tuple-element.24), channel_id=1, source_target_pairs={{0,1},{1,0},{2,3},{3,2},{4,5},{5,4},{6,7},{7,6},{8,9},{9,8},{10,11... | collective-permute-start | bytes 786440 | tf_op jit(solution)/shard_map/ppermute | solution.py:551
  5.8 3.2 %shard_map.60 = (bf16[1,2,4,1,128,128]{5,4,3,2,1,0:T(8,128)(2,1)}, bf16[1,2,4,1,128,128]{5,4,3,2,1,0:T(8,128)(2,1)}) custom-call(s32[256]{0:T(256)} %az.7, s32[256]{0:T(256)} %rg.7, bf16[8,2,128,1024]{3,2,1,0:T(8,128)(2,1)} %img.7, bf16[1,2,4,1,128,128]{5,4,3,2,1,0:T(8,128)(2,1)} %get-tuple-element.23.rest_0_.refs_0_), custom_call_target="tpu_custom_call" | custom-call | flops 524288 | bytes 1048576 | tf_op jit(solution)/shard_map/pallas_call | solution.py:153
  9.0 0.0 collective-permute-start.1
  9.0 0.0 copy-start.4
  9.0 0.0 copy-start.2
  9.0 0.0 copy-start.3
  9.0 5.2 %shard_map.61 = (bf16[3,2,4,1,128,128]{5,4,3,2,1,0:T(8,128)(2,1)}, bf16[3,2,2,1,128,128]{5,4,3,2,1,0:T(8,128)(2,1)}, bf16[3,2,2,1,128,128]{5,4,3,2,1,0:T(8,128)(2,1)}) custom-call(s32[256]{0:T(256)} %az.7, s32[256]{0:T(256)} %rg.7, bf16[8,2,128,1024]{3,2,1,0:T(8,128)(2,1)} %img.7, bf16[1,2,4,1,128,128]{5,4,3,2,1,0:T(8,128)(2,1)} %get-tuple-element.25.rest_0_.refs_2_), custom_call_target="tpu_custom_call" | custom-call | flops 1572864 | bytes 3145728 | tf_op jit(solution)/shard_map/pallas_call | solution.py:153
  14.2 0.0 copy-start
  14.2 1.5 %collective-permute-start.2 = (bf16[3,2,2,1,128,128]{5,4,3,2,1,0:T(8,128)(2,1)}, bf16[3,2,2,1,128,128]{5,4,3,2,1,0:T(8,128)(2,1)S(1)}, u32[]{:S(2)}, u32[]{:S(2)}) collective-permute-start(bf16[3,2,2,1,128,128]{5,4,3,2,1,0:T(8,128)(2,1)} %get-tuple-element.28), channel_id=1, source_target_pairs={{0,1},{1,0},{2,3},{3,2},{4,5},{5,4},{6,7},{7,6},{8,9},{9,8},{10,11... | collective-permute-start | bytes 1179656 | tf_op jit(solution)/shard_map/ppermute | solution.py:551
  15.7 5.0 %shard_map.62 = (bf16[3,2,4,1,128,128]{5,4,3,2,1,0:T(8,128)(2,1)}, bf16[3,2,1,1,128,128]{5,4,3,2,1,0:T(8,128)(2,1)}, bf16[3,2,1,1,128,128]{5,4,3,2,1,0:T(8,128)(...) custom-call(s32[256]{0:T(256)} %az.7, s32[256]{0:T(256)} %rg.7, ...), custom_call_target="tpu_custom_call" | custom-call | flops 1572864 | bytes 3145728 | tf_op jit(solution)/shard_map/pallas_call | solution.py:153
  20.7 0.0 copy-start.1
  20.7 0.2 collective-permute-start.7
  20.9 1.3 %collective-permute-start.8 = (bf16[3,2,2,1,128,128]{5,4,3,2,1,0:T(8,128)(2,1)}, bf16[3,2,2,1,128,128]{5,4,3,2,1,0:T(8,128)(2,1)S(1)}, u32[]{:S(2)}, u32[]{:S(2)}) collective-permute-start(bf16[3,2,2,1,128,128]{5,4,3,2,1,0:T(8,128)(2,1)} %get-tuple-element.37), channel_id=1, source_target_pairs={{0,1},{1,0},{2,3},{3,2},{4,5},{5,4},{6,7},{7,6},{8,9},{9,8},{10,11... | collective-permute-start | bytes 1179656 | tf_op jit(solution)/shard_map/ppermute | solution.py:551
  22.2 0.0 copy-done.4
  22.2 0.3 convolution_convert_fusion.mask
  22.5 0.0 collective-permute-done.refs_1_
  22.5 0.0 copy-done.2
  22.6 7.2 %collective-permute-start.4 = (bf16[1,2,4,1,128,128]{5,4,3,2,1,0:T(8,128)(2,1)S(1)}, bf16[1,2,4,1,128,128]{5,4,3,2,1,0:T(8,128)(2,1)S(1)}, u32[]{:S(2)}, u32[]{:S(2)}) collective-permute-start(bf16[1,2,4,1,128,128]{5,4,3,2,1,0:T(8,128)(2,1)S(1)} %broadcast_select_fusion.1), channel_id=1, source_target_pairs={{2,0},{4,2},{6,4},{8,6},{10,8},{12,10},{14,12},{16,14},{18,16},{20... | collective-permute-start | bytes 786440 | tf_op jit(solution)/shard_map/ppermute | solution.py:542
  29.8 0.0 collective-permute-done.1.refs_3_
  29.8 0.0 copy-done.3
  29.8 2.4 %collective-permute-start.5 = (bf16[1,2,4,1,128,128]{5,4,3,2,1,0:T(8,128)(2,1)S(1)}, bf16[1,2,4,1,128,128]{5,4,3,2,1,0:T(8,128)(2,1)S(1)}, u32[]{:S(2)}, u32[]{:S(2)}) collective-permute-start(bf16[1,2,4,1,128,128]{5,4,3,2,1,0:T(8,128)(2,1)S(1)} %broadcast_select_fusion), channel_id=1, source_target_pairs={{2,0},{4,2},{6,4},{8,6},{10,8},{12,10},{14,12},{16,14},{18,16},{20... | collective-permute-start | bytes 786440 | tf_op jit(solution)/shard_map/ppermute | solution.py:542
  32.2 0.0 collective-permute-done.2.refs_5_
  32.2 0.0 copy-done
  32.3 2.4 %collective-permute-start.6 = (bf16[3,2,2,1,128,128]{5,4,3,2,1,0:T(8,128)(2,1)S(1)}, bf16[3,2,2,1,128,128]{5,4,3,2,1,0:T(8,128)(2,1)S(1)}, u32[]{:S(2)}, u32[]{:S(2)}) collective-permute-start(bf16[3,2,2,1,128,128]{5,4,3,2,1,0:T(8,128)(2,1)S(1)} %slice_select_fusion.1), channel_id=1, source_target_pairs={{2,0},{4,2},{6,4},{8,6},{10,8},{12,10},{14,12},{16,14},{18,16},{20... | collective-permute-start | bytes 1179656 | tf_op jit(solution)/shard_map/ppermute | solution.py:542
  34.6 4.1 %collective-permute-done.8.refs_5_ = bf16[3,2,2,1,128,128]{5,4,3,2,1,0:T(8,128)(2,1)S(1)} collective-permute-done((bf16[3,2,2,1,128,128]{5,4,3,2,1,0:T(8,128)(2,1)}, bf16[3,2,2,1,128,128]{5,4,3,2,1,0:T(8,128)(2,1)S(1)}, u32[]{:S(2)}, u32[]{:S(2)}) %collective-permute-start.8) | collective-permute-done | bytes 393248 | tf_op jit(solution)/shard_map/ppermute | solution.py:551
  38.8 6.6 %collective-permute-start.10 = (bf16[3,2,2,1,128,128]{5,4,3,2,1,0:T(8,128)(2,1)S(1)}, bf16[3,2,2,1,128,128]{5,4,3,2,1,0:T(8,128)(2,1)S(1)}, u32[]{:S(2)}, u32[]{:S(2)}) collective-permute-start(bf16[3,2,2,1,128,128]{5,4,3,2,1,0:T(8,128)(2,1)S(1)} %slice_select_fusion), channel_id=1, source_target_pairs={{2,0},{4,2},{6,4},{8,6},{10,8},{12,10},{14,12},{16,14},{18,16},{20... | collective-permute-start | bytes 1179656 | tf_op jit(solution)/shard_map/ppermute | solution.py:542
  45.4 0.0 collective-permute-done.7.refs_7_
  45.4 1.3 %collective-permute-start.3 = (bf16[3,2,1,1,128,128]{5,4,3,2,1,0:T(8,128)(2,1)}, bf16[3,2,1,1,128,128]{5,4,3,2,1,0:T(8,128)(2,1)S(1)}, u32[]{:S(2)}, u32[]{:S(2)}) collective-permute-start(bf16[3,2,1,1,128,128]{5,4,3,2,1,0:T(8,128)(2,1)} %get-tuple-element.30), channel_id=1, source_target_pairs={{0,1},{1,0},{2,3},{3,2},{4,5},{5,4},{6,7},{7,6},{8,9},{9,8},{10,11... | collective-permute-start | bytes 589832 | tf_op jit(solution)/shard_map/ppermute | solution.py:551
  46.7 0.0 collective-permute-done.4.refs_8_
  46.7 0.3 collective-permute-start.9
  47.0 0.0 collective-permute-done.5.refs_9_
  47.0 1.2 %collective-permute-start.11 = (bf16[3,2,1,1,128,128]{5,4,3,2,1,0:T(8,128)(2,1)}, bf16[3,2,1,1,128,128]{5,4,3,2,1,0:T(8,128)(2,1)S(1)}, u32[]{:S(2)}, u32[]{:S(2)}) collective-permute-start(bf16[3,2,1,1,128,128]{5,4,3,2,1,0:T(8,128)(2,1)} %get-tuple-element.41), channel_id=1, source_target_pairs={{0,1},{1,0},{2,3},{3,2},{4,5},{5,4},{6,7},{7,6},{8,9},{9,8},{10,11... | collective-permute-start | bytes 589832 | tf_op jit(solution)/shard_map/ppermute | solution.py:551
  48.2 0.1 select_add_fusion
  48.3 0.2 collective-permute-done.6.refs_10_
  48.5 0.0 copy-done.1
  48.5 4.2 %shard_map.63.refs_11_ = f32[1,4,24,128]{3,2,1,0:T(8,128)S(1)} custom-call(s32[5,256]{1,0:T(8,128)S(1)} %convolution_convert_fusion.mask, bf16[1,2,4,1,128,128]{5,4,3,2,1,0:T(8,128)(2,1)S(1)} %copy-done.2, bf16[1,2,4,1,128,128]{5,4,3,2,1,0:T(8,128)(2,1)S(1)} %collective-permute-done.refs_1_, bf16[1,2,4,1,128,128]{5,4,3,2,1,0:T(8,128)(2,1)S(1)} %copy-done.3, ...), custom_call_target="tpu_custom_call" | custom-call | flops 10485760 | bytes 1310720 | tf_op jit(solution)/shard_map/pallas_call | solution.py:296
  52.7 0.0 collective-permute-done.3.refs_7_
  52.7 3.3 %shard_map.64.refs_11_.rest_0_ = f32[2,4,24,128]{3,2,1,0:T(8,128)S(1)} custom-call(s32[5,256]{1,0:T(8,128)S(1)} %convolution_convert_fusion.mask, bf16[1,2,4,1,128,128]{5,4,3,2,1,0:T(8,128)(2,1)S(1)} %copy-done.2, bf16[1,2,4,1,128,128]{5,4,3,2,1,0:T(8,128)(2,1)S(1)} %collective-permute-done.refs_1_, bf16[1,2,4,1,128,128]{5,4,3,2,1,0:T(8,128)(2,1)S(1)} %copy-done.3, ...), custom_call_target="tpu_custom_call" | custom-call | flops 10485760 | bytes 1310720 | tf_op jit(solution)/shard_map/pallas_call | solution.py:296
  56.0 1.2 %collective-permute-start.12 = (f32[2,4,24,128]{3,2,1,0:T(8,128)S(1)}, f32[2,4,24,128]{3,2,1,0:T(8,128)S(1)}, u32[]{:S(2)}, u32[]{:S(2)}) collective-permute-start(f32[2,4,24,128]{3,2,1,0:T(8,128)S(1)} %shard_map.64.refs_11_.rest_0_), channel_id=1, source_target_pairs={{0,1},{1,0},{2,3},{3,2},{4,5},{5,4},{6,7},{7,6},{8,9},{9,8},{10,11... | collective-permute-start | bytes 294920 | tf_op jit(solution)/shard_map/ppermute | solution.py:563
  57.2 0.0 collective-permute-done.9.refs_7_
  57.2 0.0 collective-permute-done.10.refs_10_
  57.2 3.3 %shard_map.65.refs_11_.rest_1_ = f32[1,4,24,128]{3,2,1,0:T(8,128)S(1)} custom-call(s32[5,256]{1,0:T(8,128)S(1)} %convolution_convert_fusion.mask, bf16[1,2,4,1,128,128]{5,4,3,2,1,0:T(8,128)(2,1)S(1)} %copy-done.2, bf16[1,2,4,1,128,128]{5,4,3,2,1,0:T(8,128)(2,1)S(1)} %collective-permute-done.refs_1_, bf16[1,2,4,1,128,128]{5,4,3,2,1,0:T(8,128)(2,1)S(1)} %copy-done.3, ...), custom_call_target="tpu_custom_call" | custom-call | flops 10485760 | bytes 1310720 | tf_op jit(solution)/shard_map/pallas_call | solution.py:296
  60.5 0.4 collective-permute-start.13
  60.9 0.0 collective-permute-done.11.refs_7_
  60.9 3.3 %shard_map.66.rest_2_ = f32[1,4,24,128]{3,2,1,0:T(8,128)S(1)} custom-call(s32[5,256]{1,0:T(8,128)S(1)} %convolution_convert_fusion.mask, bf16[1,2,4,1,128,128]{5,4,3,2,1,0:T(8,128)(2,1)S(1)} %copy-done.2, bf16[1,2,4,1,128,128]{5,4,3,2,1,0:T(8,128)(2,1)S(1)} %collective-permute-done.refs_1_, bf16[1,2,4,1,128,128]{5,4,3,2,1,0:T(8,128)(2,1)S(1)} %copy-done.3, ...), custom_call_target="tpu_custom_call" | custom-call | flops 10485760 | bytes 1310720 | tf_op jit(solution)/shard_map/pallas_call | solution.py:296
  64.1 1.2 %collective-permute-start.14 = (f32[1,4,24,128]{3,2,1,0:T(8,128)S(1)}, f32[1,4,24,128]{3,2,1,0:T(8,128)S(1)}, u32[]{:S(2)}, u32[]{:S(2)}) collective-permute-start(f32[1,4,24,128]{3,2,1,0:T(8,128)S(1)} %shard_map.66.rest_2_), channel_id=1, source_target_pairs={{0,1},{1,0},{2,3},{3,2},{4,5},{5,4},{6,7},{7,6},{8,9},{9,8},{10,11... | collective-permute-start | bytes 147464 | tf_op jit(solution)/shard_map/ppermute | solution.py:563
  65.4 0.0 collective-permute-done.13.rest_4_
  65.4 1.8 %collective-permute-done.14.rest_5_ = f32[1,4,24,128]{3,2,1,0:T(8,128)S(1)} collective-permute-done((f32[1,4,24,128]{3,2,1,0:T(8,128)S(1)}, f32[1,4,24,128]{3,2,1,0:T(8,128)S(1)}, u32[]{:S(2)}, u32[]{:S(2)}) %collective-permute-start.14) | collective-permute-done | bytes 49184 | tf_op jit(solution)/shard_map/ppermute | solution.py:563
  67.2 0.0 collective-permute-done.12.rest_3_
  67.2 1.3 %smooth.1 = f32[4,4,2,24,128]{4,3,2,1,0:T(8,128)S(1)} custom-call(f32[2,4,24,128]{3,2,1,0:T(8,128)S(1)} %shard_map.64.refs_11_.rest_0_, f32[1,4,24,128]{3,2,1,0:T(8,128)S(1)} %shard_map.65.refs_11_.rest_1_, f32[1,4,24,128]{3,2,1,0:T(8,128)S(1)} %shard_map.66.rest_2_, f32[2,4,24,128]{3,2,1,0:T(8,128)S(1)} %collective-permute-done.12.rest_3_, ...), custom_call_target="tpu_custom_call" | custom-call | tf_op jit(solution)/shard_map/smooth/pallas_call | solution.py:378
  68.5 0.7 convert_element_type.25
  69.2 10.1 %all-to-all-start = ((f16[16,2,24,128]{3,2,1,0:T(8,128)(2,1)}), f16[16,2,24,128]{3,2,1,0:T(8,128)(2,1)S(1)}, u32[]{:S(2)}, u32[]{:S(2)}) async-start(f16[16,2,24,128]{3,2,1,0:T(8,128)(2,1)} %bitcast.2), calls=%async_computation | async-start | bytes 393216 | tf_op jit(solution)/shard_map/all_to_all | solution.py:575
  79.3 0.5 convolution_add_fusion.normal
  79.8 3.3 %invert.1.inverse = f32[256,256]{1,0:T(8,128)S(1)} custom-call(f32[256,256]{1,0:T(8,128)S(1)} %convolution_add_fusion.normal), custom_call_target="tpu_custom_call" | custom-call | flops 2013265920 | bytes 524288 | tf_op jit(solution)/shard_map/invert/pallas_call | solution.py:431
  83.0 4.1 %all-to-all-done = f16[16,2,24,128]{3,2,1,0:T(8,128)(2,1)S(1)} async-done(((f16[16,2,24,128]{3,2,1,0:T(8,128)(2,1)}), f16[16,2,24,128]{3,2,1,0:T(8,128)(2,1)S(1)}, u32[]{:S(2)}, u32[]{:S(2)}) %all-to-all-start) | async-done | bytes 196640 | tf_op jit(solution)/shard_map/all_to_all | solution.py:575
  87.2 1.1 %series.1 = (f32[2,8,8,256]{3,2,1,0:T(8,128)}, f32[2,8,8,256]{3,2,1,0:T(8,128)}) custom-call(f32[16,2,24,128]{3,2,1,0:T(8,128)S(1)} %convert_element_type.27.got, f32[256,256]{1,0:T(8,128)S(1)} %invert.1.inverse), custom_call_target="tpu_custom_call" | custom-call | tf_op jit(solution)/shard_map/series/pallas_call | solution.py:472
  (13 shorter events, 0.2 us)
Async XLA Ops:
  3.8 18.7 %collective-permute-start = (bf16[1,2,4,1,128,128]{5,4,3,2,1,0:T(8,128)(2,1)}, bf16[1,2,4,1,128,128]{5,4,3,2,1,0:T(8,128)(2,1)S(1)}, u32[]{:S(2)}, u32[]{:S(2)}) collective-permute-start(bf16[1,2,4,1,128,128]{5,4,3,2,1,0:T(8,128)(2,1)} %get-tuple-element.24), channel_id=1, source_target_pairs={{0,1},{1,0},{2,3},{3,2},{4,5},{5,4},{6,7},{7,6},{8,9},{9,8},{10,11... | collective-permute-start | bytes 786440 | tf_op jit(solution)/shard_map/ppermute | solution.py:551
  9.0 20.8 %collective-permute-start.1 = (bf16[1,2,4,1,128,128]{5,4,3,2,1,0:T(8,128)(2,1)}, bf16[1,2,4,1,128,128]{5,4,3,2,1,0:T(8,128)(2,1)S(1)}, u32[]{:S(2)}, u32[]{:S(2)}) collective-permute-start(bf16[1,2,4,1,128,128]{5,4,3,2,1,0:T(8,128)(2,1)} %get-tuple-element.26), channel_id=1, source_target_pairs={{0,1},{1,0},{2,3},{3,2},{4,5},{5,4},{6,7},{7,6},{8,9},{9,8},{10,11... | collective-permute-start | bytes 786440 | tf_op jit(solution)/shard_map/ppermute | solution.py:551
  9.0 13.2 %copy-start.4 = (s32[1000,2]{0,1:T(2,128)S(1)}, s32[1000,2]{0,1:T(2,128)}, u32[]{:S(2)}) copy-start(s32[1000,2]{0,1:T(2,128)} %param.7) | copy-start | bytes 24004
  9.0 13.5 %copy-start.2 = (bf16[1,2,4,1,128,128]{5,4,3,2,1,0:T(8,128)(2,1)S(1)}, bf16[1,2,4,1,128,128]{5,4,3,2,1,0:T(8,128)(2,1)}, u32[]{:S(2)}) copy-start(bf16[1,2,4,1,128,128]{5,4,3,2,1,0:T(8,128)(2,1)} %get-tuple-element.23.rest_0_.refs_0_) | copy-start | bytes 786436
  9.0 20.8 %copy-start.3 = (bf16[1,2,4,1,128,128]{5,4,3,2,1,0:T(8,128)(2,1)S(1)}, bf16[1,2,4,1,128,128]{5,4,3,2,1,0:T(8,128)(2,1)}, u32[]{:S(2)}) copy-start(bf16[1,2,4,1,128,128]{5,4,3,2,1,0:T(8,128)(2,1)} %get-tuple-element.25.rest_0_.refs_2_) | copy-start | bytes 786436
  14.2 18.0 %copy-start = (bf16[3,2,4,1,128,128]{5,4,3,2,1,0:T(8,128)(2,1)S(1)}, bf16[3,2,4,1,128,128]{5,4,3,2,1,0:T(8,128)(2,1)}, u32[]{:S(2)}) copy-start(bf16[3,2,4,1,128,128]{5,4,3,2,1,0:T(8,128)(2,1)} %get-tuple-element.27.rest_0_.refs_4_) | copy-start | bytes 2359300
  14.2 18.0 %collective-permute-start.2 = (bf16[3,2,2,1,128,128]{5,4,3,2,1,0:T(8,128)(2,1)}, bf16[3,2,2,1,128,128]{5,4,3,2,1,0:T(8,128)(2,1)S(1)}, u32[]{:S(2)}, u32[]{:S(2)}) collective-permute-start(bf16[3,2,2,1,128,128]{5,4,3,2,1,0:T(8,128)(2,1)} %get-tuple-element.28), channel_id=1, source_target_pairs={{0,1},{1,0},{2,3},{3,2},{4,5},{5,4},{6,7},{7,6},{8,9},{9,8},{10,11... | collective-permute-start | bytes 1179656 | tf_op jit(solution)/shard_map/ppermute | solution.py:551
  20.7 27.8 %copy-start.1 = (bf16[3,2,4,1,128,128]{5,4,3,2,1,0:T(8,128)(2,1)S(1)}, bf16[3,2,4,1,128,128]{5,4,3,2,1,0:T(8,128)(2,1)}, u32[]{:S(2)}) copy-start(bf16[3,2,4,1,128,128]{5,4,3,2,1,0:T(8,128)(2,1)} %get-tuple-element.29.refs_6_) | copy-start | bytes 2359300
  20.7 24.7 %collective-permute-start.7 = (bf16[3,2,1,1,128,128]{5,4,3,2,1,0:T(8,128)(2,1)}, bf16[3,2,1,1,128,128]{5,4,3,2,1,0:T(8,128)(2,1)}, u32[]{:S(2)}, u32[]{:S(2)}) collective-permute-start(bf16[3,2,1,1,128,128]{5,4,3,2,1,0:T(8,128)(2,1)} %get-tuple-element.36), channel_id=1, source_target_pairs={{0,1},{1,0},{2,3},{3,2},{4,5},{5,4},{6,7},{7,6},{8,9},{9,8},{10,11... | collective-permute-start | bytes 589832 | tf_op jit(solution)/shard_map/ppermute | solution.py:551
  20.9 17.8 %collective-permute-start.8 = (bf16[3,2,2,1,128,128]{5,4,3,2,1,0:T(8,128)(2,1)}, bf16[3,2,2,1,128,128]{5,4,3,2,1,0:T(8,128)(2,1)S(1)}, u32[]{:S(2)}, u32[]{:S(2)}) collective-permute-start(bf16[3,2,2,1,128,128]{5,4,3,2,1,0:T(8,128)(2,1)} %get-tuple-element.37), channel_id=1, source_target_pairs={{0,1},{1,0},{2,3},{3,2},{4,5},{5,4},{6,7},{7,6},{8,9},{9,8},{10,11... | collective-permute-start | bytes 1179656 | tf_op jit(solution)/shard_map/ppermute | solution.py:551
  22.6 24.1 %collective-permute-start.4 = (bf16[1,2,4,1,128,128]{5,4,3,2,1,0:T(8,128)(2,1)S(1)}, bf16[1,2,4,1,128,128]{5,4,3,2,1,0:T(8,128)(2,1)S(1)}, u32[]{:S(2)}, u32[]{:S(2)}) collective-permute-start(bf16[1,2,4,1,128,128]{5,4,3,2,1,0:T(8,128)(2,1)S(1)} %broadcast_select_fusion.1), channel_id=1, source_target_pairs={{2,0},{4,2},{6,4},{8,6},{10,8},{12,10},{14,12},{16,14},{18,16},{20... | collective-permute-start | bytes 786440 | tf_op jit(solution)/shard_map/ppermute | solution.py:542
  29.8 17.1 %collective-permute-start.5 = (bf16[1,2,4,1,128,128]{5,4,3,2,1,0:T(8,128)(2,1)S(1)}, bf16[1,2,4,1,128,128]{5,4,3,2,1,0:T(8,128)(2,1)S(1)}, u32[]{:S(2)}, u32[]{:S(2)}) collective-permute-start(bf16[1,2,4,1,128,128]{5,4,3,2,1,0:T(8,128)(2,1)S(1)} %broadcast_select_fusion), channel_id=1, source_target_pairs={{2,0},{4,2},{6,4},{8,6},{10,8},{12,10},{14,12},{16,14},{18,16},{20... | collective-permute-start | bytes 786440 | tf_op jit(solution)/shard_map/ppermute | solution.py:542
  32.3 16.2 %collective-permute-start.6 = (bf16[3,2,2,1,128,128]{5,4,3,2,1,0:T(8,128)(2,1)S(1)}, bf16[3,2,2,1,128,128]{5,4,3,2,1,0:T(8,128)(2,1)S(1)}, u32[]{:S(2)}, u32[]{:S(2)}) collective-permute-start(bf16[3,2,2,1,128,128]{5,4,3,2,1,0:T(8,128)(2,1)S(1)} %slice_select_fusion.1), channel_id=1, source_target_pairs={{2,0},{4,2},{6,4},{8,6},{10,8},{12,10},{14,12},{16,14},{18,16},{20... | collective-permute-start | bytes 1179656 | tf_op jit(solution)/shard_map/ppermute | solution.py:542
  38.8 18.4 %collective-permute-start.10 = (bf16[3,2,2,1,128,128]{5,4,3,2,1,0:T(8,128)(2,1)S(1)}, bf16[3,2,2,1,128,128]{5,4,3,2,1,0:T(8,128)(2,1)S(1)}, u32[]{:S(2)}, u32[]{:S(2)}) collective-permute-start(bf16[3,2,2,1,128,128]{5,4,3,2,1,0:T(8,128)(2,1)S(1)} %slice_select_fusion), channel_id=1, source_target_pairs={{2,0},{4,2},{6,4},{8,6},{10,8},{12,10},{14,12},{16,14},{18,16},{20... | collective-permute-start | bytes 1179656 | tf_op jit(solution)/shard_map/ppermute | solution.py:542
  45.4 7.2 %collective-permute-start.3 = (bf16[3,2,1,1,128,128]{5,4,3,2,1,0:T(8,128)(2,1)}, bf16[3,2,1,1,128,128]{5,4,3,2,1,0:T(8,128)(2,1)S(1)}, u32[]{:S(2)}, u32[]{:S(2)}) collective-permute-start(bf16[3,2,1,1,128,128]{5,4,3,2,1,0:T(8,128)(2,1)} %get-tuple-element.30), channel_id=1, source_target_pairs={{0,1},{1,0},{2,3},{3,2},{4,5},{5,4},{6,7},{7,6},{8,9},{9,8},{10,11... | collective-permute-start | bytes 589832 | tf_op jit(solution)/shard_map/ppermute | solution.py:551
  46.7 10.5 %collective-permute-start.9 = (bf16[3,2,1,1,128,128]{5,4,3,2,1,0:T(8,128)(2,1)}, bf16[3,2,1,1,128,128]{5,4,3,2,1,0:T(8,128)(2,1)S(1)}, u32[]{:S(2)}, u32[]{:S(2)}) collective-permute-start(bf16[3,2,1,1,128,128]{5,4,3,2,1,0:T(8,128)(2,1)} %get-tuple-element.38), channel_id=1, source_target_pairs={{0,1},{1,0},{2,3},{3,2},{4,5},{5,4},{6,7},{7,6},{8,9},{9,8},{10,11... | collective-permute-start | bytes 589832 | tf_op jit(solution)/shard_map/ppermute | solution.py:551
  47.0 13.9 %collective-permute-start.11 = (bf16[3,2,1,1,128,128]{5,4,3,2,1,0:T(8,128)(2,1)}, bf16[3,2,1,1,128,128]{5,4,3,2,1,0:T(8,128)(2,1)S(1)}, u32[]{:S(2)}, u32[]{:S(2)}) collective-permute-start(bf16[3,2,1,1,128,128]{5,4,3,2,1,0:T(8,128)(2,1)} %get-tuple-element.41), channel_id=1, source_target_pairs={{0,1},{1,0},{2,3},{3,2},{4,5},{5,4},{6,7},{7,6},{8,9},{9,8},{10,11... | collective-permute-start | bytes 589832 | tf_op jit(solution)/shard_map/ppermute | solution.py:551
  56.0 11.2 %collective-permute-start.12 = (f32[2,4,24,128]{3,2,1,0:T(8,128)S(1)}, f32[2,4,24,128]{3,2,1,0:T(8,128)S(1)}, u32[]{:S(2)}, u32[]{:S(2)}) collective-permute-start(f32[2,4,24,128]{3,2,1,0:T(8,128)S(1)} %shard_map.64.refs_11_.rest_0_), channel_id=1, source_target_pairs={{0,1},{1,0},{2,3},{3,2},{4,5},{5,4},{6,7},{7,6},{8,9},{9,8},{10,11... | collective-permute-start | bytes 294920 | tf_op jit(solution)/shard_map/ppermute | solution.py:563
  60.5 4.9 %collective-permute-start.13 = (f32[1,4,24,128]{3,2,1,0:T(8,128)S(1)}, f32[1,4,24,128]{3,2,1,0:T(8,128)S(1)}, u32[]{:S(2)}, u32[]{:S(2)}) collective-permute-start(f32[1,4,24,128]{3,2,1,0:T(8,128)S(1)} %shard_map.65.refs_11_.rest_1_), channel_id=1, source_target_pairs={{0,1},{1,0},{2,3},{3,2},{4,5},{5,4},{6,7},{7,6},{8,9},{9,8},{10,11... | collective-permute-start | bytes 147464 | tf_op jit(solution)/shard_map/ppermute | solution.py:563
  64.1 3.0 %collective-permute-start.14 = (f32[1,4,24,128]{3,2,1,0:T(8,128)S(1)}, f32[1,4,24,128]{3,2,1,0:T(8,128)S(1)}, u32[]{:S(2)}, u32[]{:S(2)}) collective-permute-start(f32[1,4,24,128]{3,2,1,0:T(8,128)S(1)} %shard_map.66.rest_2_), channel_id=1, source_target_pairs={{0,1},{1,0},{2,3},{3,2},{4,5},{5,4},{6,7},{7,6},{8,9},{9,8},{10,11... | collective-permute-start | bytes 147464 | tf_op jit(solution)/shard_map/ppermute | solution.py:563
  69.2 17.9 %all-to-all-start = ((f16[16,2,24,128]{3,2,1,0:T(8,128)(2,1)}), f16[16,2,24,128]{3,2,1,0:T(8,128)(2,1)S(1)}, u32[]{:S(2)}, u32[]{:S(2)}) async-start(f16[16,2,24,128]{3,2,1,0:T(8,128)(2,1)} %bitcast.2), calls=%async_computation | async-start | bytes 393216 | tf_op jit(solution)/shard_map/all_to_all | solution.py:575

commit v6 on v5

--- a/solution.py
+++ b/solution.py
@@ -64,8 +64,8 @@
             shifted[pl.ds(t * high + MAXA + lines, MAXA), :] = blank
         source = lax.broadcasted_iota(jnp.int32, (span, span), 0)
         target = lax.broadcasted_iota(jnp.int32, (1, span), 1)
-        column, few = target & 7, (target >> 3) & 3
-        stripe, many = (target >> 5) & 3, target >> 7
+        column, few = target & 7, ((target >> 6) & 1) * 2 + ((target >> 3) & 1)
+        stripe, many = (target >> 4) & 3, target >> 7
         wanted = stripe * LANES + column * LR + many * 4 + few
         spread[...] = jnp.where(source == wanted, 1.0, 0.0).astype(jnp.bfloat16)
 
@@ -174,12 +174,6 @@
     )(az, rg, images, *earlier)
 
 
-def merge(x, y, bit, distance):
-    return jnp.where(
-        bit, x + pltpu.roll(x, LANES - distance, 1), y + pltpu.roll(y, distance, 1)
-    )
-
-
 def pair_kernel(own, starts, reached, mask, *refs):
     count = len(starts)
     parts, following = refs[: 2 * count], refs[2 * count : 2 * count + len(reached)]
@@ -215,22 +209,19 @@
 
     lax.fori_loop(0, block, multiply, 0)
     lane = lax.broadcasted_iota(jnp.int32, (8, LANES), 1)
-    real = lane & 8 == 0
+    real = lane < LANES // 2
     place = lane >> 4
 
     def slot(d, g):
         at = (d * MAXB + g) * 16
-        value = merge(
-            products[pl.ds(pl.multiple_of(at, 8), 8), :],
-            products[pl.ds(pl.multiple_of(at + 8, 8), 8), :],
-            real,
-            8,
-        )
-        value = value + pltpu.roll(value, LANES - 16, 1)
+        re = products[pl.ds(pl.multiple_of(at, 8), 8), :]
+        im = products[pl.ds(pl.multiple_of(at + 8, 8), 8), :]
+        value = jnp.where(real, re, im) + pltpu.roll(jnp.where(real, im, re), LANES // 2, 1)
+        value = value + pltpu.roll(value, LANES - 8, 1)
         value = (value * (1.0 / (LA * LR))).astype(jnp.bfloat16).astype(jnp.float32)
         return value * mask[g, date0 + d].astype(jnp.float32)
 
-    step = 4 if block % 4 == 0 else 1
+    step = next(k for k in (16, 8, 4, 1) if block % k == 0)
 
     def gather(i, carry):
         totals = [None] * (step + MAXB)
@@ -251,16 +242,17 @@
     lax.fori_loop(0, block // step, gather, 0)
     for group in range(right.shape[2] // 8):
         rows = [sums[pl.ds(64 * group + u, 8, stride=8), :] for u in range(8)]
+        rows = [jnp.where(lane & 8 == 0, v, pltpu.roll(v, LANES // 2 + 8, 1)) for v in rows]
         turned = []
         for s in range(8):
             joined = rows[s]
             for z in range(1, STRIPES):
-                joined = jnp.where(place == 2 * z, rows[(s + 2 * z) % 8], joined)
+                joined = jnp.where(place == z, rows[(s + z) % 8], joined)
             turned.append(pltpu.roll(joined, 16 * s, 1) if s else joined)
         for z in range(STRIPES):
             out = turned[0]
             for s in range(1, 8):
-                out = jnp.where(place == (2 * z + s) % 8, turned[s], out)
+                out = jnp.where(place == (z + s) % 8, turned[s], out)
             right[right.shape[0] - 1, z, pl.ds(8 * group, 8), :] = out
     if right.shape[0] > 1:
         right[0] = refs[-5][0]

time: 89.1 us -> 87.8 us (0.985)
  Pallas kernels: 36.3 us -> 35 us
  starting transfers between devices: 39.2 us -> 38.3 us
  waiting for transfers between devices: 10.2 us -> 11.1 us
    pallas_call x4, Pallas kernels: 14 us -> 12.7 us  [pair_sums(): pl.pallas_call(partial(pair_kernel, own, [p[0] for p in pieces], [f[0] fo...]
    all_to_all x1, starting transfers between devices: 10.1 us -> 9.11 us  [local(): lax.all_to_all(outgoing, ('pairs', 'z'), split_axis=0, concat_axis=0, til...]
  transfers between devices with their start and end apart: 16 -> 16, of which waited for: 4 -> 5; matrix products, arithmetic and copies ran while one was open for 1% -> 1% of each run, Pallas kernels for 35% -> 34%
where the time goes in v6:
time: 87.8 us; the launch traced here: 87 us
  starting transfers between devices  38.3 us (44%)
  Pallas kernels  35 us (40%)
  waiting for transfers between devices  11.1 us (13%)
  other arithmetic  1.02 us (1%)
    ppermute x4, starting transfers between devices, send_back(): going.append(lax.ppermute(v, ('pairs', 'z'), route))  18.5 us
    pallas_call x4, Pallas kernels, resample(): pl.pallas_call(partial(resample_kernel, images.shape[0], first, parts), g...  16.6 us
    pallas_call x4, Pallas kernels, pair_sums(): pl.pallas_call(partial(pair_kernel, own, [p[0] for p in pieces], [f[0] fo...  12.7 us
    all_to_all x1, starting transfers between devices, local(): lax.all_to_all(outgoing, ('pairs', 'z'), split_axis=0, concat_axis=0, til...  9.11 us
    ppermute x8, starting transfers between devices, local(): received.append(lax.ppermute(v, 'x', swap))  7.73 us
    ppermute x8, waiting for transfers between devices, local(): received.append(lax.ppermute(v, 'x', swap))  4.32 us
    all_to_all x1, waiting for transfers between devices, local(): lax.all_to_all(outgoing, ('pairs', 'z'), split_axis=0, concat_axis=0, til...  4.09 us
    pallas_call x1, Pallas kernels, invert(): pl.pallas_call(invert_kernel, in_specs=[vmem()], out_specs=vmem(), out_sh...  3.26 us
  transfers between devices with their start and end apart: 16, of which 5 were waited for; matrix products, arithmetic and copies ran while one was open for 1% of the time, Pallas kernels for 34%

profile of v6, /device:TPU:1, one launch (start us, length us, event | category | flops | bytes accessed | tf_op | source)
XLA Modules:
  0.0 87.0 jit_solution(16214293984410758118)
XLA Ops:
  0.6 3.2 %shard_map.59 = (bf16[1,2,4,1,128,128]{5,4,3,2,1,0:T(8,128)(2,1)}, bf16[1,2,4,1,128,128]{5,4,3,2,1,0:T(8,128)(2,1)}) custom-call(s32[256]{0:T(256)} %az.7, s32[256]{0:T(256)} %rg.7, bf16[8,2,128,1024]{3,2,1,0:T(8,128)(2,1)} %img.7), custom_call_target="tpu_custom_call" | custom-call | flops 524288 | bytes 1048576 | tf_op jit(solution)/shard_map/pallas_call | solution.py:153
  3.8 2.0 %collective-permute-start = (bf16[1,2,4,1,128,128]{5,4,3,2,1,0:T(8,128)(2,1)}, bf16[1,2,4,1,128,128]{5,4,3,2,1,0:T(8,128)(2,1)S(1)}, u32[]{:S(2)}, u32[]{:S(2)}) collective-permute-start(bf16[1,2,4,1,128,128]{5,4,3,2,1,0:T(8,128)(2,1)} %get-tuple-element.24), channel_id=1, source_target_pairs={{0,1},{1,0},{2,3},{3,2},{4,5},{5,4},{6,7},{7,6},{8,9},{9,8},{10,11... | collective-permute-start | bytes 786440 | tf_op jit(solution)/shard_map/ppermute | solution.py:543
  5.8 3.2 %shard_map.60 = (bf16[1,2,4,1,128,128]{5,4,3,2,1,0:T(8,128)(2,1)}, bf16[1,2,4,1,128,128]{5,4,3,2,1,0:T(8,128)(2,1)}) custom-call(s32[256]{0:T(256)} %az.7, s32[256]{0:T(256)} %rg.7, bf16[8,2,128,1024]{3,2,1,0:T(8,128)(2,1)} %img.7, bf16[1,2,4,1,128,128]{5,4,3,2,1,0:T(8,128)(2,1)} %get-tuple-element.23.rest_0_.refs_0_), custom_call_target="tpu_custom_call" | custom-call | flops 524288 | bytes 1048576 | tf_op jit(solution)/shard_map/pallas_call | solution.py:153
  9.0 0.0 collective-permute-start.1
  9.0 0.0 copy-start.4
  9.0 0.0 copy-start.2
  9.0 0.0 copy-start.3
  9.0 5.2 %shard_map.61 = (bf16[3,2,4,1,128,128]{5,4,3,2,1,0:T(8,128)(2,1)}, bf16[3,2,2,1,128,128]{5,4,3,2,1,0:T(8,128)(2,1)}, bf16[3,2,2,1,128,128]{5,4,3,2,1,0:T(8,128)(2,1)}) custom-call(s32[256]{0:T(256)} %az.7, s32[256]{0:T(256)} %rg.7, bf16[8,2,128,1024]{3,2,1,0:T(8,128)(2,1)} %img.7, bf16[1,2,4,1,128,128]{5,4,3,2,1,0:T(8,128)(2,1)} %get-tuple-element.25.rest_0_.refs_2_), custom_call_target="tpu_custom_call" | custom-call | flops 1572864 | bytes 3145728 | tf_op jit(solution)/shard_map/pallas_call | solution.py:153
  14.2 0.0 copy-start
  14.2 1.4 %collective-permute-start.2 = (bf16[3,2,2,1,128,128]{5,4,3,2,1,0:T(8,128)(2,1)}, bf16[3,2,2,1,128,128]{5,4,3,2,1,0:T(8,128)(2,1)S(1)}, u32[]{:S(2)}, u32[]{:S(2)}) collective-permute-start(bf16[3,2,2,1,128,128]{5,4,3,2,1,0:T(8,128)(2,1)} %get-tuple-element.28), channel_id=1, source_target_pairs={{0,1},{1,0},{2,3},{3,2},{4,5},{5,4},{6,7},{7,6},{8,9},{9,8},{10,11... | collective-permute-start | bytes 1179656 | tf_op jit(solution)/shard_map/ppermute | solution.py:543
  15.7 5.0 %shard_map.62 = (bf16[3,2,4,1,128,128]{5,4,3,2,1,0:T(8,128)(2,1)}, bf16[3,2,1,1,128,128]{5,4,3,2,1,0:T(8,128)(2,1)}, bf16[3,2,1,1,128,128]{5,4,3,2,1,0:T(8,128)(...) custom-call(s32[256]{0:T(256)} %az.7, s32[256]{0:T(256)} %rg.7, ...), custom_call_target="tpu_custom_call" | custom-call | flops 1572864 | bytes 3145728 | tf_op jit(solution)/shard_map/pallas_call | solution.py:153
  20.7 0.0 copy-start.1
  20.7 0.2 collective-permute-start.7
  20.9 1.3 %collective-permute-start.8 = (bf16[3,2,2,1,128,128]{5,4,3,2,1,0:T(8,128)(2,1)}, bf16[3,2,2,1,128,128]{5,4,3,2,1,0:T(8,128)(2,1)S(1)}, u32[]{:S(2)}, u32[]{:S(2)}) collective-permute-start(bf16[3,2,2,1,128,128]{5,4,3,2,1,0:T(8,128)(2,1)} %get-tuple-element.37), channel_id=1, source_target_pairs={{0,1},{1,0},{2,3},{3,2},{4,5},{5,4},{6,7},{7,6},{8,9},{9,8},{10,11... | collective-permute-start | bytes 1179656 | tf_op jit(solution)/shard_map/ppermute | solution.py:543
  22.2 0.0 copy-done.4
  22.2 0.3 convolution_convert_fusion.mask
  22.5 0.0 collective-permute-done.refs_1_
  22.6 0.0 copy-done.2
  22.6 7.2 %collective-permute-start.4 = (bf16[1,2,4,1,128,128]{5,4,3,2,1,0:T(8,128)(2,1)S(1)}, bf16[1,2,4,1,128,128]{5,4,3,2,1,0:T(8,128)(2,1)S(1)}, u32[]{:S(2)}, u32[]{:S(2)}) collective-permute-start(bf16[1,2,4,1,128,128]{5,4,3,2,1,0:T(8,128)(2,1)S(1)} %broadcast_select_fusion.1), channel_id=1, source_target_pairs={{2,0},{4,2},{6,4},{8,6},{10,8},{12,10},{14,12},{16,14},{18,16},{20... | collective-permute-start | bytes 786440 | tf_op jit(solution)/shard_map/ppermute | solution.py:534
  29.8 0.0 collective-permute-done.1.refs_3_
  29.8 0.0 copy-done.3
  29.8 2.4 %collective-permute-start.5 = (bf16[1,2,4,1,128,128]{5,4,3,2,1,0:T(8,128)(2,1)S(1)}, bf16[1,2,4,1,128,128]{5,4,3,2,1,0:T(8,128)(2,1)S(1)}, u32[]{:S(2)}, u32[]{:S(2)}) collective-permute-start(bf16[1,2,4,1,128,128]{5,4,3,2,1,0:T(8,128)(2,1)S(1)} %broadcast_select_fusion), channel_id=1, source_target_pairs={{2,0},{4,2},{6,4},{8,6},{10,8},{12,10},{14,12},{16,14},{18,16},{20... | collective-permute-start | bytes 786440 | tf_op jit(solution)/shard_map/ppermute | solution.py:534
  32.2 0.0 collective-permute-done.2.refs_5_
  32.2 0.0 copy-done
  32.3 2.4 %collective-permute-start.6 = (bf16[3,2,2,1,128,128]{5,4,3,2,1,0:T(8,128)(2,1)S(1)}, bf16[3,2,2,1,128,128]{5,4,3,2,1,0:T(8,128)(2,1)S(1)}, u32[]{:S(2)}, u32[]{:S(2)}) collective-permute-start(bf16[3,2,2,1,128,128]{5,4,3,2,1,0:T(8,128)(2,1)S(1)} %slice_select_fusion.1), channel_id=1, source_target_pairs={{2,0},{4,2},{6,4},{8,6},{10,8},{12,10},{14,12},{16,14},{18,16},{20... | collective-permute-start | bytes 1179656 | tf_op jit(solution)/shard_map/ppermute | solution.py:534
  34.7 4.1 %collective-permute-done.8.refs_5_ = bf16[3,2,2,1,128,128]{5,4,3,2,1,0:T(8,128)(2,1)S(1)} collective-permute-done((bf16[3,2,2,1,128,128]{5,4,3,2,1,0:T(8,128)(2,1)}, bf16[3,2,2,1,128,128]{5,4,3,2,1,0:T(8,128)(2,1)S(1)}, u32[]{:S(2)}, u32[]{:S(2)}) %collective-permute-start.8) | collective-permute-done | bytes 393248 | tf_op jit(solution)/shard_map/ppermute | solution.py:543
  38.8 6.6 %collective-permute-start.10 = (bf16[3,2,2,1,128,128]{5,4,3,2,1,0:T(8,128)(2,1)S(1)}, bf16[3,2,2,1,128,128]{5,4,3,2,1,0:T(8,128)(2,1)S(1)}, u32[]{:S(2)}, u32[]{:S(2)}) collective-permute-start(bf16[3,2,2,1,128,128]{5,4,3,2,1,0:T(8,128)(2,1)S(1)} %slice_select_fusion), channel_id=1, source_target_pairs={{2,0},{4,2},{6,4},{8,6},{10,8},{12,10},{14,12},{16,14},{18,16},{20... | collective-permute-start | bytes 1179656 | tf_op jit(solution)/shard_map/ppermute | solution.py:534
  45.4 0.0 collective-permute-done.7.refs_7_
  45.4 1.3 %collective-permute-start.3 = (bf16[3,2,1,1,128,128]{5,4,3,2,1,0:T(8,128)(2,1)}, bf16[3,2,1,1,128,128]{5,4,3,2,1,0:T(8,128)(2,1)S(1)}, u32[]{:S(2)}, u32[]{:S(2)}) collective-permute-start(bf16[3,2,1,1,128,128]{5,4,3,2,1,0:T(8,128)(2,1)} %get-tuple-element.30), channel_id=1, source_target_pairs={{0,1},{1,0},{2,3},{3,2},{4,5},{5,4},{6,7},{7,6},{8,9},{9,8},{10,11... | collective-permute-start | bytes 589832 | tf_op jit(solution)/shard_map/ppermute | solution.py:543
  46.7 0.0 collective-permute-done.4.refs_8_
  46.7 0.3 collective-permute-start.9
  47.0 0.0 collective-permute-done.5.refs_9_
  47.0 1.2 %collective-permute-start.11 = (bf16[3,2,1,1,128,128]{5,4,3,2,1,0:T(8,128)(2,1)}, bf16[3,2,1,1,128,128]{5,4,3,2,1,0:T(8,128)(2,1)S(1)}, u32[]{:S(2)}, u32[]{:S(2)}) collective-permute-start(bf16[3,2,1,1,128,128]{5,4,3,2,1,0:T(8,128)(2,1)} %get-tuple-element.41), channel_id=1, source_target_pairs={{0,1},{1,0},{2,3},{3,2},{4,5},{5,4},{6,7},{7,6},{8,9},{9,8},{10,11... | collective-permute-start | bytes 589832 | tf_op jit(solution)/shard_map/ppermute | solution.py:543
  48.2 0.1 select_add_fusion
  48.3 0.2 collective-permute-done.6.refs_10_
  48.5 0.0 copy-done.1
  48.5 3.9 %shard_map.63.refs_11_ = f32[1,4,24,128]{3,2,1,0:T(8,128)S(1)} custom-call(s32[5,256]{1,0:T(8,128)S(1)} %convolution_convert_fusion.mask, bf16[1,2,4,1,128,128]{5,4,3,2,1,0:T(8,128)(2,1)S(1)} %copy-done.2, bf16[1,2,4,1,128,128]{5,4,3,2,1,0:T(8,128)(2,1)S(1)} %collective-permute-done.refs_1_, bf16[1,2,4,1,128,128]{5,4,3,2,1,0:T(8,128)(2,1)S(1)} %copy-done.3, ...), custom_call_target="tpu_custom_call" | custom-call | flops 10485760 | bytes 1310720 | tf_op jit(solution)/shard_map/pallas_call | solution.py:288
  52.4 0.3 collective-permute-done.3.refs_7_
  52.6 3.0 %shard_map.64.refs_11_.rest_0_ = f32[2,4,24,128]{3,2,1,0:T(8,128)S(1)} custom-call(s32[5,256]{1,0:T(8,128)S(1)} %convolution_convert_fusion.mask, bf16[1,2,4,1,128,128]{5,4,3,2,1,0:T(8,128)(2,1)S(1)} %copy-done.2, bf16[1,2,4,1,128,128]{5,4,3,2,1,0:T(8,128)(2,1)S(1)} %collective-permute-done.refs_1_, bf16[1,2,4,1,128,128]{5,4,3,2,1,0:T(8,128)(2,1)S(1)} %copy-done.3, ...), custom_call_target="tpu_custom_call" | custom-call | flops 10485760 | bytes 1310720 | tf_op jit(solution)/shard_map/pallas_call | solution.py:288
  55.6 1.3 %collective-permute-start.12 = (f32[2,4,24,128]{3,2,1,0:T(8,128)S(1)}, f32[2,4,24,128]{3,2,1,0:T(8,128)S(1)}, u32[]{:S(2)}, u32[]{:S(2)}) collective-permute-start(f32[2,4,24,128]{3,2,1,0:T(8,128)S(1)} %shard_map.64.refs_11_.rest_0_), channel_id=1, source_target_pairs={{0,1},{1,0},{2,3},{3,2},{4,5},{5,4},{6,7},{7,6},{8,9},{9,8},{10,11... | collective-permute-start | bytes 294920 | tf_op jit(solution)/shard_map/ppermute | solution.py:555
  56.9 0.0 collective-permute-done.9.refs_7_
  56.9 0.0 collective-permute-done.10.refs_10_
  56.9 3.0 %shard_map.65.refs_11_.rest_1_ = f32[1,4,24,128]{3,2,1,0:T(8,128)S(1)} custom-call(s32[5,256]{1,0:T(8,128)S(1)} %convolution_convert_fusion.mask, bf16[1,2,4,1,128,128]{5,4,3,2,1,0:T(8,128)(2,1)S(1)} %copy-done.2, bf16[1,2,4,1,128,128]{5,4,3,2,1,0:T(8,128)(2,1)S(1)} %collective-permute-done.refs_1_, bf16[1,2,4,1,128,128]{5,4,3,2,1,0:T(8,128)(2,1)S(1)} %copy-done.3, ...), custom_call_target="tpu_custom_call" | custom-call | flops 10485760 | bytes 1310720 | tf_op jit(solution)/shard_map/pallas_call | solution.py:288
  59.8 1.0 %collective-permute-start.13 = (f32[1,4,24,128]{3,2,1,0:T(8,128)S(1)}, f32[1,4,24,128]{3,2,1,0:T(8,128)S(1)}, u32[]{:S(2)}, u32[]{:S(2)}) collective-permute-start(f32[1,4,24,128]{3,2,1,0:T(8,128)S(1)} %shard_map.65.refs_11_.rest_1_), channel_id=1, source_target_pairs={{0,1},{1,0},{2,3},{3,2},{4,5},{5,4},{6,7},{7,6},{8,9},{9,8},{10,11... | collective-permute-start | bytes 147464 | tf_op jit(solution)/shard_map/ppermute | solution.py:555
  60.9 0.0 collective-permute-done.11.refs_7_
  60.9 3.0 %shard_map.66.rest_2_ = f32[1,4,24,128]{3,2,1,0:T(8,128)S(1)} custom-call(s32[5,256]{1,0:T(8,128)S(1)} %convolution_convert_fusion.mask, bf16[1,2,4,1,128,128]{5,4,3,2,1,0:T(8,128)(2,1)S(1)} %copy-done.2, bf16[1,2,4,1,128,128]{5,4,3,2,1,0:T(8,128)(2,1)S(1)} %collective-permute-done.refs_1_, bf16[1,2,4,1,128,128]{5,4,3,2,1,0:T(8,128)(2,1)S(1)} %copy-done.3, ...), custom_call_target="tpu_custom_call" | custom-call | flops 10485760 | bytes 1310720 | tf_op jit(solution)/shard_map/pallas_call | solution.py:288
  63.8 0.6 collective-permute-start.14
  64.4 0.0 collective-permute-done.13.rest_4_
  64.4 2.4 %collective-permute-done.14.rest_5_ = f32[1,4,24,128]{3,2,1,0:T(8,128)S(1)} collective-permute-done((f32[1,4,24,128]{3,2,1,0:T(8,128)S(1)}, f32[1,4,24,128]{3,2,1,0:T(8,128)S(1)}, u32[]{:S(2)}, u32[]{:S(2)}) %collective-permute-start.14) | collective-permute-done | bytes 49184 | tf_op jit(solution)/shard_map/ppermute | solution.py:555
  66.8 0.0 collective-permute-done.12.rest_3_
  66.8 1.3 %smooth.1 = f32[4,4,2,24,128]{4,3,2,1,0:T(8,128)S(1)} custom-call(f32[2,4,24,128]{3,2,1,0:T(8,128)S(1)} %shard_map.64.refs_11_.rest_0_, f32[1,4,24,128]{3,2,1,0:T(8,128)S(1)} %shard_map.65.refs_11_.rest_1_, f32[1,4,24,128]{3,2,1,0:T(8,128)S(1)} %shard_map.66.rest_2_, f32[2,4,24,128]{3,2,1,0:T(8,128)S(1)} %collective-permute-done.12.rest_3_, ...), custom_call_target="tpu_custom_call" | custom-call | tf_op jit(solution)/shard_map/smooth/pallas_call | solution.py:370
  68.2 0.7 convert_element_type.25
  68.9 9.1 %all-to-all-start = ((f16[16,2,24,128]{3,2,1,0:T(8,128)(2,1)}), f16[16,2,24,128]{3,2,1,0:T(8,128)(2,1)S(1)}, u32[]{:S(2)}, u32[]{:S(2)}) async-start(f16[16,2,24,128]{3,2,1,0:T(8,128)(2,1)} %bitcast.2), calls=%async_computation | async-start | bytes 393216 | tf_op jit(solution)/shard_map/all_to_all | solution.py:567
  78.0 0.5 convolution_add_fusion.normal
  78.5 3.3 %invert.1.inverse = f32[256,256]{1,0:T(8,128)S(1)} custom-call(f32[256,256]{1,0:T(8,128)S(1)} %convolution_add_fusion.normal), custom_call_target="tpu_custom_call" | custom-call | flops 2013265920 | bytes 524288 | tf_op jit(solution)/shard_map/invert/pallas_call | solution.py:423
  81.8 4.1 %all-to-all-done = f16[16,2,24,128]{3,2,1,0:T(8,128)(2,1)S(1)} async-done(((f16[16,2,24,128]{3,2,1,0:T(8,128)(2,1)}), f16[16,2,24,128]{3,2,1,0:T(8,128)(2,1)S(1)}, u32[]{:S(2)}, u32[]{:S(2)}) %all-to-all-start) | async-done | bytes 196640 | tf_op jit(solution)/shard_map/all_to_all | solution.py:567
  85.9 1.1 %series.1 = (f32[2,8,8,256]{3,2,1,0:T(8,128)}, f32[2,8,8,256]{3,2,1,0:T(8,128)}) custom-call(f32[16,2,24,128]{3,2,1,0:T(8,128)S(1)} %convert_element_type.27.got, f32[256,256]{1,0:T(8,128)S(1)} %invert.1.inverse), custom_call_target="tpu_custom_call" | custom-call | tf_op jit(solution)/shard_map/series/pallas_call | solution.py:464
  (13 shorter events, 0.2 us)
Async XLA Ops:
  3.8 18.8 %collective-permute-start = (bf16[1,2,4,1,128,128]{5,4,3,2,1,0:T(8,128)(2,1)}, bf16[1,2,4,1,128,128]{5,4,3,2,1,0:T(8,128)(2,1)S(1)}, u32[]{:S(2)}, u32[]{:S(2)}) collective-permute-start(bf16[1,2,4,1,128,128]{5,4,3,2,1,0:T(8,128)(2,1)} %get-tuple-element.24), channel_id=1, source_target_pairs={{0,1},{1,0},{2,3},{3,2},{4,5},{5,4},{6,7},{7,6},{8,9},{9,8},{10,11... | collective-permute-start | bytes 786440 | tf_op jit(solution)/shard_map/ppermute | solution.py:543
  9.0 20.8 %collective-permute-start.1 = (bf16[1,2,4,1,128,128]{5,4,3,2,1,0:T(8,128)(2,1)}, bf16[1,2,4,1,128,128]{5,4,3,2,1,0:T(8,128)(2,1)S(1)}, u32[]{:S(2)}, u32[]{:S(2)}) collective-permute-start(bf16[1,2,4,1,128,128]{5,4,3,2,1,0:T(8,128)(2,1)} %get-tuple-element.26), channel_id=1, source_target_pairs={{0,1},{1,0},{2,3},{3,2},{4,5},{5,4},{6,7},{7,6},{8,9},{9,8},{10,11... | collective-permute-start | bytes 786440 | tf_op jit(solution)/shard_map/ppermute | solution.py:543
  9.0 13.2 %copy-start.4 = (s32[1000,2]{0,1:T(2,128)S(1)}, s32[1000,2]{0,1:T(2,128)}, u32[]{:S(2)}) copy-start(s32[1000,2]{0,1:T(2,128)} %param.7) | copy-start | bytes 24004
  9.0 13.6 %copy-start.2 = (bf16[1,2,4,1,128,128]{5,4,3,2,1,0:T(8,128)(2,1)S(1)}, bf16[1,2,4,1,128,128]{5,4,3,2,1,0:T(8,128)(2,1)}, u32[]{:S(2)}) copy-start(bf16[1,2,4,1,128,128]{5,4,3,2,1,0:T(8,128)(2,1)} %get-tuple-element.23.rest_0_.refs_0_) | copy-start | bytes 786436
  9.0 20.8 %copy-start.3 = (bf16[1,2,4,1,128,128]{5,4,3,2,1,0:T(8,128)(2,1)S(1)}, bf16[1,2,4,1,128,128]{5,4,3,2,1,0:T(8,128)(2,1)}, u32[]{:S(2)}) copy-start(bf16[1,2,4,1,128,128]{5,4,3,2,1,0:T(8,128)(2,1)} %get-tuple-element.25.rest_0_.refs_2_) | copy-start | bytes 786436
  14.2 18.0 %copy-start = (bf16[3,2,4,1,128,128]{5,4,3,2,1,0:T(8,128)(2,1)S(1)}, bf16[3,2,4,1,128,128]{5,4,3,2,1,0:T(8,128)(2,1)}, u32[]{:S(2)}) copy-start(bf16[3,2,4,1,128,128]{5,4,3,2,1,0:T(8,128)(2,1)} %get-tuple-element.27.rest_0_.refs_4_) | copy-start | bytes 2359300
  14.2 18.0 %collective-permute-start.2 = (bf16[3,2,2,1,128,128]{5,4,3,2,1,0:T(8,128)(2,1)}, bf16[3,2,2,1,128,128]{5,4,3,2,1,0:T(8,128)(2,1)S(1)}, u32[]{:S(2)}, u32[]{:S(2)}) collective-permute-start(bf16[3,2,2,1,128,128]{5,4,3,2,1,0:T(8,128)(2,1)} %get-tuple-element.28), channel_id=1, source_target_pairs={{0,1},{1,0},{2,3},{3,2},{4,5},{5,4},{6,7},{7,6},{8,9},{9,8},{10,11... | collective-permute-start | bytes 1179656 | tf_op jit(solution)/shard_map/ppermute | solution.py:543
  20.7 27.8 %copy-start.1 = (bf16[3,2,4,1,128,128]{5,4,3,2,1,0:T(8,128)(2,1)S(1)}, bf16[3,2,4,1,128,128]{5,4,3,2,1,0:T(8,128)(2,1)}, u32[]{:S(2)}) copy-start(bf16[3,2,4,1,128,128]{5,4,3,2,1,0:T(8,128)(2,1)} %get-tuple-element.29.refs_6_) | copy-start | bytes 2359300
  20.7 24.7 %collective-permute-start.7 = (bf16[3,2,1,1,128,128]{5,4,3,2,1,0:T(8,128)(2,1)}, bf16[3,2,1,1,128,128]{5,4,3,2,1,0:T(8,128)(2,1)}, u32[]{:S(2)}, u32[]{:S(2)}) collective-permute-start(bf16[3,2,1,1,128,128]{5,4,3,2,1,0:T(8,128)(2,1)} %get-tuple-element.36), channel_id=1, source_target_pairs={{0,1},{1,0},{2,3},{3,2},{4,5},{5,4},{6,7},{7,6},{8,9},{9,8},{10,11... | collective-permute-start | bytes 589832 | tf_op jit(solution)/shard_map/ppermute | solution.py:543
  20.9 17.8 %collective-permute-start.8 = (bf16[3,2,2,1,128,128]{5,4,3,2,1,0:T(8,128)(2,1)}, bf16[3,2,2,1,128,128]{5,4,3,2,1,0:T(8,128)(2,1)S(1)}, u32[]{:S(2)}, u32[]{:S(2)}) collective-permute-start(bf16[3,2,2,1,128,128]{5,4,3,2,1,0:T(8,128)(2,1)} %get-tuple-element.37), channel_id=1, source_target_pairs={{0,1},{1,0},{2,3},{3,2},{4,5},{5,4},{6,7},{7,6},{8,9},{9,8},{10,11... | collective-permute-start | bytes 1179656 | tf_op jit(solution)/shard_map/ppermute | solution.py:543
  22.6 24.1 %collective-permute-start.4 = (bf16[1,2,4,1,128,128]{5,4,3,2,1,0:T(8,128)(2,1)S(1)}, bf16[1,2,4,1,128,128]{5,4,3,2,1,0:T(8,128)(2,1)S(1)}, u32[]{:S(2)}, u32[]{:S(2)}) collective-permute-start(bf16[1,2,4,1,128,128]{5,4,3,2,1,0:T(8,128)(2,1)S(1)} %broadcast_select_fusion.1), channel_id=1, source_target_pairs={{2,0},{4,2},{6,4},{8,6},{10,8},{12,10},{14,12},{16,14},{18,16},{20... | collective-permute-start | bytes 786440 | tf_op jit(solution)/shard_map/ppermute | solution.py:534
  29.8 17.1 %collective-permute-start.5 = (bf16[1,2,4,1,128,128]{5,4,3,2,1,0:T(8,128)(2,1)S(1)}, bf16[1,2,4,1,128,128]{5,4,3,2,1,0:T(8,128)(2,1)S(1)}, u32[]{:S(2)}, u32[]{:S(2)}) collective-permute-start(bf16[1,2,4,1,128,128]{5,4,3,2,1,0:T(8,128)(2,1)S(1)} %broadcast_select_fusion), channel_id=1, source_target_pairs={{2,0},{4,2},{6,4},{8,6},{10,8},{12,10},{14,12},{16,14},{18,16},{20... | collective-permute-start | bytes 786440 | tf_op jit(solution)/shard_map/ppermute | solution.py:534
  32.3 16.2 %collective-permute-start.6 = (bf16[3,2,2,1,128,128]{5,4,3,2,1,0:T(8,128)(2,1)S(1)}, bf16[3,2,2,1,128,128]{5,4,3,2,1,0:T(8,128)(2,1)S(1)}, u32[]{:S(2)}, u32[]{:S(2)}) collective-permute-start(bf16[3,2,2,1,128,128]{5,4,3,2,1,0:T(8,128)(2,1)S(1)} %slice_select_fusion.1), channel_id=1, source_target_pairs={{2,0},{4,2},{6,4},{8,6},{10,8},{12,10},{14,12},{16,14},{18,16},{20... | collective-permute-start | bytes 1179656 | tf_op jit(solution)/shard_map/ppermute | solution.py:534
  38.8 18.1 %collective-permute-start.10 = (bf16[3,2,2,1,128,128]{5,4,3,2,1,0:T(8,128)(2,1)S(1)}, bf16[3,2,2,1,128,128]{5,4,3,2,1,0:T(8,128)(2,1)S(1)}, u32[]{:S(2)}, u32[]{:S(2)}) collective-permute-start(bf16[3,2,2,1,128,128]{5,4,3,2,1,0:T(8,128)(2,1)S(1)} %slice_select_fusion), channel_id=1, source_target_pairs={{2,0},{4,2},{6,4},{8,6},{10,8},{12,10},{14,12},{16,14},{18,16},{20... | collective-permute-start | bytes 1179656 | tf_op jit(solution)/shard_map/ppermute | solution.py:534
  45.4 7.2 %collective-permute-start.3 = (bf16[3,2,1,1,128,128]{5,4,3,2,1,0:T(8,128)(2,1)}, bf16[3,2,1,1,128,128]{5,4,3,2,1,0:T(8,128)(2,1)S(1)}, u32[]{:S(2)}, u32[]{:S(2)}) collective-permute-start(bf16[3,2,1,1,128,128]{5,4,3,2,1,0:T(8,128)(2,1)} %get-tuple-element.30), channel_id=1, source_target_pairs={{0,1},{1,0},{2,3},{3,2},{4,5},{5,4},{6,7},{7,6},{8,9},{9,8},{10,11... | collective-permute-start | bytes 589832 | tf_op jit(solution)/shard_map/ppermute | solution.py:543
  46.7 10.2 %collective-permute-start.9 = (bf16[3,2,1,1,128,128]{5,4,3,2,1,0:T(8,128)(2,1)}, bf16[3,2,1,1,128,128]{5,4,3,2,1,0:T(8,128)(2,1)S(1)}, u32[]{:S(2)}, u32[]{:S(2)}) collective-permute-start(bf16[3,2,1,1,128,128]{5,4,3,2,1,0:T(8,128)(2,1)} %get-tuple-element.38), channel_id=1, source_target_pairs={{0,1},{1,0},{2,3},{3,2},{4,5},{5,4},{6,7},{7,6},{8,9},{9,8},{10,11... | collective-permute-start | bytes 589832 | tf_op jit(solution)/shard_map/ppermute | solution.py:543
  47.0 13.9 %collective-permute-start.11 = (bf16[3,2,1,1,128,128]{5,4,3,2,1,0:T(8,128)(2,1)}, bf16[3,2,1,1,128,128]{5,4,3,2,1,0:T(8,128)(2,1)S(1)}, u32[]{:S(2)}, u32[]{:S(2)}) collective-permute-start(bf16[3,2,1,1,128,128]{5,4,3,2,1,0:T(8,128)(2,1)} %get-tuple-element.41), channel_id=1, source_target_pairs={{0,1},{1,0},{2,3},{3,2},{4,5},{5,4},{6,7},{7,6},{8,9},{9,8},{10,11... | collective-permute-start | bytes 589832 | tf_op jit(solution)/shard_map/ppermute | solution.py:543
  55.6 11.3 %collective-permute-start.12 = (f32[2,4,24,128]{3,2,1,0:T(8,128)S(1)}, f32[2,4,24,128]{3,2,1,0:T(8,128)S(1)}, u32[]{:S(2)}, u32[]{:S(2)}) collective-permute-start(f32[2,4,24,128]{3,2,1,0:T(8,128)S(1)} %shard_map.64.refs_11_.rest_0_), channel_id=1, source_target_pairs={{0,1},{1,0},{2,3},{3,2},{4,5},{5,4},{6,7},{7,6},{8,9},{9,8},{10,11... | collective-permute-start | bytes 294920 | tf_op jit(solution)/shard_map/ppermute | solution.py:555
  59.8 4.6 %collective-permute-start.13 = (f32[1,4,24,128]{3,2,1,0:T(8,128)S(1)}, f32[1,4,24,128]{3,2,1,0:T(8,128)S(1)}, u32[]{:S(2)}, u32[]{:S(2)}) collective-permute-start(f32[1,4,24,128]{3,2,1,0:T(8,128)S(1)} %shard_map.65.refs_11_.rest_1_), channel_id=1, source_target_pairs={{0,1},{1,0},{2,3},{3,2},{4,5},{5,4},{6,7},{7,6},{8,9},{9,8},{10,11... | collective-permute-start | bytes 147464 | tf_op jit(solution)/shard_map/ppermute | solution.py:555
  63.8 3.0 %collective-permute-start.14 = (f32[1,4,24,128]{3,2,1,0:T(8,128)S(1)}, f32[1,4,24,128]{3,2,1,0:T(8,128)S(1)}, u32[]{:S(2)}, u32[]{:S(2)}) collective-permute-start(f32[1,4,24,128]{3,2,1,0:T(8,128)S(1)} %shard_map.66.rest_2_), channel_id=1, source_target_pairs={{0,1},{1,0},{2,3},{3,2},{4,5},{5,4},{6,7},{7,6},{8,9},{9,8},{10,11... | collective-permute-start | bytes 147464 | tf_op jit(solution)/shard_map/ppermute | solution.py:555
  68.9 17.0 %all-to-all-start = ((f16[16,2,24,128]{3,2,1,0:T(8,128)(2,1)}), f16[16,2,24,128]{3,2,1,0:T(8,128)(2,1)S(1)}, u32[]{:S(2)}, u32[]{:S(2)}) async-start(f16[16,2,24,128]{3,2,1,0:T(8,128)(2,1)} %bitcast.2), calls=%async_computation | async-start | bytes 393216 | tf_op jit(solution)/shard_map/all_to_all | solution.py:567

commit v7 on v6

--- a/solution.py
+++ b/solution.py
@@ -276,7 +276,7 @@
         got = received[chunk * len(received) // chunks]
         operands.append(got)
         specs.append(window(got, len(received)))
-    joined = chunk == 1
+    joined = chunk % 2 == 1
     if earlier is not None:
         operands.append(earlier)
         specs.append(
@@ -411,7 +411,7 @@
     while error > 1e-8:
         scale = 2.0 / (2.0 - error * error)
         residual = unit - times_normal(guess)
-        precision = lax.Precision.HIGHEST if error < 0.1 else lax.Precision.DEFAULT
+        precision = lax.Precision.HIGHEST if error < 1e-3 else lax.Precision.DEFAULT
         change = jnp.dot(guess, residual, precision=precision, preferred_element_type=jnp.float32)
         guess = scale * (guess + change)
         error = error * error / (2.0 - error * error)
@@ -551,7 +551,7 @@
     for c in range(rows):
         earlier = sums[-1] if sums else None
         sums.append(pair_sums(mask, pieces, following, earlier, c, rows, own, deep))
-    sums = sums[1:]
+    sums = sums[1::2]
     partner = [lax.ppermute(s, "x", swap) for s in sums]
 
     lane = jnp.arange(LANES, dtype=jnp.int32)

time: 87.8 us -> 86.7 us (0.987)
  starting transfers between devices: 38.3 us -> 36.2 us
  waiting for transfers between devices: 11.1 us -> 12.3 us
    all_to_all x1, starting transfers between devices: 9.11 us -> 7.2 us  [local(): lax.all_to_all(outgoing, ('pairs', 'z'), split_axis=0, concat_axis=0, til...]
    ppermute x8, waiting for transfers between devices: 4.32 us -> 5.77 us  [local(): received.append(lax.ppermute(v, 'x', swap))]
    ppermute x3 -> x2, waiting for transfers between devices: 2.45 us -> 2 us  [local(): partner = [lax.ppermute(s, 'x', swap) for s in sums]]
    ppermute x3 -> x2, starting transfers between devices: 2.87 us -> 2.8 us  [local(): partner = [lax.ppermute(s, 'x', swap) for s in sums]]
  transfers between devices with their start and end apart: 16 -> 15, of which waited for: 5 -> 6; matrix products, arithmetic and copies ran while one was open for 1% -> 1% of each run, Pallas kernels for 34% -> 34%
where the time goes in v7:
time: 86.7 us; the launch traced here: 85.9 us
  starting transfers between devices  36.2 us (42%)
  Pallas kernels  34.7 us (40%)
  waiting for transfers between devices  12.3 us (14%)
  other arithmetic  1 us (1%)
    ppermute x4, starting transfers between devices, send_back(): going.append(lax.ppermute(v, ('pairs', 'z'), route))  18.5 us
    pallas_call x4, Pallas kernels, resample(): pl.pallas_call(partial(resample_kernel, images.shape[0], first, parts), g...  16.5 us
    pallas_call x4, Pallas kernels, pair_sums(): pl.pallas_call(partial(pair_kernel, own, [p[0] for p in pieces], [f[0] fo...  12.7 us
    ppermute x8, starting transfers between devices, local(): received.append(lax.ppermute(v, 'x', swap))  7.73 us
    all_to_all x1, starting transfers between devices, local(): lax.all_to_all(outgoing, ('pairs', 'z'), split_axis=0, concat_axis=0, til...  7.2 us
    ppermute x8, waiting for transfers between devices, local(): received.append(lax.ppermute(v, 'x', swap))  5.77 us
    all_to_all x1, waiting for transfers between devices, local(): lax.all_to_all(outgoing, ('pairs', 'z'), split_axis=0, concat_axis=0, til...  4.39 us
    pallas_call x1, Pallas kernels, invert(): pl.pallas_call(invert_kernel, in_specs=[vmem()], out_specs=vmem(), out_sh...  2.96 us
  transfers between devices with their start and end apart: 15, of which 6 were waited for; matrix products, arithmetic and copies ran while one was open for 1% of the time, Pallas kernels for 34%

profile of v7, /device:TPU:1, one launch (start us, length us, event | category | flops | bytes accessed | tf_op | source)
XLA Modules:
  0.0 85.9 jit_solution(14516033265433799692)
XLA Ops:
  0.6 3.2 %shard_map.59 = (bf16[1,2,4,1,128,128]{5,4,3,2,1,0:T(8,128)(2,1)}, bf16[1,2,4,1,128,128]{5,4,3,2,1,0:T(8,128)(2,1)}) custom-call(s32[256]{0:T(256)} %az.7, s32[256]{0:T(256)} %rg.7, bf16[8,2,128,1024]{3,2,1,0:T(8,128)(2,1)} %img.7), custom_call_target="tpu_custom_call" | custom-call | flops 524288 | bytes 1048576 | tf_op jit(solution)/shard_map/pallas_call | solution.py:153
  3.8 2.0 %collective-permute-start = (bf16[1,2,4,1,128,128]{5,4,3,2,1,0:T(8,128)(2,1)}, bf16[1,2,4,1,128,128]{5,4,3,2,1,0:T(8,128)(2,1)S(1)}, u32[]{:S(2)}, u32[]{:S(2)}) collective-permute-start(bf16[1,2,4,1,128,128]{5,4,3,2,1,0:T(8,128)(2,1)} %get-tuple-element.24), channel_id=1, source_target_pairs={{0,1},{1,0},{2,3},{3,2},{4,5},{5,4},{6,7},{7,6},{8,9},{9,8},{10,11... | collective-permute-start | bytes 786440 | tf_op jit(solution)/shard_map/ppermute | solution.py:543
  5.8 3.2 %shard_map.60 = (bf16[1,2,4,1,128,128]{5,4,3,2,1,0:T(8,128)(2,1)}, bf16[1,2,4,1,128,128]{5,4,3,2,1,0:T(8,128)(2,1)}) custom-call(s32[256]{0:T(256)} %az.7, s32[256]{0:T(256)} %rg.7, bf16[8,2,128,1024]{3,2,1,0:T(8,128)(2,1)} %img.7, bf16[1,2,4,1,128,128]{5,4,3,2,1,0:T(8,128)(2,1)} %get-tuple-element.23.rest_0_.refs_0_), custom_call_target="tpu_custom_call" | custom-call | flops 524288 | bytes 1048576 | tf_op jit(solution)/shard_map/pallas_call | solution.py:153
  9.0 0.0 collective-permute-start.1
  9.0 0.0 copy-start.4
  9.0 0.0 copy-start.2
  9.0 0.0 copy-start.3
  9.0 5.2 %shard_map.61 = (bf16[3,2,4,1,128,128]{5,4,3,2,1,0:T(8,128)(2,1)}, bf16[3,2,2,1,128,128]{5,4,3,2,1,0:T(8,128)(2,1)}, bf16[3,2,2,1,128,128]{5,4,3,2,1,0:T(8,128)(2,1)}) custom-call(s32[256]{0:T(256)} %az.7, s32[256]{0:T(256)} %rg.7, bf16[8,2,128,1024]{3,2,1,0:T(8,128)(2,1)} %img.7, bf16[1,2,4,1,128,128]{5,4,3,2,1,0:T(8,128)(2,1)} %get-tuple-element.25.rest_0_.refs_2_), custom_call_target="tpu_custom_call" | custom-call | flops 1572864 | bytes 3145728 | tf_op jit(solution)/shard_map/pallas_call | solution.py:153
  14.2 0.0 copy-start
  14.2 1.5 %collective-permute-start.2 = (bf16[3,2,2,1,128,128]{5,4,3,2,1,0:T(8,128)(2,1)}, bf16[3,2,2,1,128,128]{5,4,3,2,1,0:T(8,128)(2,1)S(1)}, u32[]{:S(2)}, u32[]{:S(2)}) collective-permute-start(bf16[3,2,2,1,128,128]{5,4,3,2,1,0:T(8,128)(2,1)} %get-tuple-element.28), channel_id=1, source_target_pairs={{0,1},{1,0},{2,3},{3,2},{4,5},{5,4},{6,7},{7,6},{8,9},{9,8},{10,11... | collective-permute-start | bytes 1179656 | tf_op jit(solution)/shard_map/ppermute | solution.py:543
  15.6 5.0 %shard_map.62 = (bf16[3,2,4,1,128,128]{5,4,3,2,1,0:T(8,128)(2,1)}, bf16[3,2,1,1,128,128]{5,4,3,2,1,0:T(8,128)(2,1)}, bf16[3,2,1,1,128,128]{5,4,3,2,1,0:T(8,128)(...) custom-call(s32[256]{0:T(256)} %az.7, s32[256]{0:T(256)} %rg.7, ...), custom_call_target="tpu_custom_call" | custom-call | flops 1572864 | bytes 3145728 | tf_op jit(solution)/shard_map/pallas_call | solution.py:153
  20.7 0.0 copy-start.1
  20.7 0.2 collective-permute-start.7
  20.8 1.3 %collective-permute-start.8 = (bf16[3,2,2,1,128,128]{5,4,3,2,1,0:T(8,128)(2,1)}, bf16[3,2,2,1,128,128]{5,4,3,2,1,0:T(8,128)(2,1)S(1)}, u32[]{:S(2)}, u32[]{:S(2)}) collective-permute-start(bf16[3,2,2,1,128,128]{5,4,3,2,1,0:T(8,128)(2,1)} %get-tuple-element.37), channel_id=1, source_target_pairs={{0,1},{1,0},{2,3},{3,2},{4,5},{5,4},{6,7},{7,6},{8,9},{9,8},{10,11... | collective-permute-start | bytes 1179656 | tf_op jit(solution)/shard_map/ppermute | solution.py:543
  22.2 0.0 copy-done.4
  22.2 0.3 convolution_convert_fusion.mask
  22.5 0.0 collective-permute-done.refs_1_
  22.5 0.0 copy-done.2
  22.6 7.2 %collective-permute-start.4 = (bf16[1,2,4,1,128,128]{5,4,3,2,1,0:T(8,128)(2,1)S(1)}, bf16[1,2,4,1,128,128]{5,4,3,2,1,0:T(8,128)(2,1)S(1)}, u32[]{:S(2)}, u32[]{:S(2)}) collective-permute-start(bf16[1,2,4,1,128,128]{5,4,3,2,1,0:T(8,128)(2,1)S(1)} %broadcast_select_fusion.1), channel_id=1, source_target_pairs={{2,0},{4,2},{6,4},{8,6},{10,8},{12,10},{14,12},{16,14},{18,16},{20... | collective-permute-start | bytes 786440 | tf_op jit(solution)/shard_map/ppermute | solution.py:534
  29.7 0.0 collective-permute-done.1.refs_3_
  29.7 0.0 copy-done.3
  29.8 2.4 %collective-permute-start.5 = (bf16[1,2,4,1,128,128]{5,4,3,2,1,0:T(8,128)(2,1)S(1)}, bf16[1,2,4,1,128,128]{5,4,3,2,1,0:T(8,128)(2,1)S(1)}, u32[]{:S(2)}, u32[]{:S(2)}) collective-permute-start(bf16[1,2,4,1,128,128]{5,4,3,2,1,0:T(8,128)(2,1)S(1)} %broadcast_select_fusion), channel_id=1, source_target_pairs={{2,0},{4,2},{6,4},{8,6},{10,8},{12,10},{14,12},{16,14},{18,16},{20... | collective-permute-start | bytes 786440 | tf_op jit(solution)/shard_map/ppermute | solution.py:534
  32.2 0.0 collective-permute-done.2.refs_5_
  32.2 0.0 copy-done
  32.3 2.3 %collective-permute-start.6 = (bf16[3,2,2,1,128,128]{5,4,3,2,1,0:T(8,128)(2,1)S(1)}, bf16[3,2,2,1,128,128]{5,4,3,2,1,0:T(8,128)(2,1)S(1)}, u32[]{:S(2)}, u32[]{:S(2)}) collective-permute-start(bf16[3,2,2,1,128,128]{5,4,3,2,1,0:T(8,128)(2,1)S(1)} %slice_select_fusion.1), channel_id=1, source_target_pairs={{2,0},{4,2},{6,4},{8,6},{10,8},{12,10},{14,12},{16,14},{18,16},{20... | collective-permute-start | bytes 1179656 | tf_op jit(solution)/shard_map/ppermute | solution.py:534
  34.6 4.1 %collective-permute-done.8.refs_5_ = bf16[3,2,2,1,128,128]{5,4,3,2,1,0:T(8,128)(2,1)S(1)} collective-permute-done((bf16[3,2,2,1,128,128]{5,4,3,2,1,0:T(8,128)(2,1)}, bf16[3,2,2,1,128,128]{5,4,3,2,1,0:T(8,128)(2,1)S(1)}, u32[]{:S(2)}, u32[]{:S(2)}) %collective-permute-start.8) | collective-permute-done | bytes 393248 | tf_op jit(solution)/shard_map/ppermute | solution.py:543
  38.8 6.6 %collective-permute-start.10 = (bf16[3,2,2,1,128,128]{5,4,3,2,1,0:T(8,128)(2,1)S(1)}, bf16[3,2,2,1,128,128]{5,4,3,2,1,0:T(8,128)(2,1)S(1)}, u32[]{:S(2)}, u32[]{:S(2)}) collective-permute-start(bf16[3,2,2,1,128,128]{5,4,3,2,1,0:T(8,128)(2,1)S(1)} %slice_select_fusion), channel_id=1, source_target_pairs={{2,0},{4,2},{6,4},{8,6},{10,8},{12,10},{14,12},{16,14},{18,16},{20... | collective-permute-start | bytes 1179656 | tf_op jit(solution)/shard_map/ppermute | solution.py:534
  45.4 0.0 collective-permute-done.7.refs_7_
  45.4 1.3 %collective-permute-start.3 = (bf16[3,2,1,1,128,128]{5,4,3,2,1,0:T(8,128)(2,1)}, bf16[3,2,1,1,128,128]{5,4,3,2,1,0:T(8,128)(2,1)S(1)}, u32[]{:S(2)}, u32[]{:S(2)}) collective-permute-start(bf16[3,2,1,1,128,128]{5,4,3,2,1,0:T(8,128)(2,1)} %get-tuple-element.30), channel_id=1, source_target_pairs={{0,1},{1,0},{2,3},{3,2},{4,5},{5,4},{6,7},{7,6},{8,9},{9,8},{10,11... | collective-permute-start | bytes 589832 | tf_op jit(solution)/shard_map/ppermute | solution.py:543
  46.7 0.0 collective-permute-done.4.refs_8_
  46.7 0.3 collective-permute-start.9
  47.0 0.0 collective-permute-done.5.refs_9_
  47.0 1.2 %collective-permute-start.11 = (bf16[3,2,1,1,128,128]{5,4,3,2,1,0:T(8,128)(2,1)}, bf16[3,2,1,1,128,128]{5,4,3,2,1,0:T(8,128)(2,1)S(1)}, u32[]{:S(2)}, u32[]{:S(2)}) collective-permute-start(bf16[3,2,1,1,128,128]{5,4,3,2,1,0:T(8,128)(2,1)} %get-tuple-element.41), channel_id=1, source_target_pairs={{0,1},{1,0},{2,3},{3,2},{4,5},{5,4},{6,7},{7,6},{8,9},{9,8},{10,11... | collective-permute-start | bytes 589832 | tf_op jit(solution)/shard_map/ppermute | solution.py:543
  48.2 0.1 select_add_fusion
  48.3 0.2 collective-permute-done.6.refs_10_
  48.4 0.0 copy-done.1
  48.4 3.9 %shard_map.63.refs_11_ = f32[1,4,24,128]{3,2,1,0:T(8,128)S(1)} custom-call(s32[5,256]{1,0:T(8,128)S(1)} %convolution_convert_fusion.mask, bf16[1,2,4,1,128,128]{5,4,3,2,1,0:T(8,128)(2,1)S(1)} %copy-done.2, bf16[1,2,4,1,128,128]{5,4,3,2,1,0:T(8,128)(2,1)S(1)} %collective-permute-done.refs_1_, bf16[1,2,4,1,128,128]{5,4,3,2,1,0:T(8,128)(2,1)S(1)} %copy-done.3, ...), custom_call_target="tpu_custom_call" | custom-call | flops 10485760 | bytes 1310720 | tf_op jit(solution)/shard_map/pallas_call | solution.py:288
  52.3 0.3 collective-permute-done.3.refs_7_
  52.6 3.0 %shard_map.64.refs_11_.rest_0_ = f32[2,4,24,128]{3,2,1,0:T(8,128)S(1)} custom-call(s32[5,256]{1,0:T(8,128)S(1)} %convolution_convert_fusion.mask, bf16[1,2,4,1,128,128]{5,4,3,2,1,0:T(8,128)(2,1)S(1)} %copy-done.2, bf16[1,2,4,1,128,128]{5,4,3,2,1,0:T(8,128)(2,1)S(1)} %collective-permute-done.refs_1_, bf16[1,2,4,1,128,128]{5,4,3,2,1,0:T(8,128)(2,1)S(1)} %copy-done.3, ...), custom_call_target="tpu_custom_call" | custom-call | flops 10485760 | bytes 1310720 | tf_op jit(solution)/shard_map/pallas_call | solution.py:288
  55.6 1.3 %collective-permute-start.12 = (f32[2,4,24,128]{3,2,1,0:T(8,128)S(1)}, f32[2,4,24,128]{3,2,1,0:T(8,128)S(1)}, u32[]{:S(2)}, u32[]{:S(2)}) collective-permute-start(f32[2,4,24,128]{3,2,1,0:T(8,128)S(1)} %shard_map.64.refs_11_.rest_0_), channel_id=1, source_target_pairs={{0,1},{1,0},{2,3},{3,2},{4,5},{5,4},{6,7},{7,6},{8,9},{9,8},{10,11... | collective-permute-start | bytes 294920 | tf_op jit(solution)/shard_map/ppermute | solution.py:555
  56.9 1.3 %collective-permute-done.11.refs_7_ = bf16[3,2,1,1,128,128]{5,4,3,2,1,0:T(8,128)(2,1)S(1)} collective-permute-done((bf16[3,2,1,1,128,128]{5,4,3,2,1,0:T(8,128)(2,1)}, bf16[3,2,1,1,128,128]{5,4,3,2,1,0:T(8,128)(2,1)S(1)}, u32[]{:S(2)}, u32[]{:S(2)}) %collective-permute-start.11) | collective-permute-done | bytes 196640 | tf_op jit(solution)/shard_map/ppermute | solution.py:543
  58.2 0.0 collective-permute-done.10.refs_10_
  58.2 3.0 %shard_map.65.refs_11_ = f32[1,4,24,128]{3,2,1,0:T(8,128)S(1)} custom-call(s32[5,256]{1,0:T(8,128)S(1)} %convolution_convert_fusion.mask, bf16[1,2,4,1,128,128]{5,4,3,2,1,0:T(8,128)(2,1)S(1)} %copy-done.2, bf16[1,2,4,1,128,128]{5,4,3,2,1,0:T(8,128)(2,1)S(1)} %collective-permute-done.refs_1_, bf16[1,2,4,1,128,128]{5,4,3,2,1,0:T(8,128)(2,1)S(1)} %copy-done.3, ...), custom_call_target="tpu_custom_call" | custom-call | flops 10485760 | bytes 1310720 | tf_op jit(solution)/shard_map/pallas_call | solution.py:288
  61.2 0.0 collective-permute-done.9.refs_7_
  61.2 3.0 %shard_map.66.rest_1_ = f32[2,4,24,128]{3,2,1,0:T(8,128)S(1)} custom-call(s32[5,256]{1,0:T(8,128)S(1)} %convolution_convert_fusion.mask, bf16[1,2,4,1,128,128]{5,4,3,2,1,0:T(8,128)(2,1)S(1)} %copy-done.2, bf16[1,2,4,1,128,128]{5,4,3,2,1,0:T(8,128)(2,1)S(1)} %collective-permute-done.refs_1_, bf16[1,2,4,1,128,128]{5,4,3,2,1,0:T(8,128)(2,1)S(1)} %copy-done.3, ...), custom_call_target="tpu_custom_call" | custom-call | flops 10485760 | bytes 1310720 | tf_op jit(solution)/shard_map/pallas_call | solution.py:288
  64.1 1.5 %collective-permute-start.13 = (f32[2,4,24,128]{3,2,1,0:T(8,128)S(1)}, f32[2,4,24,128]{3,2,1,0:T(8,128)S(1)}, u32[]{:S(2)}, u32[]{:S(2)}) collective-permute-start(f32[2,4,24,128]{3,2,1,0:T(8,128)S(1)} %shard_map.66.rest_1_), channel_id=1, source_target_pairs={{0,1},{1,0},{2,3},{3,2},{4,5},{5,4},{6,7},{7,6},{8,9},{9,8},{10,11... | collective-permute-start | bytes 294920 | tf_op jit(solution)/shard_map/ppermute | solution.py:555
  65.7 0.0 collective-permute-done.12.rest_2_
  65.7 2.0 %collective-permute-done.13.rest_3_ = f32[2,4,24,128]{3,2,1,0:T(8,128)S(1)} collective-permute-done((f32[2,4,24,128]{3,2,1,0:T(8,128)S(1)}, f32[2,4,24,128]{3,2,1,0:T(8,128)S(1)}, u32[]{:S(2)}, u32[]{:S(2)}) %collective-permute-start.13) | collective-permute-done | bytes 98336 | tf_op jit(solution)/shard_map/ppermute | solution.py:555
  67.7 1.3 %smooth.1 = f32[4,4,2,24,128]{4,3,2,1,0:T(8,128)S(1)} custom-call(f32[2,4,24,128]{3,2,1,0:T(8,128)S(1)} %shard_map.64.refs_11_.rest_0_, f32[2,4,24,128]{3,2,1,0:T(8,128)S(1)} %shard_map.66.rest_1_, f32[2,4,24,128]{3,2,1,0:T(8,128)S(1)} %collective-permute-done.12.rest_2_, f32[2,4,24,128]{3,2,1,0:T(8,128)S(1)} %collective-permute-done.13.rest_3_, ...), custom_call_target="tpu_custom_call" | custom-call | tf_op jit(solution)/shard_map/smooth/pallas_call | solution.py:370
  69.0 0.7 convert_element_type.25
  69.7 7.2 %all-to-all-start = ((f16[16,2,24,128]{3,2,1,0:T(8,128)(2,1)}), f16[16,2,24,128]{3,2,1,0:T(8,128)(2,1)S(1)}, u32[]{:S(2)}, u32[]{:S(2)}) async-start(f16[16,2,24,128]{3,2,1,0:T(8,128)(2,1)} %bitcast.2), calls=%async_computation | async-start | bytes 393216 | tf_op jit(solution)/shard_map/all_to_all | solution.py:567
  76.9 0.5 convolution_add_fusion.normal
  77.4 3.0 %invert.1.inverse = f32[256,256]{1,0:T(8,128)S(1)} custom-call(f32[256,256]{1,0:T(8,128)S(1)} %convolution_add_fusion.normal), custom_call_target="tpu_custom_call" | custom-call | flops 2013265920 | bytes 524288 | tf_op jit(solution)/shard_map/invert/pallas_call | solution.py:423
  80.3 4.4 %all-to-all-done = f16[16,2,24,128]{3,2,1,0:T(8,128)(2,1)S(1)} async-done(((f16[16,2,24,128]{3,2,1,0:T(8,128)(2,1)}), f16[16,2,24,128]{3,2,1,0:T(8,128)(2,1)S(1)}, u32[]{:S(2)}, u32[]{:S(2)}) %all-to-all-start) | async-done | bytes 196640 | tf_op jit(solution)/shard_map/all_to_all | solution.py:567
  84.8 1.1 %series.1 = (f32[2,8,8,256]{3,2,1,0:T(8,128)}, f32[2,8,8,256]{3,2,1,0:T(8,128)}) custom-call(f32[16,2,24,128]{3,2,1,0:T(8,128)S(1)} %convert_element_type.27.got, f32[256,256]{1,0:T(8,128)S(1)} %invert.1.inverse), custom_call_target="tpu_custom_call" | custom-call | tf_op jit(solution)/shard_map/series/pallas_call | solution.py:464
  (13 shorter events, 0.2 us)
Async XLA Ops:
  3.8 18.7 %collective-permute-start = (bf16[1,2,4,1,128,128]{5,4,3,2,1,0:T(8,128)(2,1)}, bf16[1,2,4,1,128,128]{5,4,3,2,1,0:T(8,128)(2,1)S(1)}, u32[]{:S(2)}, u32[]{:S(2)}) collective-permute-start(bf16[1,2,4,1,128,128]{5,4,3,2,1,0:T(8,128)(2,1)} %get-tuple-element.24), channel_id=1, source_target_pairs={{0,1},{1,0},{2,3},{3,2},{4,5},{5,4},{6,7},{7,6},{8,9},{9,8},{10,11... | collective-permute-start | bytes 786440 | tf_op jit(solution)/shard_map/ppermute | solution.py:543
  9.0 20.7 %collective-permute-start.1 = (bf16[1,2,4,1,128,128]{5,4,3,2,1,0:T(8,128)(2,1)}, bf16[1,2,4,1,128,128]{5,4,3,2,1,0:T(8,128)(2,1)S(1)}, u32[]{:S(2)}, u32[]{:S(2)}) collective-permute-start(bf16[1,2,4,1,128,128]{5,4,3,2,1,0:T(8,128)(2,1)} %get-tuple-element.26), channel_id=1, source_target_pairs={{0,1},{1,0},{2,3},{3,2},{4,5},{5,4},{6,7},{7,6},{8,9},{9,8},{10,11... | collective-permute-start | bytes 786440 | tf_op jit(solution)/shard_map/ppermute | solution.py:543
  9.0 13.2 %copy-start.4 = (s32[1000,2]{0,1:T(2,128)S(1)}, s32[1000,2]{0,1:T(2,128)}, u32[]{:S(2)}) copy-start(s32[1000,2]{0,1:T(2,128)} %param.7) | copy-start | bytes 24004
  9.0 13.5 %copy-start.2 = (bf16[1,2,4,1,128,128]{5,4,3,2,1,0:T(8,128)(2,1)S(1)}, bf16[1,2,4,1,128,128]{5,4,3,2,1,0:T(8,128)(2,1)}, u32[]{:S(2)}) copy-start(bf16[1,2,4,1,128,128]{5,4,3,2,1,0:T(8,128)(2,1)} %get-tuple-element.23.rest_0_.refs_0_) | copy-start | bytes 786436
  9.0 20.7 %copy-start.3 = (bf16[1,2,4,1,128,128]{5,4,3,2,1,0:T(8,128)(2,1)S(1)}, bf16[1,2,4,1,128,128]{5,4,3,2,1,0:T(8,128)(2,1)}, u32[]{:S(2)}) copy-start(bf16[1,2,4,1,128,128]{5,4,3,2,1,0:T(8,128)(2,1)} %get-tuple-element.25.rest_0_.refs_2_) | copy-start | bytes 786436
  14.2 18.0 %copy-start = (bf16[3,2,4,1,128,128]{5,4,3,2,1,0:T(8,128)(2,1)S(1)}, bf16[3,2,4,1,128,128]{5,4,3,2,1,0:T(8,128)(2,1)}, u32[]{:S(2)}) copy-start(bf16[3,2,4,1,128,128]{5,4,3,2,1,0:T(8,128)(2,1)} %get-tuple-element.27.rest_0_.refs_4_) | copy-start | bytes 2359300
  14.2 18.0 %collective-permute-start.2 = (bf16[3,2,2,1,128,128]{5,4,3,2,1,0:T(8,128)(2,1)}, bf16[3,2,2,1,128,128]{5,4,3,2,1,0:T(8,128)(2,1)S(1)}, u32[]{:S(2)}, u32[]{:S(2)}) collective-permute-start(bf16[3,2,2,1,128,128]{5,4,3,2,1,0:T(8,128)(2,1)} %get-tuple-element.28), channel_id=1, source_target_pairs={{0,1},{1,0},{2,3},{3,2},{4,5},{5,4},{6,7},{7,6},{8,9},{9,8},{10,11... | collective-permute-start | bytes 1179656 | tf_op jit(solution)/shard_map/ppermute | solution.py:543
  20.7 27.8 %copy-start.1 = (bf16[3,2,4,1,128,128]{5,4,3,2,1,0:T(8,128)(2,1)S(1)}, bf16[3,2,4,1,128,128]{5,4,3,2,1,0:T(8,128)(2,1)}, u32[]{:S(2)}) copy-start(bf16[3,2,4,1,128,128]{5,4,3,2,1,0:T(8,128)(2,1)} %get-tuple-element.29.refs_6_) | copy-start | bytes 2359300
  20.7 24.7 %collective-permute-start.7 = (bf16[3,2,1,1,128,128]{5,4,3,2,1,0:T(8,128)(2,1)}, bf16[3,2,1,1,128,128]{5,4,3,2,1,0:T(8,128)(2,1)}, u32[]{:S(2)}, u32[]{:S(2)}) collective-permute-start(bf16[3,2,1,1,128,128]{5,4,3,2,1,0:T(8,128)(2,1)} %get-tuple-element.36), channel_id=1, source_target_pairs={{0,1},{1,0},{2,3},{3,2},{4,5},{5,4},{6,7},{7,6},{8,9},{9,8},{10,11... | collective-permute-start | bytes 589832 | tf_op jit(solution)/shard_map/ppermute | solution.py:543
  20.8 17.9 %collective-permute-start.8 = (bf16[3,2,2,1,128,128]{5,4,3,2,1,0:T(8,128)(2,1)}, bf16[3,2,2,1,128,128]{5,4,3,2,1,0:T(8,128)(2,1)S(1)}, u32[]{:S(2)}, u32[]{:S(2)}) collective-permute-start(bf16[3,2,2,1,128,128]{5,4,3,2,1,0:T(8,128)(2,1)} %get-tuple-element.37), channel_id=1, source_target_pairs={{0,1},{1,0},{2,3},{3,2},{4,5},{5,4},{6,7},{7,6},{8,9},{9,8},{10,11... | collective-permute-start | bytes 1179656 | tf_op jit(solution)/shard_map/ppermute | solution.py:543
  22.6 24.1 %collective-permute-start.4 = (bf16[1,2,4,1,128,128]{5,4,3,2,1,0:T(8,128)(2,1)S(1)}, bf16[1,2,4,1,128,128]{5,4,3,2,1,0:T(8,128)(2,1)S(1)}, u32[]{:S(2)}, u32[]{:S(2)}) collective-permute-start(bf16[1,2,4,1,128,128]{5,4,3,2,1,0:T(8,128)(2,1)S(1)} %broadcast_select_fusion.1), channel_id=1, source_target_pairs={{2,0},{4,2},{6,4},{8,6},{10,8},{12,10},{14,12},{16,14},{18,16},{20... | collective-permute-start | bytes 786440 | tf_op jit(solution)/shard_map/ppermute | solution.py:534
  29.8 17.2 %collective-permute-start.5 = (bf16[1,2,4,1,128,128]{5,4,3,2,1,0:T(8,128)(2,1)S(1)}, bf16[1,2,4,1,128,128]{5,4,3,2,1,0:T(8,128)(2,1)S(1)}, u32[]{:S(2)}, u32[]{:S(2)}) collective-permute-start(bf16[1,2,4,1,128,128]{5,4,3,2,1,0:T(8,128)(2,1)S(1)} %broadcast_select_fusion), channel_id=1, source_target_pairs={{2,0},{4,2},{6,4},{8,6},{10,8},{12,10},{14,12},{16,14},{18,16},{20... | collective-permute-start | bytes 786440 | tf_op jit(solution)/shard_map/ppermute | solution.py:534
  32.3 16.2 %collective-permute-start.6 = (bf16[3,2,2,1,128,128]{5,4,3,2,1,0:T(8,128)(2,1)S(1)}, bf16[3,2,2,1,128,128]{5,4,3,2,1,0:T(8,128)(2,1)S(1)}, u32[]{:S(2)}, u32[]{:S(2)}) collective-permute-start(bf16[3,2,2,1,128,128]{5,4,3,2,1,0:T(8,128)(2,1)S(1)} %slice_select_fusion.1), channel_id=1, source_target_pairs={{2,0},{4,2},{6,4},{8,6},{10,8},{12,10},{14,12},{16,14},{18,16},{20... | collective-permute-start | bytes 1179656 | tf_op jit(solution)/shard_map/ppermute | solution.py:534
  38.8 19.4 %collective-permute-start.10 = (bf16[3,2,2,1,128,128]{5,4,3,2,1,0:T(8,128)(2,1)S(1)}, bf16[3,2,2,1,128,128]{5,4,3,2,1,0:T(8,128)(2,1)S(1)}, u32[]{:S(2)}, u32[]{:S(2)}) collective-permute-start(bf16[3,2,2,1,128,128]{5,4,3,2,1,0:T(8,128)(2,1)S(1)} %slice_select_fusion), channel_id=1, source_target_pairs={{2,0},{4,2},{6,4},{8,6},{10,8},{12,10},{14,12},{16,14},{18,16},{20... | collective-permute-start | bytes 1179656 | tf_op jit(solution)/shard_map/ppermute | solution.py:534
  45.4 7.2 %collective-permute-start.3 = (bf16[3,2,1,1,128,128]{5,4,3,2,1,0:T(8,128)(2,1)}, bf16[3,2,1,1,128,128]{5,4,3,2,1,0:T(8,128)(2,1)S(1)}, u32[]{:S(2)}, u32[]{:S(2)}) collective-permute-start(bf16[3,2,1,1,128,128]{5,4,3,2,1,0:T(8,128)(2,1)} %get-tuple-element.30), channel_id=1, source_target_pairs={{0,1},{1,0},{2,3},{3,2},{4,5},{5,4},{6,7},{7,6},{8,9},{9,8},{10,11... | collective-permute-start | bytes 589832 | tf_op jit(solution)/shard_map/ppermute | solution.py:543
  46.7 14.5 %collective-permute-start.9 = (bf16[3,2,1,1,128,128]{5,4,3,2,1,0:T(8,128)(2,1)}, bf16[3,2,1,1,128,128]{5,4,3,2,1,0:T(8,128)(2,1)S(1)}, u32[]{:S(2)}, u32[]{:S(2)}) collective-permute-start(bf16[3,2,1,1,128,128]{5,4,3,2,1,0:T(8,128)(2,1)} %get-tuple-element.38), channel_id=1, source_target_pairs={{0,1},{1,0},{2,3},{3,2},{4,5},{5,4},{6,7},{7,6},{8,9},{9,8},{10,11... | collective-permute-start | bytes 589832 | tf_op jit(solution)/shard_map/ppermute | solution.py:543
  47.0 11.2 %collective-permute-start.11 = (bf16[3,2,1,1,128,128]{5,4,3,2,1,0:T(8,128)(2,1)}, bf16[3,2,1,1,128,128]{5,4,3,2,1,0:T(8,128)(2,1)S(1)}, u32[]{:S(2)}, u32[]{:S(2)}) collective-permute-start(bf16[3,2,1,1,128,128]{5,4,3,2,1,0:T(8,128)(2,1)} %get-tuple-element.41), channel_id=1, source_target_pairs={{0,1},{1,0},{2,3},{3,2},{4,5},{5,4},{6,7},{7,6},{8,9},{9,8},{10,11... | collective-permute-start | bytes 589832 | tf_op jit(solution)/shard_map/ppermute | solution.py:543
  55.6 10.1 %collective-permute-start.12 = (f32[2,4,24,128]{3,2,1,0:T(8,128)S(1)}, f32[2,4,24,128]{3,2,1,0:T(8,128)S(1)}, u32[]{:S(2)}, u32[]{:S(2)}) collective-permute-start(f32[2,4,24,128]{3,2,1,0:T(8,128)S(1)} %shard_map.64.refs_11_.rest_0_), channel_id=1, source_target_pairs={{0,1},{1,0},{2,3},{3,2},{4,5},{5,4},{6,7},{7,6},{8,9},{9,8},{10,11... | collective-permute-start | bytes 294920 | tf_op jit(solution)/shard_map/ppermute | solution.py:555
  64.1 3.5 %collective-permute-start.13 = (f32[2,4,24,128]{3,2,1,0:T(8,128)S(1)}, f32[2,4,24,128]{3,2,1,0:T(8,128)S(1)}, u32[]{:S(2)}, u32[]{:S(2)}) collective-permute-start(f32[2,4,24,128]{3,2,1,0:T(8,128)S(1)} %shard_map.66.rest_1_), channel_id=1, source_target_pairs={{0,1},{1,0},{2,3},{3,2},{4,5},{5,4},{6,7},{7,6},{8,9},{9,8},{10,11... | collective-permute-start | bytes 294920 | tf_op jit(solution)/shard_map/ppermute | solution.py:555
  69.7 15.0 %all-to-all-start = ((f16[16,2,24,128]{3,2,1,0:T(8,128)(2,1)}), f16[16,2,24,128]{3,2,1,0:T(8,128)(2,1)S(1)}, u32[]{:S(2)}, u32[]{:S(2)}) async-start(f16[16,2,24,128]{3,2,1,0:T(8,128)(2,1)} %bitcast.2), calls=%async_computation | async-start | bytes 393216 | tf_op jit(solution)/shard_map/all_to_all | solution.py:567
